TPU v7x, 32 devices: a whole 2x2x4 slice. The times are simulated.
32 devices in a mesh: occ: 4 (over y, x), sec: 8 (over z, core).
Axes of the slice: x: 2, y: 2, z: 4, core: 2. Of those that a mesh axis runs over, the one named last changes fastest.
Arguments:
- amplitudes: float32 [192, 512, 512], P('occ', None, 'sec'), may hold values from -5 to 5
- live_pairs: int32 [4], replicated, may hold values from 12 to 48, as said below
- ladder_ints: float32 [512, 512, 1024], P('occ', 'sec'), may hold values from -0.015625 to 0.015625
- cycle_ints: float32 [48, 512, 6144], P(None, 'sec', 'occ'), may hold values from -0.0390625 to 0.0390625
- pair_ints: float32 [192, 1024], P('occ', 'sec'), may hold values from -6 to 6
- occ_energy: float32 [48], replicated, may hold values from -2 to -0.5
- vir_energy: float32 [512], replicated, may hold values from 0.5 to 4
Outputs:
- new_amplitudes: float32 [192, 1024], P('occ', 'sec')
Inputs may be any that keep to these rules, and one draw needn't show every extreme that they name: live_pairs[o] live pairs are the first ones of owner o's 48 pairs; some owner has all of its pairs live.
All inputs are finite; a program needn't handle non-finite values.
Results may differ from a plain program's by a relative error of at most 0.00005.
Values sent between devices are 32-bit elements; how exact they have to be, the bound alone decides.
No kernel may reach another device: no remote copies, remote signals or barrier semaphores. Data moves between devices by JAX's collectives and lax.ppermute only.
A program may use at most 128 MiB of HBM per device.

v0:
```python
import jax
import jax.numpy as jnp
from jax import lax
from jax.sharding import PartitionSpec as P

OCCUPIED = 48
VIRTUAL = 512
A_WINDOW = 8
B_WINDOW = 128
I_OWNER = 1


highest = lax.Precision.HIGHEST


def shards(amplitudes, live_pairs, ladder_ints, cycle_ints, pair_ints, occ_energy, vir_energy):
    owners = lax.axis_size("occ")
    sections = lax.axis_size("sec")
    owner_index = lax.axis_index("occ")
    section = lax.axis_index("sec")
    owner_rows = I_OWNER * OCCUPIED
    window_rows = I_OWNER * owners
    owner_cols = OCCUPIED // owners
    col_share = A_WINDOW * B_WINDOW // sections
    d_share = amplitudes.shape[2]
    live_count = lax.dynamic_slice_in_dim(live_pairs, owner_index, 1)[0]
    local_rows = lax.broadcasted_iota(jnp.int32, (owner_rows, 1, 1), 0)
    live_rows = (local_rows < live_count).astype(jnp.float32)
    masked = amplitudes * live_rows
    flat_tiles = masked.reshape(owner_rows, owners, VIRTUAL // owners * d_share)
    regrouped = lax.all_to_all(flat_tiles, "occ", split_axis=1, concat_axis=0, tiled=True)
    pair_total = regrouped.shape[0]
    ladder_part = 0.5 * jnp.dot(
        regrouped.reshape(pair_total, -1),
        ladder_ints.reshape(-1, A_WINDOW * B_WINDOW),
        precision=highest,
        preferred_element_type=jnp.float32,
    )
    cycle_local = masked[:, :A_WINDOW, :].reshape(owner_rows, A_WINDOW * d_share)
    cycle_flat = lax.all_gather(cycle_local, "occ", axis=0, tiled=True)
    cycle_rows = cycle_flat.reshape(window_rows, OCCUPIED, A_WINDOW, d_share)
    cycle_part = jnp.einsum(
        "ikac,kcn->ian",
        cycle_rows,
        cycle_ints,
        precision=highest,
        preferred_element_type=jnp.float32,
    )
    cycle_part = (
        cycle_part.reshape(window_rows, A_WINDOW, owner_cols, B_WINDOW)
        .transpose(0, 2, 1, 3)
        .reshape(window_rows, owner_cols, A_WINDOW * B_WINDOW)
    )
    ladder_grid = ladder_part.reshape(window_rows, OCCUPIED, A_WINDOW * B_WINDOW)
    offset = owner_index * owner_cols
    current_part = lax.dynamic_slice_in_dim(ladder_grid, offset, owner_cols, 1)
    ladder_grid = lax.dynamic_update_slice_in_dim(ladder_grid, current_part + cycle_part, offset, 1)
    combined = ladder_grid.reshape(pair_total, A_WINDOW * B_WINDOW)
    first_sum = lax.psum_scatter(combined, "sec", scatter_dimension=1, tiled=True)
    summed = lax.psum_scatter(first_sum, "occ", scatter_dimension=0, tiled=True)
    residual = summed + pair_ints
    occ_rows = lax.dynamic_slice_in_dim(occ_energy, owner_index * I_OWNER, I_OWNER)
    pair_energy = (occ_rows[:, None] + occ_energy[None, :]).reshape(owner_rows, 1)
    vir_pairs = (vir_energy[:A_WINDOW, None] + vir_energy[None, :B_WINDOW]).reshape(
        A_WINDOW * B_WINDOW
    )
    vir_cols = lax.dynamic_slice_in_dim(vir_pairs, section * col_share, col_share)
    denominator = pair_energy - vir_cols[None, :]
    live_out = (lax.broadcasted_iota(jnp.int32, (owner_rows, 1), 0) < live_count).astype(
        jnp.float32
    )
    return residual / denominator * live_out


def solution(mesh):
    in_specs = (
        P("occ", None, "sec"),
        P(),
        P("occ", "sec", None),
        P(None, "sec", "occ"),
        P("occ", "sec"),
        P(),
        P(),
    )
    out_specs = P("occ", "sec")
    return jax.shard_map(shards, mesh=mesh, in_specs=in_specs, out_specs=out_specs, check_vma=False)
```

profile of v0, /device:TPU:0, one launch (start us, length us, event | category | flops | bytes accessed | tf_op | source)
XLA Modules:
  0.0 235.5 jit_solution(9436662550981658536)
XLA Ops:
  6.5 1.2 dynamic_slice.12
  7.8 0.6 compare_convert_fusion
  8.4 6.7 %broadcast_multiply_fusion = f32[48,512,64]{1,2,0:T(8,128)} fusion(f32[48,512,64]{1,2,0:T(8,128)} %param.7, f32[48]{0:T(128)S(1)} %compare_convert_fusion), kind=kLoop, calls=%fused_computation.3 | loop fusion | flops 1572864 | bytes 12583104 | tf_op jit(solution)/shard_map/mul | solution.py:29
  15.1 9.5 %copy.17 = f32[48,512,64]{2,1,0:T(8,128)} copy(f32[48,512,64]{1,2,0:T(8,128)} %broadcast_multiply_fusion) | data formatting | bytes 12582912 | tf_op jit(solution)/shard_map/mul | solution.py:29
  24.7 11.8 %reshape.55 = f32[48,4,8192]{2,1,0:T(4,128)} reshape(f32[48,512,64]{2,1,0:T(8,128)} %copy.17) | data formatting | bytes 12582912 | tf_op jit(solution)/shard_map/reshape | solution.py:30
  36.4 9.2 %copy.18 = f32[48,4,8192]{2,0,1:T(8,128)} copy(f32[48,4,8192]{2,1,0:T(4,128)} %reshape.55) | data formatting | bytes 12582912 | tf_op jit(solution)/shard_map/reshape | solution.py:30
  45.6 5.2 %all-to-all-start = ((f32[48,4,8192]{2,0,1:T(8,128)}), f32[48,4,8192]{2,0,1:T(8,128)}, u32[]{:S(2)}, u32[]{:S(2)}) async-start(f32[48,4,8192]{2,0,1:T(8,128)} %copy.18), calls=%async_computation | async-start | bytes 12582912 | tf_op jit(solution)/shard_map/all_to_all | solution.py:31
  50.9 0.0 reduce-scatter.5.cloned.1.call-start
  51.0 0.4 copy.20
  51.4 0.1 reshape.59
  51.5 75.8 %all_gather.3 = f32[192,512]{1,0:T(8,128)S(1)} all-gather(f32[48,512]{1,0:T(8,128)S(1)} %reshape.59), channel_id=1, replica_groups=mesh['occ'=4,'sec'=8] {'occ'}, dimensions={0}, use_global_device_ids=true | all-gather | bytes 491520 | tf_op jit(solution)/shard_map/all_gather | solution.py:40
  127.3 0.2 reshape.63
  127.5 13.9 %fusion.2 = f32[4,12,8,128]{3,2,1,0:T(8,128)S(1)} fusion(f32[4,48,8,64,1]{3,2,1,0,4:T(8,128)S(1)} %reshape.63, f32[48,64,1536]{2,1,0:T(8,128)} %param.10), kind=kOutput, calls=%fused_computation.5 | convolution fusion | flops 1811939328 | bytes 19464192 | tf_op jit(solution)/shard_map/ikac,kcn->ian/dot_general | solution.py:42
  141.5 0.1 reshape.61
  141.6 0.0 copy-start.2
  141.6 0.0 slice-start.1
  141.6 0.0 copy-start.1
  141.6 26.3 %convolution_multiply_fusion = f32[192,1024]{1,0:T(8,128)S(1)} fusion(f32[192,8192]{1,0:T(8,128)} %bitcast.3, f32[8192,1024]{1,0:T(8,128)} %bitcast.42), kind=kOutput, calls=%fused_computation.4 | convolution fusion | flops 19327549440 | bytes 40632320 | tf_op jit(solution)/shard_map/dot_general | solution.py:33
  168.0 0.2 copy_add_fusion
  168.2 0.1 copy.24
  168.3 0.3 dynamic_update_slice.3
  168.6 0.9 copy-done
  169.5 0.0 reduce-scatter.5.cloned.1.call-update
  169.5 0.0 reduce-scatter.7.cloned.1.call-start
  169.6 0.6 dynamic_slice.14
  170.2 0.1 add_bitcast_fusion
  170.3 0.1 dynamic_slice.15
  170.3 31.6 %reduce-scatter.5.cloned.1.call-done = f32[192,128]{1,0:T(8,128)} async-done(((f32[192,1024]{1,0:T(8,128)}), f32[192,128]{1,0:T(8,128)}) %reduce-scatter.5.cloned.1.call-update) | async-done | bytes 98320 | tf_op jit(solution)/shard_map/reduce_scatter | solution.py:59
  202.0 0.0 reduce-scatter.7.cloned.1.call-update
  202.0 0.7 broadcast_add_fusion
  202.6 24.6 %reduce-scatter.7.cloned.1.call-done = f32[48,128]{1,0:T(8,128)} async-done(((f32[192,128]{1,0:T(8,128)}), f32[48,128]{1,0:T(8,128)}) %reduce-scatter.7.cloned.1.call-update) | async-done | bytes 24592
  227.3 1.4 divide_multiply_fusion
  (11 shorter events, 0.1 us)
Async XLA Ops:
  36.4 14.5 %slice-start = ((f32[48,512,64]{1,2,0:T(8,128)}), f32[48,8,64]{1,2,0:T(8,128)S(1)}, s32[]{:S(2)}) async-start(f32[48,512,64]{1,2,0:T(8,128)} %broadcast_multiply_fusion), calls=%async_computation.5 | async-start | bytes 3145728 | tf_op jit(solution)/shard_map/slice | solution.py:39
  45.6 95.9 %all-to-all-start = ((f32[48,4,8192]{2,0,1:T(8,128)}), f32[48,4,8192]{2,0,1:T(8,128)}, u32[]{:S(2)}, u32[]{:S(2)}) async-start(f32[48,4,8192]{2,0,1:T(8,128)} %copy.18), calls=%async_computation | async-start | bytes 12582912 | tf_op jit(solution)/shard_map/all_to_all | solution.py:31
  50.9 151.1 %reduce-scatter.5.cloned.1.call-start = ((), (), s32[]{:S(2)}) async-start(), calls=%async_computation.3 | async-start | bytes 884736 | tf_op jit(solution)/shard_map/reduce_scatter | solution.py:59
  141.6 28.0 %copy-start.2 = (f32[48]{0:T(128)S(1)}, f32[48]{0:T(128)}, u32[]{:S(2)}) copy-start(f32[48]{0:T(128)} %param.12) | copy-start | bytes 580
  141.6 28.6 %slice-start.1 = ((f32[512]{0:T(512)}), f32[128]{0:T(128)S(1)}, s32[]{:S(2)}) async-start(f32[512]{0:T(512)} %param.13), calls=%async_computation.6 | async-start | bytes 1024 | tf_op jit(solution)/shard_map/slice | solution.py:64
  141.6 28.6 %slice-start.2 = ((f32[512]{0:T(512)}), f32[8]{0:T(128)S(1)}, s32[]{:S(2)}) async-start(f32[512]{0:T(512)} %param.13), calls=%async_computation.7 | async-start | bytes 1024 | tf_op jit(solution)/shard_map/slice | solution.py:64
  141.6 85.7 %copy-start.1 = (f32[48,128]{1,0:T(8,128)S(1)}, f32[48,128]{1,0:T(8,128)}, u32[]{:S(2)}) copy-start(f32[48,128]{1,0:T(8,128)} %param.11) | copy-start | bytes 73732
  168.6 0.9 copy-start
  169.5 57.7 %reduce-scatter.7.cloned.1.call-start = ((), (), s32[]{:S(2)}) async-start(), calls=%async_computation.4 | async-start | bytes 122880
Sparse Core Ops, SparseCore 0:
  169.7 32.2 reduce-scatter.4
  204.7 22.5 reduce-scatter.6
where the time goes:
time: 236 us
  blocking collectives  75.8 us (32%)
  waiting for transfers between devices  56.3 us (24%)
  matrix products  40.3 us (17%)
  local copies, waits for them, and re-layouts  34.6 us (15%)
  between operations  13.6 us (6%)
  other arithmetic  9.64 us (4%)
  starting transfers between devices  5.33 us (2%)
    all_gather x1, blocking collectives, shards(): cycle_flat = lax.all_gather(cycle_local, 'occ', axis=0, tiled=True)  75.8 us
    reduce_scatter x1, waiting for transfers between devices, shards(): lax.psum_scatter(combined, 'sec', scatter_dimension=1, tiled=True)  31.6 us
    dot_general x1, matrix products, shards(): jnp.dot(regrouped.reshape(pair_total, -1), ladder_ints.reshape(-1, A_WIND...  26.3 us
    unnamed x3, waiting for transfers between devices  24.7 us
    reshape x2, local copies, waits for them, and re-layouts, shards(): flat_tiles = masked.reshape(owner_rows, owners, VIRTUAL // owners * d_share)  21 us
    dot_general x1, matrix products, shards(): jnp.einsum('ikac,kcn->ian', cycle_rows, cycle_ints, precision=highest, pr...  13.9 us
    mul x1, local copies, waits for them, and re-layouts, shards(): masked = amplitudes * live_rows  9.55 us
    mul x1, other arithmetic, shards(): masked = amplitudes * live_rows  6.69 us
  transfers between devices with their start and end apart: 3, of which 2 were waited for; matrix products, arithmetic and copies ran while one was open for 7% of the time, Pallas kernels for 0%

commit v1 on v0

--- a/solution.py
+++ b/solution.py
@@ -1,19 +1,343 @@
+import functools
+
 import jax
 import jax.numpy as jnp
 from jax import lax
+from jax.experimental import pallas as pl
+from jax.experimental.pallas import tpu as pltpu
 from jax.sharding import PartitionSpec as P
+
 
 OCCUPIED = 48
 VIRTUAL = 512
 A_WINDOW = 8
 B_WINDOW = 128
 I_OWNER = 1
-
-
+LANES = 128
+D_STEP = 8
+CHUNK_UNITS = 8
+CHUNKS = (0, 3, 6, 7)
+CYCLE_PAD = 16
+
+
+f32 = jnp.float32
+bf16 = jnp.bfloat16
 highest = lax.Precision.HIGHEST
-
-
-def shards(amplitudes, live_pairs, ladder_ints, cycle_ints, pair_ints, occ_energy, vir_energy):
+VMEM_LIMIT = 48 * 1024 * 1024
+SMALL_LIMIT = 16 * 1024 * 1024
+
+
+def split(x):
+    hi = x.astype(bf16)
+    return hi, (x - hi.astype(f32)).astype(bf16)
+
+
+def dot(a, b):
+    return jnp.dot(a, b, preferred_element_type=f32)
+
+
+def dot_split(a, w):
+    rows = a.shape[0]
+    a_hi, a_lo = split(a)
+    w_hi, w_lo = split(w)
+    both = dot(jnp.concatenate([a_hi, a_lo], axis=0), w_hi)
+    return both[:rows] + both[rows:] + dot(a_hi, w_lo)
+
+
+def sds(*shape):
+    return jax.ShapeDtypeStruct(shape, f32)
+
+
+def small(kernel, out_shape, operands, scratch=()):
+    vmem = pl.BlockSpec(memory_space=pltpu.VMEM)
+    outs = out_shape if isinstance(out_shape, list) else [out_shape]
+    moved = 4 * sum(x.size for x in [*operands, *outs])
+    return pl.pallas_call(
+        kernel,
+        out_shape=out_shape,
+        in_specs=[vmem] * len(operands),
+        out_specs=[vmem] * len(outs) if isinstance(out_shape, list) else vmem,
+        scratch_shapes=list(scratch),
+        compiler_params=pltpu.CompilerParams(vmem_limit_bytes=SMALL_LIMIT),
+        cost_estimate=pl.CostEstimate(flops=0, bytes_accessed=moved, transcendentals=0),
+    )(*operands)
+
+
+def after(value, earlier):
+    return lax.optimization_barrier((value, earlier))[0]
+
+
+def block_of(index):
+    return pl.ds(pl.multiple_of(index * LANES, LANES), LANES)
+
+
+def slice_kernel(d0, a_ref, *refs):
+    outs, sem = refs[:-1], refs[-1]
+    owner = lax.axis_index("occ")
+    copies = [
+        pltpu.make_async_copy(a_ref.at[:, pl.ds(d0, out.shape[1]), block_of(owner ^ k)], out, sem.at[k - 1])
+        for k, out in enumerate(outs, start=1)
+    ]
+    for copy in copies:
+        copy.start()
+    for copy in copies:
+        copy.wait()
+
+
+def slice_chunk(turn, flipped, owners, d0, dn):
+    rows = flipped.shape[0]
+    n = owners - 1
+    return pl.pallas_call(
+        lambda _, *refs: slice_kernel(d0, *refs),
+        out_shape=[sds(rows, dn, LANES)] * n,
+        in_specs=[pl.BlockSpec(memory_space=pl.ANY)] * 2,
+        out_specs=[pl.BlockSpec(memory_space=pltpu.VMEM)] * n,
+        scratch_shapes=[pltpu.SemaphoreType.DMA((n,))],
+        compiler_params=pltpu.CompilerParams(vmem_limit_bytes=VMEM_LIMIT),
+        cost_estimate=pl.CostEstimate(flops=0, bytes_accessed=8 * n * rows * dn * LANES, transcendentals=0),
+        name="slices",
+    )(turn, flipped)
+
+
+def window_kernel(window, counts, a_ref, out_ref):
+    rows, depth, _ = a_ref.shape
+    flat = a_ref[...].reshape(rows * depth, LANES)
+    pair = lax.broadcasted_iota(jnp.int32, (window, rows * depth), 1) // depth
+    out_ref[...] = jnp.where(pair < counts[lax.axis_index("occ")], flat.T[:window], 0.0)
+
+
+def cycle_window(counts, flipped, window):
+    rows, depth, _ = flipped.shape
+    return pl.pallas_call(
+        functools.partial(window_kernel, window),
+        out_shape=sds(window, rows * depth),
+        grid_spec=pltpu.PrefetchScalarGridSpec(
+            num_scalar_prefetch=1,
+            grid=(1,),
+            in_specs=[pl.BlockSpec((rows, depth, LANES), lambda i, counts: (0, 0, 0))],
+            out_specs=pl.BlockSpec((window, rows * depth), lambda i, counts: (0, 0)),
+        ),
+        compiler_params=pltpu.CompilerParams(vmem_limit_bytes=VMEM_LIMIT),
+        cost_estimate=pl.CostEstimate(flops=0, bytes_accessed=4 * rows * depth * LANES, transcendentals=0),
+        name="cycle_window",
+    )(counts, flipped)
+
+
+def ladder_kernel(n, first, last, steps, ids, *refs):
+    a_refs, w_ref, rest = refs[:n], refs[n], refs[n + 1 :]
+    acc_ref = rest[-1]
+    step = pl.program_id(0)
+
+    @pl.when(step == 0)
+    def _():
+        acc_ref[...] = jnp.zeros_like(acc_ref) if first else rest[0][...]
+
+    for d in range(0, D_STEP, 2):
+        a = jnp.concatenate(
+            [jnp.concatenate([r[:, d, :], r[:, d + 1, :]], axis=1) for r in a_refs], axis=0
+        )
+        w = jnp.concatenate([w_ref[:, d, :], w_ref[:, d + 1, :]], axis=0)
+        acc_ref[...] += dot_split(a, w)
+
+    if last:
+
+        @pl.when(step == steps - 1)
+        def _():
+            pair_halves(acc_ref, rest[-3], rest[-2])
+
+
+def pair_halves(src_ref, send_ref, keep_ref):
+    core = lax.rem(lax.axis_index("sec"), 2)
+    for z in range(send_ref.shape[1] // LANES):
+        cols = slice(z * LANES, (z + 1) * LANES)
+        send_ref[:, cols] = src_ref[:, block_of(2 * z + 1 - core)]
+        keep_ref[:, cols] = src_ref[:, block_of(2 * z + core)]
+
+
+def ladder_product(ids, flipped, arrived, ladder_ints, acc, d0, last):
+    n = len(arrived) + 1
+    rows, dn, _ = arrived[0].shape
+    cols = ladder_ints.shape[2]
+    first = acc is None
+    steps = dn // D_STEP
+    total = pl.BlockSpec((n * rows, cols), lambda i, ids: (0, 0))
+    half = pl.BlockSpec((n * rows, cols // 2), lambda i, ids: (0, 0))
+    return pl.pallas_call(
+        functools.partial(ladder_kernel, n, first, last, steps),
+        out_shape=[sds(n * rows, cols // 2)] * 2 if last else sds(n * rows, cols),
+        grid_spec=pltpu.PrefetchScalarGridSpec(
+            num_scalar_prefetch=1,
+            grid=(steps,),
+            in_specs=[pl.BlockSpec((rows, D_STEP, LANES), lambda i, ids: (0, d0 // D_STEP + i, ids[0]))]
+            + [pl.BlockSpec((rows, D_STEP, LANES), lambda i, ids: (0, i, 0))] * (n - 1)
+            + [pl.BlockSpec((LANES, D_STEP, cols), lambda i, ids: (0, d0 // D_STEP + i, 0))]
+            + ([] if first else [total]),
+            out_specs=[half] * 2 if last else total,
+            scratch_shapes=[pltpu.VMEM((n * rows, cols), f32)] if last else [],
+        ),
+        compiler_params=pltpu.CompilerParams(vmem_limit_bytes=VMEM_LIMIT),
+        cost_estimate=pl.CostEstimate(
+            flops=6 * n * rows * dn * LANES * cols,
+            bytes_accessed=4 * dn * LANES * cols,
+            transcendentals=0,
+        ),
+        name="ladder_product",
+    )(ids, flipped, *arrived, ladder_ints, *([] if first else [acc]))
+
+
+def cycle_kernel(owners, steps, *refs):
+    a_refs, u_ref, (send_ref, keep_ref, acc_ref, flat_ref) = refs[:owners], refs[owners], refs[owners + 1 :]
+    step = pl.program_id(0)
+
+    @pl.when(step == 0)
+    def _():
+        acc_ref[...] = jnp.zeros_like(acc_ref)
+        flat_ref[...] = jnp.zeros_like(flat_ref)
+
+    u = u_ref[...]
+    a = jnp.concatenate([r[...] for r in a_refs], axis=0)
+    acc_ref[...] += dot_split(a, u.reshape(u.shape[0] * u.shape[1], u.shape[2]))
+
+    @pl.when(step == steps - 1)
+    def _():
+        window = acc_ref.shape[0] // owners
+        for k in range(owners):
+            for j in range(acc_ref.shape[1] // LANES):
+                for a in range(window):
+                    flat_ref[k * CYCLE_PAD + j : k * CYCLE_PAD + j + 1, a * LANES : (a + 1) * LANES] = acc_ref[
+                        k * window + a : k * window + a + 1, j * LANES : (j + 1) * LANES
+                    ]
+        pair_halves(flat_ref, send_ref, keep_ref)
+
+
+def cycle_product(windows, cycle_ints):
+    owners = len(windows)
+    window, depth = windows[0].shape
+    ks, cs, cols = cycle_ints.shape
+    kb = 8
+    steps = ks // kb
+    half = (owners * CYCLE_PAD, window * LANES // 2)
+    return pl.pallas_call(
+        functools.partial(cycle_kernel, owners, steps),
+        out_shape=[sds(*half)] * 2,
+        grid=(steps,),
+        in_specs=[pl.BlockSpec((window, kb * cs), lambda i: (0, i))] * owners
+        + [pl.BlockSpec((kb, cs, cols), lambda i: (i, 0, 0))],
+        out_specs=[pl.BlockSpec(half, lambda i: (0, 0))] * 2,
+        scratch_shapes=[
+            pltpu.VMEM((owners * window, cols), f32),
+            pltpu.VMEM((owners * CYCLE_PAD, window * LANES), f32),
+        ],
+        compiler_params=pltpu.CompilerParams(vmem_limit_bytes=VMEM_LIMIT),
+        cost_estimate=pl.CostEstimate(
+            flops=6 * owners * window * depth * cols, bytes_accessed=4 * depth * cols, transcendentals=0
+        ),
+        name="cycle_product",
+    )(*windows, cycle_ints)
+
+
+def add_blocks_kernel(keep_ref, recv_ref, *outs):
+    rows = outs[0].shape[0]
+    for k, out in enumerate(outs):
+        part = slice(k * rows, (k + 1) * rows)
+        out[...] = keep_ref[part] + recv_ref[part]
+
+
+def add_blocks(keep, recv, n):
+    rows, cols = keep.shape
+    return small(add_blocks_kernel, [sds(rows // n, cols)] * n, [keep, recv])
+
+
+def line_kernel(owners, owner_cols, *refs):
+    blocks, terms, outs, all_ref = refs[:owners], refs[owners : 2 * owners], refs[2 * owners : -1], refs[-1]
+    owner = lax.axis_index("occ")
+    total = terms[0][...]
+    for t in terms[1:]:
+        total = total + t[...]
+    all_ref[...] = 0.5 * total
+    for k, src in enumerate(blocks):
+        offset = (owner ^ k) * owner_cols
+        for j in range(owner_cols):
+            all_ref[pl.ds(offset + j, 1), :] += src[j : j + 1, :]
+    z = lax.axis_index("sec") // 2
+    for q, out in enumerate(outs):
+        out[...] = all_ref[:, block_of(z ^ q)]
+
+
+def final_kernel(*refs):
+    *terms, pair_ref, den_ref, live_ref, out_ref = refs
+    total = pair_ref[...]
+    for t in terms:
+        total = total + t[...]
+    out_ref[...] = total / den_ref[...] * live_ref[...]
+
+
+def streamed_parts(amplitudes, live_pairs, ladder_ints, cycle_ints, pair_ints, occ_energy, vir_energy):
+    owners = lax.axis_size("occ")
+    sections = lax.axis_size("sec")
+    owner_index = lax.axis_index("occ")
+    section = lax.axis_index("sec")
+    owner_rows = I_OWNER * OCCUPIED
+    owner_cols = OCCUPIED // owners
+    col_share = A_WINDOW * B_WINDOW // sections
+    d_share = amplitudes.shape[2]
+    ids = owner_index.reshape(1).astype(jnp.int32)
+    flipped = amplitudes.transpose(0, 2, 1)
+    live_count = lax.dynamic_slice_in_dim(live_pairs, owner_index, 1)[0]
+
+    def exchange(values):
+        return [
+            lax.ppermute(value, "occ", [(o, o ^ k) for o in range(owners)])
+            for k, value in enumerate(values, start=1)
+        ]
+
+    def swap_pair(value):
+        return lax.ppermute(value, "sec", [(s, s ^ 1) for s in range(sections)])
+
+    starts = [d_share * c // CHUNK_UNITS for c in CHUNKS]
+    chunks = list(zip(starts, [*starts[1:], d_share]))
+    window = cycle_window(live_pairs, flipped, A_WINDOW)
+    windows = [window] + exchange([window] * (owners - 1))
+    arrived = []
+    turn = window
+    for d0, d1 in chunks:
+        pieces = slice_chunk(after(ids, turn), flipped, owners, d0, d1 - d0)
+        arrived.append(exchange(pieces))
+        turn = pieces[0]
+
+    send, keep = cycle_product(windows, cycle_ints)
+    recv = swap_pair(send)
+    own, *sends = add_blocks(keep, recv, owners)
+    blocks = [own, *exchange(sends)]
+
+    acc = None
+    turn = own
+    for (d0, d1), values in zip(chunks, arrived):
+        acc = ladder_product(after(ids, turn), flipped, values, ladder_ints, acc, d0, d1 == d_share)
+        turn = ids
+    send, keep = acc
+    own, *sends = add_blocks(keep, swap_pair(send), owners)
+    terms = [*blocks, own, *exchange(sends)]
+    lines = sections // 2
+    pieces = small(
+        functools.partial(line_kernel, owners, owner_cols),
+        [sds(owner_rows, LANES)] * lines,
+        terms,
+        [pltpu.VMEM((owner_rows, lines * LANES), f32)],
+    )
+    recvs = [lax.ppermute(pieces[q], "sec", [(s, s ^ (2 * q)) for s in range(sections)]) for q in range(1, lines)]
+
+    occ_rows = lax.dynamic_slice_in_dim(occ_energy, owner_index * I_OWNER, I_OWNER)
+    pair_energy = (occ_rows[:, None] + occ_energy[None, :]).reshape(owner_rows, 1)
+    vir_pairs = (vir_energy[:A_WINDOW, None] + vir_energy[None, :B_WINDOW]).reshape(A_WINDOW * B_WINDOW)
+    vir_cols = lax.dynamic_slice_in_dim(vir_pairs, section * col_share, col_share)
+    denominator = pair_energy - vir_cols[None, :]
+    live_out = (lax.broadcasted_iota(jnp.int32, (owner_rows, col_share), 0) < live_count).astype(f32)
+    operands = [pieces[0], *recvs, pair_ints, denominator, live_out]
+    return small(final_kernel, sds(owner_rows, col_share), operands)
+
+
+def gathered(amplitudes, live_pairs, ladder_ints, cycle_ints, pair_ints, occ_energy, vir_energy):
     owners = lax.axis_size("occ")
     sections = lax.axis_size("sec")
     owner_index = lax.axis_index("occ")
@@ -72,6 +396,25 @@
     return residual / denominator * live_out
 
 
+def power_of_two(n):
+    return n & (n - 1) == 0
+
+
+def streams(owners, sections):
+    return (
+        1 < owners
+        and power_of_two(owners)
+        and 2 < sections
+        and power_of_two(sections)
+        and VIRTUAL == owners * LANES
+        and A_WINDOW * B_WINDOW == sections * LANES
+        and B_WINDOW == LANES
+        and OCCUPIED // owners <= CYCLE_PAD
+        and sections // 2 == owners
+        and VIRTUAL // sections % (D_STEP * CHUNK_UNITS) == 0
+    )
+
+
 def solution(mesh):
     in_specs = (
         P("occ", None, "sec"),
@@ -83,4 +426,6 @@
         P(),
     )
     out_specs = P("occ", "sec")
-    return jax.shard_map(shards, mesh=mesh, in_specs=in_specs, out_specs=out_specs, check_vma=False)
+    if not streams(mesh.shape["occ"], mesh.shape["sec"]):
+        return jax.shard_map(gathered, mesh=mesh, in_specs=in_specs, out_specs=out_specs, check_vma=False)
+    return jax.shard_map(streamed_parts, mesh=mesh, in_specs=in_specs, out_specs=out_specs, check_vma=False)

time: 236 us -> 137 us (0.58)
  blocking collectives: 75.8 us -> 0 us
  Pallas kernels: 0 us -> 52.8 us
  matrix products: 40.3 us -> 0 us
  starting transfers between devices: 5.33 us -> 35.5 us
  local copies, waits for them, and re-layouts: 34.6 us -> 11.1 us
  waiting for transfers between devices: 56.3 us -> 34.9 us
  between operations: 13.6 us -> 0.31 us
  other arithmetic: 9.64 us -> 1.46 us
    all_gather x1 -> x0, blocking collectives: 75.8 us -> none  [shards(): cycle_flat = lax.all_gather(cycle_local, 'occ', axis=0, tiled=True)]
    pallas_call x0 -> x14, Pallas kernels: none -> 52.8 us  [the longest x4 31.9 us: ladder_product(): pl.pallas_call(functools.partial(ladder_kernel, n, first, last, steps), o...]
    dot_general x2 -> x0, matrix products: 40.3 us -> none  [the longest x1 26.3 us: shards(): jnp.dot(regrouped.reshape(pair_total, -1), ladder_ints.reshape(-1, A_WIND...]
    ppermute x0 -> x26, starting transfers between devices: none -> 35.5 us  [the longest x21 31 us: exchange(): lax.ppermute(value, 'occ', [(o, o ^ k) for o in range(owners)])]
    ppermute x0 -> x26, waiting for transfers between devices: none -> 34.9 us  [the longest x21 30.1 us: exchange(): lax.ppermute(value, 'occ', [(o, o ^ k) for o in range(owners)])]
    reduce_scatter x1 -> x0, waiting for transfers between devices: 31.6 us -> none  [shards(): lax.psum_scatter(combined, 'sec', scatter_dimension=1, tiled=True)]
    unnamed x3 -> x0, waiting for transfers between devices: 24.7 us -> none
    reshape x5 -> x0, local copies, waits for them, and re-layouts: 21.3 us -> none  [the longest x2 21 us: shards(): flat_tiles = masked.reshape(owner_rows, owners, VIRTUAL // owners * d_share)]
  transfers between devices with their start and end apart: 3 -> 26, of which waited for: 2 -> 7; matrix products, arithmetic and copies ran while one was open for 7% -> 2% of each run, Pallas kernels for 0% -> 31%
where the time goes in v1:
time: 137 us; the launch traced here: 136 us
  Pallas kernels  52.8 us (39%)
  starting transfers between devices  35.5 us (26%)
  waiting for transfers between devices  34.9 us (25%)
  local copies, waits for them, and re-layouts  11.1 us (8%)
  other arithmetic  1.46 us (1%)
    pallas_call x4, Pallas kernels, ladder_product(): pl.pallas_call(functools.partial(ladder_kernel, n, first, last, steps), o...  31.9 us
    ppermute x21, starting transfers between devices, exchange(): lax.ppermute(value, 'occ', [(o, o ^ k) for o in range(owners)])  31 us
    ppermute x21, waiting for transfers between devices, exchange(): lax.ppermute(value, 'occ', [(o, o ^ k) for o in range(owners)])  30.1 us
    unnamed x48, local copies, waits for them, and re-layouts  9.71 us
    pallas_call x1, Pallas kernels, cycle_product(): pl.pallas_call(functools.partial(cycle_kernel, owners, steps), out_shape=...  9.46 us
    pallas_call x4, Pallas kernels, slice_chunk(): pl.pallas_call(lambda _, *refs: slice_kernel(d0, *refs), out_shape=[sds(r...  7.53 us
    ppermute x3, waiting for transfers between devices, streamed_parts(): lax.ppermute(pieces[q], 'sec', [(s, s ^ 2 * q) for s in range(sections)])  4.83 us
    ppermute x3, starting transfers between devices, streamed_parts(): lax.ppermute(pieces[q], 'sec', [(s, s ^ 2 * q) for s in range(sections)])  4.45 us
  transfers between devices with their start and end apart: 26, of which 7 were waited for; matrix products, arithmetic and copies ran while one was open for 2% of the time, Pallas kernels for 31%

profile of v1, /device:TPU:0, one launch (start us, length us, event | category | flops | bytes accessed | tf_op | source)
XLA Modules:
  0.0 136.1 jit_solution(13888375630605472543)
XLA Ops:
  0.7 2.4 %cycle_window.1.refs_0_ = f32[8,3072]{1,0:T(8,128)S(1)} custom-call(s32[4]{0:T(128)S(1)} %copy-done.7, f32[48,64,512]{2,1,0:T(8,128)} %bitcast.6), custom_call_target="tpu_custom_call" | custom-call | bytes 1572864 | tf_op jit(solution)/shard_map/cycle_window/pallas_call | solution.py:111
  3.0 2.5 %slices.4 = (f32[48,24,128]{2,1,0:T(8,128)S(1)}, f32[48,24,128]{2,1,0:T(8,128)}, f32[48,24,128]{2,1,0:T(8,128)}) custom-call(s32[1]{0:T(128)} %bitcast.1._.ids, f32[48,64,512]{2,1,0:T(8,128)} %bitcast.7), custom_call_target="tpu_custom_call" | custom-call | bytes 3538944 | tf_op jit(solution)/shard_map/slices/pallas_call | solution.py:90
  5.6 3.0 %collective-permute-start.16 = (f32[48,24,128]{2,1,0:T(8,128)S(1)}, f32[48,24,128]{2,1,0:T(8,128)S(1)}, u32[]{:S(2)}, u32[]{:S(2)}) collective-permute-start(f32[48,24,128]{2,1,0:T(8,128)S(1)} %get-tuple-element.47), channel_id=1, source_target_pairs={{0,8},{8,0},{16,24},{24,16},{1,9},{9,1},{17,25},{25,17},{2,10},{10... | collective-permute-start | bytes 1769480 | tf_op jit(solution)/shard_map/ppermute | solution.py:290
  8.7 2.0 %collective-permute-start.17 = (f32[48,24,128]{2,1,0:T(8,128)}, f32[48,24,128]{2,1,0:T(8,128)S(1)}, u32[]{:S(2)}, u32[]{:S(2)}) collective-permute-start(f32[48,24,128]{2,1,0:T(8,128)} %get-tuple-element.61), channel_id=1, source_target_pairs={{0,16},{8,24},{16,0},{24,8},{1,17},{9,25},{17,1},{25,9},{2,18},{10... | collective-permute-start | bytes 1769480 | tf_op jit(solution)/shard_map/ppermute | solution.py:290
  10.6 1.4 %collective-permute-start.18 = (f32[48,24,128]{2,1,0:T(8,128)}, f32[48,24,128]{2,1,0:T(8,128)S(1)}, u32[]{:S(2)}, u32[]{:S(2)}) collective-permute-start(f32[48,24,128]{2,1,0:T(8,128)} %get-tuple-element.62), channel_id=1, source_target_pairs={{0,24},{8,16},{16,8},{24,0},{1,25},{9,17},{17,9},{25,1},{2,26},{10... | collective-permute-start | bytes 1769480 | tf_op jit(solution)/shard_map/ppermute | solution.py:290
  12.1 1.5 %collective-permute-start.1 = (f32[8,3072]{1,0:T(8,128)S(1)}, f32[8,3072]{1,0:T(8,128)S(1)}, u32[]{:S(2)}, u32[]{:S(2)}) collective-permute-start(f32[8,3072]{1,0:T(8,128)S(1)} %cycle_window.1.refs_0_), channel_id=1, source_target_pairs={{0,16},{8,24},{16,0},{24,8},{1,17},{9,25},{17,1},{25,9},{2,18},{10... | collective-permute-start | bytes 294920 | tf_op jit(solution)/shard_map/ppermute | solution.py:290
  13.6 11.3 %collective-permute-done.refs_1_ = f32[8,3072]{1,0:T(8,128)S(1)} collective-permute-done((f32[8,3072]{1,0:T(8,128)S(1)}, f32[8,3072]{1,0:T(8,128)S(1)}, u32[]{:S(2)}, u32[]{:S(2)}) %collective-permute-start) | collective-permute-done | bytes 98336 | tf_op jit(solution)/shard_map/ppermute | solution.py:290
  24.9 3.0 %collective-permute-start.2 = (f32[8,3072]{1,0:T(8,128)S(1)}, f32[8,3072]{1,0:T(8,128)S(1)}, u32[]{:S(2)}, u32[]{:S(2)}) collective-permute-start(f32[8,3072]{1,0:T(8,128)S(1)} %cycle_window.1.refs_0_), channel_id=1, source_target_pairs={{0,24},{8,16},{16,8},{24,0},{1,25},{9,17},{17,9},{25,1},{2,26},{10... | collective-permute-start | bytes 294920 | tf_op jit(solution)/shard_map/ppermute | solution.py:290
  27.8 12.7 %collective-permute-done.1.refs_2_ = f32[8,3072]{1,0:T(8,128)S(1)} collective-permute-done((f32[8,3072]{1,0:T(8,128)S(1)}, f32[8,3072]{1,0:T(8,128)S(1)}, u32[]{:S(2)}, u32[]{:S(2)}) %collective-permute-start.1) | collective-permute-done | bytes 98336 | tf_op jit(solution)/shard_map/ppermute | solution.py:290
  40.5 9.5 %cycle_product.1 = (f32[64,512]{1,0:T(8,128)S(1)}, f32[64,512]{1,0:T(8,128)S(1)}) custom-call(f32[8,3072]{1,0:T(8,128)S(1)} %cycle_window.1.refs_0_, f32[8,3072]{1,0:T(8,128)S(1)} %collective-permute-done.refs_1_, f32[8,3072]{1,0:T(8,128)S(1)} %collective-permute-done.1.refs_2_, f32[8,3072]{1,0:T(8,128)S(1)} %collective-permute-done.2.refs_3_, ...), custom_call_target="tpu_custom_call" | custom-call | flops 905969664 | bytes 18874368 | tf_op jit(solution)/shard_map/cycle_product/pallas_call | solution.py:220
  50.6 2.7 %slices.5 = (f32[48,24,128]{2,1,0:T(8,128)}, f32[48,24,128]{2,1,0:T(8,128)}, f32[48,24,128]{2,1,0:T(8,128)}) custom-call(s32[1]{0:T(128)} %bitcast.1._.ids, f32[48,64,512]{2,1,0:T(8,128)} %bitcast.8), custom_call_target="tpu_custom_call" | custom-call | bytes 3538944 | tf_op jit(solution)/shard_map/slices/pallas_call | solution.py:90
  53.4 1.7 %collective-permute-start.13 = (f32[48,24,128]{2,1,0:T(8,128)}, f32[48,24,128]{2,1,0:T(8,128)S(1)}, u32[]{:S(2)}, u32[]{:S(2)}) collective-permute-start(f32[48,24,128]{2,1,0:T(8,128)} %get-tuple-element.49), channel_id=1, source_target_pairs={{0,8},{8,0},{16,24},{24,16},{1,9},{9,1},{17,25},{25,17},{2,10},{10... | collective-permute-start | bytes 1769480 | tf_op jit(solution)/shard_map/ppermute | solution.py:290
  55.8 1.5 %collective-permute-start.14 = (f32[48,24,128]{2,1,0:T(8,128)}, f32[48,24,128]{2,1,0:T(8,128)S(1)}, u32[]{:S(2)}, u32[]{:S(2)}) collective-permute-start(f32[48,24,128]{2,1,0:T(8,128)} %get-tuple-element.58), channel_id=1, source_target_pairs={{0,16},{8,24},{16,0},{24,8},{1,17},{9,25},{17,1},{25,9},{2,18},{10... | collective-permute-start | bytes 1769480 | tf_op jit(solution)/shard_map/ppermute | solution.py:290
  57.6 1.1 slices.6
  60.8 1.1 slices.7
  68.9 1.7 %collective-permute-start.10 = (f32[48,8,128]{2,1,0:T(8,128)}, f32[48,8,128]{2,1,0:T(8,128)S(1)}, u32[]{:S(2)}, u32[]{:S(2)}) collective-permute-start(f32[48,8,128]{2,1,0:T(8,128)} %copy-done.18), channel_id=1, source_target_pairs={{0,8},{8,0},{16,24},{24,16},{1,9},{9,1},{17,25},{25,17},{2,10},{10... | collective-permute-start | bytes 589832 | tf_op jit(solution)/shard_map/ppermute | solution.py:290
  70.6 1.6 %collective-permute-start.11 = (f32[48,8,128]{2,1,0:T(8,128)}, f32[48,8,128]{2,1,0:T(8,128)S(1)}, u32[]{:S(2)}, u32[]{:S(2)}) collective-permute-start(f32[48,8,128]{2,1,0:T(8,128)} %copy-done.17), channel_id=1, source_target_pairs={{0,16},{8,24},{16,0},{24,8},{1,17},{9,25},{17,1},{25,9},{2,18},{10... | collective-permute-start | bytes 589832 | tf_op jit(solution)/shard_map/ppermute | solution.py:290
  72.2 10.7 %ladder_product.4.refs_5_ = f32[192,1024]{1,0:T(8,128)S(1)} custom-call(s32[1]{0:T(128)} %bitcast.1._.ids, f32[48,64,512]{2,1,0:T(8,128)} %bitcast.11, f32[48,24,128]{2,1,0:T(8,128)S(1)} %collective-permute-done.16.refs_1_, f32[48,24,128]{2,1,0:T(8,128)S(1)} %collective-permute-done.17.refs_2_, f32[48,24,128]{2,1,0:T(8,128)S(1)} %collective-permute-done.18.refs_3_, ...), custom_call_target="tpu_custom_call" | custom-call | flops 3623878656 | bytes 12582912 | tf_op jit(solution)/shard_map/ladder_product/pallas_call | solution.py:165
  82.9 3.3 %collective-permute-done.10.refs_1_ = f32[48,8,128]{2,1,0:T(8,128)S(1)} collective-permute-done((f32[48,8,128]{2,1,0:T(8,128)}, f32[48,8,128]{2,1,0:T(8,128)S(1)}, u32[]{:S(2)}, u32[]{:S(2)}) %collective-permute-start.10) | collective-permute-done | bytes 196640 | tf_op jit(solution)/shard_map/ppermute | solution.py:290
  86.3 2.6 %collective-permute-start.12 = (f32[48,8,128]{2,1,0:T(8,128)S(1)}, f32[48,8,128]{2,1,0:T(8,128)S(1)}, u32[]{:S(2)}, u32[]{:S(2)}) collective-permute-start(f32[48,8,128]{2,1,0:T(8,128)S(1)} %copy-done.16), channel_id=1, source_target_pairs={{0,24},{8,16},{16,8},{24,0},{1,25},{9,17},{17,9},{25,1},{2,26},{10... | collective-permute-start | bytes 589832 | tf_op jit(solution)/shard_map/ppermute | solution.py:290
  89.8 2.6 %collective-permute-start.9 = (f32[48,8,128]{2,1,0:T(8,128)S(1)}, f32[48,8,128]{2,1,0:T(8,128)S(1)}, u32[]{:S(2)}, u32[]{:S(2)}) collective-permute-start(f32[48,8,128]{2,1,0:T(8,128)S(1)} %copy-done.10), channel_id=1, source_target_pairs={{0,24},{8,16},{16,8},{24,0},{1,25},{9,17},{17,9},{25,1},{2,26},{10... | collective-permute-start | bytes 589832 | tf_op jit(solution)/shard_map/ppermute | solution.py:290
  92.4 11.0 %ladder_product.5.refs_5_ = f32[192,1024]{1,0:T(8,128)S(1)} custom-call(s32[1]{0:T(128)} %bitcast.1._.ids, f32[48,64,512]{2,1,0:T(8,128)} %bitcast.12, f32[48,24,128]{2,1,0:T(8,128)S(1)} %collective-permute-done.13.refs_1_, f32[48,24,128]{2,1,0:T(8,128)S(1)} %collective-permute-done.14.refs_2_, f32[48,24,128]{2,1,0:T(8,128)S(1)} %collective-permute-done.15.refs_3_, ...), custom_call_target="tpu_custom_call" | custom-call | flops 3623878656 | bytes 12582912 | tf_op jit(solution)/shard_map/ladder_product/pallas_call | solution.py:165
  103.4 5.1 %ladder_product.6.refs_5_ = f32[192,1024]{1,0:T(8,128)S(1)} custom-call(s32[1]{0:T(128)} %bitcast.1._.ids, f32[48,64,512]{2,1,0:T(8,128)} %bitcast.13, f32[48,8,128]{2,1,0:T(8,128)S(1)} %collective-permute-done.10.refs_1_, f32[48,8,128]{2,1,0:T(8,128)S(1)} %collective-permute-done.11.refs_2_, f32[48,8,128]{2,1,0:T(8,128)S(1)} %collective-permute-done.12.refs_3_, ...), custom_call_target="tpu_custom_call" | custom-call | flops 1207959552 | bytes 4194304 | tf_op jit(solution)/shard_map/ladder_product/pallas_call | solution.py:165
  108.6 5.2 %ladder_product.7 = (f32[192,512]{1,0:T(8,128)S(1)}, f32[192,512]{1,0:T(8,128)S(1)}) custom-call(s32[1]{0:T(128)} %bitcast.1._.ids, f32[48,64,512]{2,1,0:T(8,128)} %bitcast.14, f32[48,8,128]{2,1,0:T(8,128)S(1)} %collective-permute-done.7.refs_1_, f32[48,8,128]{2,1,0:T(8,128)S(1)} %collective-permute-done.8.refs_2_, ...), custom_call_target="tpu_custom_call" | custom-call | flops 1207959552 | bytes 4194304 | tf_op jit(solution)/shard_map/ladder_product/pallas_call | solution.py:165
  115.6 2.6 %collective-permute-start.6 = (f32[16,512]{1,0:T(8,128)S(1)}, f32[16,512]{1,0:T(8,128)S(1)}, u32[]{:S(2)}, u32[]{:S(2)}) collective-permute-start(f32[16,512]{1,0:T(8,128)S(1)} %copy-done.20), channel_id=1, source_target_pairs={{0,24},{8,16},{16,8},{24,0},{1,25},{9,17},{17,9},{25,1},{2,26},{10... | collective-permute-start | bytes 98312 | tf_op jit(solution)/shard_map/ppermute | solution.py:290
  119.2 2.6 %collective-permute-start.22 = (f32[48,512]{1,0:T(8,128)S(1)}, f32[48,512]{1,0:T(8,128)S(1)}, u32[]{:S(2)}, u32[]{:S(2)}) collective-permute-start(f32[48,512]{1,0:T(8,128)S(1)} %get-tuple-element.68), channel_id=1, source_target_pairs={{0,24},{8,16},{16,8},{24,0},{1,25},{9,17},{17,9},{25,1},{2,26},{10... | collective-permute-start | bytes 294920 | tf_op jit(solution)/shard_map/ppermute | solution.py:290
  122.5 1.4 %collective-permute-done.20.refs_5_ = f32[48,512]{1,0:T(8,128)S(1)} collective-permute-done((f32[48,512]{1,0:T(8,128)S(1)}, f32[48,512]{1,0:T(8,128)S(1)}, u32[]{:S(2)}, u32[]{:S(2)}) %collective-permute-start.20) | collective-permute-done | bytes 98336 | tf_op jit(solution)/shard_map/ppermute | solution.py:290
  123.9 1.4 %collective-permute-done.21.refs_6_ = f32[48,512]{1,0:T(8,128)S(1)} collective-permute-done((f32[48,512]{1,0:T(8,128)S(1)}, f32[48,512]{1,0:T(8,128)S(1)}, u32[]{:S(2)}, u32[]{:S(2)}) %collective-permute-start.21) | collective-permute-done | bytes 98336 | tf_op jit(solution)/shard_map/ppermute | solution.py:290
  125.5 1.7 %collective-permute-start.23 = (f32[48,128]{1,0:T(8,128)S(1)}, f32[48,128]{1,0:T(8,128)S(1)}, u32[]{:S(2)}, u32[]{:S(2)}) collective-permute-start(f32[48,128]{1,0:T(8,128)S(1)} %get-tuple-element.70), channel_id=1, source_target_pairs={{0,2},{1,3},{2,0},{3,1},{4,6},{5,7},{6,4},{7,5},{8,10},{9,11},{10,... | collective-permute-start | bytes 73736 | tf_op jit(solution)/shard_map/ppermute | solution.py:328
  127.2 2.6 %collective-permute-start.24 = (f32[48,128]{1,0:T(8,128)S(1)}, f32[48,128]{1,0:T(8,128)S(1)}, u32[]{:S(2)}, u32[]{:S(2)}) collective-permute-start(f32[48,128]{1,0:T(8,128)S(1)} %get-tuple-element.71), channel_id=1, source_target_pairs={{0,4},{1,5},{2,6},{3,7},{4,0},{5,1},{6,2},{7,3},{8,12},{9,13},{10,... | collective-permute-start | bytes 73736 | tf_op jit(solution)/shard_map/ppermute | solution.py:328
  130.6 1.4 %collective-permute-done.24.refs_2_ = f32[48,128]{1,0:T(8,128)S(1)} collective-permute-done((f32[48,128]{1,0:T(8,128)S(1)}, f32[48,128]{1,0:T(8,128)S(1)}, u32[]{:S(2)}, u32[]{:S(2)}) %collective-permute-start.24) | collective-permute-done | bytes 24608 | tf_op jit(solution)/shard_map/ppermute | solution.py:328
  132.0 3.4 %collective-permute-done.25.refs_3_ = f32[48,128]{1,0:T(8,128)S(1)} collective-permute-done((f32[48,128]{1,0:T(8,128)S(1)}, f32[48,128]{1,0:T(8,128)S(1)}, u32[]{:S(2)}, u32[]{:S(2)}) %collective-permute-start.25) | collective-permute-done | bytes 24608 | tf_op jit(solution)/shard_map/ppermute | solution.py:328
  (94 shorter events, 17.4 us)
Async XLA Ops:
  5.6 51.7 %collective-permute-start.16 = (f32[48,24,128]{2,1,0:T(8,128)S(1)}, f32[48,24,128]{2,1,0:T(8,128)S(1)}, u32[]{:S(2)}, u32[]{:S(2)}) collective-permute-start(f32[48,24,128]{2,1,0:T(8,128)S(1)} %get-tuple-element.47), channel_id=1, source_target_pairs={{0,8},{8,0},{16,24},{24,16},{1,9},{9,1},{17,25},{25,17},{2,10},{10... | collective-permute-start | bytes 1769480 | tf_op jit(solution)/shard_map/ppermute | solution.py:290
  8.6 16.3 %collective-permute-start = (f32[8,3072]{1,0:T(8,128)S(1)}, f32[8,3072]{1,0:T(8,128)S(1)}, u32[]{:S(2)}, u32[]{:S(2)}) collective-permute-start(f32[8,3072]{1,0:T(8,128)S(1)} %cycle_window.1.refs_0_), channel_id=1, source_target_pairs={{0,8},{8,0},{16,24},{24,16},{1,9},{9,1},{17,25},{25,17},{2,10},{10... | collective-permute-start | bytes 294920 | tf_op jit(solution)/shard_map/ppermute | solution.py:290
  8.7 60.3 %collective-permute-start.17 = (f32[48,24,128]{2,1,0:T(8,128)}, f32[48,24,128]{2,1,0:T(8,128)S(1)}, u32[]{:S(2)}, u32[]{:S(2)}) collective-permute-start(f32[48,24,128]{2,1,0:T(8,128)} %get-tuple-element.61), channel_id=1, source_target_pairs={{0,16},{8,24},{16,0},{24,8},{1,17},{9,25},{17,1},{25,9},{2,18},{10... | collective-permute-start | bytes 1769480 | tf_op jit(solution)/shard_map/ppermute | solution.py:290
  10.6 53.4 %copy-start.23 = (f32[48]{0:T(128)S(1)}, f32[48]{0:T(128)}, u32[]{:S(2)}) copy-start(f32[48]{0:T(128)} %param.12) | copy-start | bytes 580
  10.6 59.9 %collective-permute-start.18 = (f32[48,24,128]{2,1,0:T(8,128)}, f32[48,24,128]{2,1,0:T(8,128)S(1)}, u32[]{:S(2)}, u32[]{:S(2)}) collective-permute-start(f32[48,24,128]{2,1,0:T(8,128)} %get-tuple-element.62), channel_id=1, source_target_pairs={{0,24},{8,16},{16,8},{24,0},{1,25},{9,17},{17,9},{25,1},{2,26},{10... | collective-permute-start | bytes 1769480 | tf_op jit(solution)/shard_map/ppermute | solution.py:290
  12.1 28.4 %collective-permute-start.1 = (f32[8,3072]{1,0:T(8,128)S(1)}, f32[8,3072]{1,0:T(8,128)S(1)}, u32[]{:S(2)}, u32[]{:S(2)}) collective-permute-start(f32[8,3072]{1,0:T(8,128)S(1)} %cycle_window.1.refs_0_), channel_id=1, source_target_pairs={{0,16},{8,24},{16,0},{24,8},{1,17},{9,25},{17,1},{25,9},{2,18},{10... | collective-permute-start | bytes 294920 | tf_op jit(solution)/shard_map/ppermute | solution.py:290
  24.9 15.6 %collective-permute-start.2 = (f32[8,3072]{1,0:T(8,128)S(1)}, f32[8,3072]{1,0:T(8,128)S(1)}, u32[]{:S(2)}, u32[]{:S(2)}) collective-permute-start(f32[8,3072]{1,0:T(8,128)S(1)} %cycle_window.1.refs_0_), channel_id=1, source_target_pairs={{0,24},{8,16},{16,8},{24,0},{1,25},{9,17},{17,9},{25,1},{2,26},{10... | collective-permute-start | bytes 294920 | tf_op jit(solution)/shard_map/ppermute | solution.py:290
  50.6 4.5 %collective-permute-start.3 = (f32[64,512]{1,0:T(8,128)S(1)}, f32[64,512]{1,0:T(8,128)S(1)}, u32[]{:S(2)}, u32[]{:S(2)}) collective-permute-start(f32[64,512]{1,0:T(8,128)S(1)} %get-tuple-element.40), channel_id=1, source_target_pairs={{0,1},{1,0},{2,3},{3,2},{4,5},{5,4},{6,7},{7,6},{8,9},{9,8},{10,11... | collective-permute-start | bytes 393224 | tf_op jit(solution)/shard_map/ppermute | solution.py:295
  53.4 35.5 %collective-permute-start.13 = (f32[48,24,128]{2,1,0:T(8,128)}, f32[48,24,128]{2,1,0:T(8,128)S(1)}, u32[]{:S(2)}, u32[]{:S(2)}) collective-permute-start(f32[48,24,128]{2,1,0:T(8,128)} %get-tuple-element.49), channel_id=1, source_target_pairs={{0,8},{8,0},{16,24},{24,16},{1,9},{9,1},{17,25},{25,17},{2,10},{10... | collective-permute-start | bytes 1769480 | tf_op jit(solution)/shard_map/ppermute | solution.py:290
  55.8 33.7 %collective-permute-start.14 = (f32[48,24,128]{2,1,0:T(8,128)}, f32[48,24,128]{2,1,0:T(8,128)S(1)}, u32[]{:S(2)}, u32[]{:S(2)}) collective-permute-start(f32[48,24,128]{2,1,0:T(8,128)} %get-tuple-element.58), channel_id=1, source_target_pairs={{0,16},{8,24},{16,0},{24,8},{1,17},{9,25},{17,1},{25,9},{2,18},{10... | collective-permute-start | bytes 1769480 | tf_op jit(solution)/shard_map/ppermute | solution.py:290
  57.3 32.5 %collective-permute-start.15 = (f32[48,24,128]{2,1,0:T(8,128)}, f32[48,24,128]{2,1,0:T(8,128)S(1)}, u32[]{:S(2)}, u32[]{:S(2)}) collective-permute-start(f32[48,24,128]{2,1,0:T(8,128)} %get-tuple-element.59), channel_id=1, source_target_pairs={{0,24},{8,16},{16,8},{24,0},{1,25},{9,17},{17,9},{25,1},{2,26},{10... | collective-permute-start | bytes 1769480 | tf_op jit(solution)/shard_map/ppermute | solution.py:290
  68.9 17.4 %collective-permute-start.10 = (f32[48,8,128]{2,1,0:T(8,128)}, f32[48,8,128]{2,1,0:T(8,128)S(1)}, u32[]{:S(2)}, u32[]{:S(2)}) collective-permute-start(f32[48,8,128]{2,1,0:T(8,128)} %copy-done.18), channel_id=1, source_target_pairs={{0,8},{8,0},{16,24},{24,16},{1,9},{9,1},{17,25},{25,17},{2,10},{10... | collective-permute-start | bytes 589832 | tf_op jit(solution)/shard_map/ppermute | solution.py:290
  70.6 18.3 %copy-start.14 = (f32[48,8,128]{2,1,0:T(8,128)S(1)}, f32[48,8,128]{2,1,0:T(8,128)}, u32[]{:S(2)}) copy-start(f32[48,8,128]{2,1,0:T(8,128)} %copy-done.13) | copy-start | bytes 589828
  70.6 18.9 %copy-start.12 = (f32[48,8,128]{2,1,0:T(8,128)S(1)}, f32[48,8,128]{2,1,0:T(8,128)}, u32[]{:S(2)}) copy-start(f32[48,8,128]{2,1,0:T(8,128)} %copy-done.11) | copy-start | bytes 589828
  70.6 19.2 %copy-start.10 = (f32[48,8,128]{2,1,0:T(8,128)S(1)}, f32[48,8,128]{2,1,0:T(8,128)}, u32[]{:S(2)}) copy-start(f32[48,8,128]{2,1,0:T(8,128)} %copy-done.9) | copy-start | bytes 589828
  70.6 32.8 %collective-permute-start.11 = (f32[48,8,128]{2,1,0:T(8,128)}, f32[48,8,128]{2,1,0:T(8,128)S(1)}, u32[]{:S(2)}, u32[]{:S(2)}) collective-permute-start(f32[48,8,128]{2,1,0:T(8,128)} %copy-done.17), channel_id=1, source_target_pairs={{0,16},{8,24},{16,0},{24,8},{1,17},{9,25},{17,1},{25,9},{2,18},{10... | collective-permute-start | bytes 589832 | tf_op jit(solution)/shard_map/ppermute | solution.py:290
  86.3 17.1 %collective-permute-start.12 = (f32[48,8,128]{2,1,0:T(8,128)S(1)}, f32[48,8,128]{2,1,0:T(8,128)S(1)}, u32[]{:S(2)}, u32[]{:S(2)}) collective-permute-start(f32[48,8,128]{2,1,0:T(8,128)S(1)} %copy-done.16), channel_id=1, source_target_pairs={{0,24},{8,16},{16,8},{24,0},{1,25},{9,17},{17,9},{25,1},{2,26},{10... | collective-permute-start | bytes 589832 | tf_op jit(solution)/shard_map/ppermute | solution.py:290
  88.9 19.6 %collective-permute-start.7 = (f32[48,8,128]{2,1,0:T(8,128)S(1)}, f32[48,8,128]{2,1,0:T(8,128)S(1)}, u32[]{:S(2)}, u32[]{:S(2)}) collective-permute-start(f32[48,8,128]{2,1,0:T(8,128)S(1)} %copy-done.14), channel_id=1, source_target_pairs={{0,8},{8,0},{16,24},{24,16},{1,9},{9,1},{17,25},{25,17},{2,10},{10... | collective-permute-start | bytes 589832 | tf_op jit(solution)/shard_map/ppermute | solution.py:290
  89.5 19.1 %collective-permute-start.8 = (f32[48,8,128]{2,1,0:T(8,128)S(1)}, f32[48,8,128]{2,1,0:T(8,128)S(1)}, u32[]{:S(2)}, u32[]{:S(2)}) collective-permute-start(f32[48,8,128]{2,1,0:T(8,128)S(1)} %copy-done.12), channel_id=1, source_target_pairs={{0,16},{8,24},{16,0},{24,8},{1,17},{9,25},{17,1},{25,9},{2,18},{10... | collective-permute-start | bytes 589832 | tf_op jit(solution)/shard_map/ppermute | solution.py:290
  89.8 18.8 %collective-permute-start.9 = (f32[48,8,128]{2,1,0:T(8,128)S(1)}, f32[48,8,128]{2,1,0:T(8,128)S(1)}, u32[]{:S(2)}, u32[]{:S(2)}) collective-permute-start(f32[48,8,128]{2,1,0:T(8,128)S(1)} %copy-done.10), channel_id=1, source_target_pairs={{0,24},{8,16},{16,8},{24,0},{1,25},{9,17},{17,9},{25,1},{2,26},{10... | collective-permute-start | bytes 589832 | tf_op jit(solution)/shard_map/ppermute | solution.py:290
  108.5 16.7 %copy-start.5 = (f32[16,512]{1,0:T(8,128)S(1)}, f32[16,512]{1,0:T(8,128)}, u32[]{:S(2)}) copy-start(f32[16,512]{1,0:T(8,128)} %copy-done.4) | copy-start | bytes 98308
  108.5 26.9 %copy-start.6 = (f32[48,128]{1,0:T(8,128)S(1)}, f32[48,128]{1,0:T(8,128)}, u32[]{:S(2)}) copy-start(f32[48,128]{1,0:T(8,128)} %refs_4_.11) | copy-start | bytes 73732
  113.8 4.5 %collective-permute-start.19 = (f32[192,512]{1,0:T(8,128)S(1)}, f32[192,512]{1,0:T(8,128)S(1)}, u32[]{:S(2)}, u32[]{:S(2)}) collective-permute-start(f32[192,512]{1,0:T(8,128)S(1)} %get-tuple-element.64), channel_id=1, source_target_pairs={{0,1},{1,0},{2,3},{3,2},{4,5},{5,4},{6,7},{7,6},{8,9},{9,8},{10,11... | collective-permute-start | bytes 1179656 | tf_op jit(solution)/shard_map/ppermute | solution.py:295
  113.9 5.3 %collective-permute-start.4 = (f32[16,512]{1,0:T(8,128)}, f32[16,512]{1,0:T(8,128)S(1)}, u32[]{:S(2)}, u32[]{:S(2)}) collective-permute-start(f32[16,512]{1,0:T(8,128)} %get-tuple-element.42), channel_id=1, source_target_pairs={{0,8},{8,0},{16,24},{24,16},{1,9},{9,1},{17,25},{25,17},{2,10},{10... | collective-permute-start | bytes 98312 | tf_op jit(solution)/shard_map/ppermute | solution.py:290
  115.2 7.2 %collective-permute-start.5 = (f32[16,512]{1,0:T(8,128)S(1)}, f32[16,512]{1,0:T(8,128)S(1)}, u32[]{:S(2)}, u32[]{:S(2)}) collective-permute-start(f32[16,512]{1,0:T(8,128)S(1)} %copy-done.22), channel_id=1, source_target_pairs={{0,16},{8,24},{16,0},{24,8},{1,17},{9,25},{17,1},{25,9},{2,18},{10... | collective-permute-start | bytes 98312 | tf_op jit(solution)/shard_map/ppermute | solution.py:290
  115.6 6.9 %collective-permute-start.6 = (f32[16,512]{1,0:T(8,128)S(1)}, f32[16,512]{1,0:T(8,128)S(1)}, u32[]{:S(2)}, u32[]{:S(2)}) collective-permute-start(f32[16,512]{1,0:T(8,128)S(1)} %copy-done.20), channel_id=1, source_target_pairs={{0,24},{8,16},{16,8},{24,0},{1,25},{9,17},{17,9},{25,1},{2,26},{10... | collective-permute-start | bytes 98312 | tf_op jit(solution)/shard_map/ppermute | solution.py:290
  118.2 5.6 %collective-permute-start.20 = (f32[48,512]{1,0:T(8,128)S(1)}, f32[48,512]{1,0:T(8,128)S(1)}, u32[]{:S(2)}, u32[]{:S(2)}) collective-permute-start(f32[48,512]{1,0:T(8,128)S(1)} %get-tuple-element.66), channel_id=1, source_target_pairs={{0,8},{8,0},{16,24},{24,16},{1,9},{9,1},{17,25},{25,17},{2,10},{10... | collective-permute-start | bytes 294920 | tf_op jit(solution)/shard_map/ppermute | solution.py:290
  118.9 6.4 %collective-permute-start.21 = (f32[48,512]{1,0:T(8,128)S(1)}, f32[48,512]{1,0:T(8,128)S(1)}, u32[]{:S(2)}, u32[]{:S(2)}) collective-permute-start(f32[48,512]{1,0:T(8,128)S(1)} %get-tuple-element.67), channel_id=1, source_target_pairs={{0,16},{8,24},{16,0},{24,8},{1,17},{9,25},{17,1},{25,9},{2,18},{10... | collective-permute-start | bytes 294920 | tf_op jit(solution)/shard_map/ppermute | solution.py:290
  119.2 6.1 %collective-permute-start.22 = (f32[48,512]{1,0:T(8,128)S(1)}, f32[48,512]{1,0:T(8,128)S(1)}, u32[]{:S(2)}, u32[]{:S(2)}) collective-permute-start(f32[48,512]{1,0:T(8,128)S(1)} %get-tuple-element.68), channel_id=1, source_target_pairs={{0,24},{8,16},{16,8},{24,0},{1,25},{9,17},{17,9},{25,1},{2,26},{10... | collective-permute-start | bytes 294920 | tf_op jit(solution)/shard_map/ppermute | solution.py:290
  125.5 5.1 %collective-permute-start.23 = (f32[48,128]{1,0:T(8,128)S(1)}, f32[48,128]{1,0:T(8,128)S(1)}, u32[]{:S(2)}, u32[]{:S(2)}) collective-permute-start(f32[48,128]{1,0:T(8,128)S(1)} %get-tuple-element.70), channel_id=1, source_target_pairs={{0,2},{1,3},{2,0},{3,1},{4,6},{5,7},{6,4},{7,5},{8,10},{9,11},{10,... | collective-permute-start | bytes 73736 | tf_op jit(solution)/shard_map/ppermute | solution.py:328
  127.2 4.8 %collective-permute-start.24 = (f32[48,128]{1,0:T(8,128)S(1)}, f32[48,128]{1,0:T(8,128)S(1)}, u32[]{:S(2)}, u32[]{:S(2)}) collective-permute-start(f32[48,128]{1,0:T(8,128)S(1)} %get-tuple-element.71), channel_id=1, source_target_pairs={{0,4},{1,5},{2,6},{3,7},{4,0},{5,1},{6,2},{7,3},{8,12},{9,13},{10,... | collective-permute-start | bytes 73736 | tf_op jit(solution)/shard_map/ppermute | solution.py:328
  129.8 5.6 %collective-permute-start.25 = (f32[48,128]{1,0:T(8,128)S(1)}, f32[48,128]{1,0:T(8,128)S(1)}, u32[]{:S(2)}, u32[]{:S(2)}) collective-permute-start(f32[48,128]{1,0:T(8,128)S(1)} %get-tuple-element.72), channel_id=1, source_target_pairs={{0,6},{1,7},{2,4},{3,5},{4,2},{5,3},{6,0},{7,1},{8,14},{9,15},{10,... | collective-permute-start | bytes 73736 | tf_op jit(solution)/shard_map/ppermute | solution.py:328
  (20 other events, 63.3 us)

commit v2 on v1

--- a/solution.py
+++ b/solution.py
@@ -16,7 +16,7 @@
 LANES = 128
 D_STEP = 8
 CHUNK_UNITS = 8
-CHUNKS = (0, 3, 6, 7)
+CHUNKS = (0, 1, 5, 7)
 CYCLE_PAD = 16
 
 
@@ -24,7 +24,7 @@
 bf16 = jnp.bfloat16
 highest = lax.Precision.HIGHEST
 VMEM_LIMIT = 48 * 1024 * 1024
-SMALL_LIMIT = 16 * 1024 * 1024
+SMALL_LIMIT = 24 * 1024 * 1024
 
 
 def split(x):
@@ -36,10 +36,9 @@
     return jnp.dot(a, b, preferred_element_type=f32)
 
 
-def dot_split(a, w):
+def dot_split(a, w_hi, w_lo):
     rows = a.shape[0]
     a_hi, a_lo = split(a)
-    w_hi, w_lo = split(w)
     both = dot(jnp.concatenate([a_hi, a_lo], axis=0), w_hi)
     return both[:rows] + both[rows:] + dot(a_hi, w_lo)
 
@@ -71,12 +70,12 @@
     return pl.ds(pl.multiple_of(index * LANES, LANES), LANES)
 
 
-def slice_kernel(d0, a_ref, *refs):
+def slice_kernel(d0, first, turn_ref, a_ref, *refs):
     outs, sem = refs[:-1], refs[-1]
     owner = lax.axis_index("occ")
     copies = [
-        pltpu.make_async_copy(a_ref.at[:, pl.ds(d0, out.shape[1]), block_of(owner ^ k)], out, sem.at[k - 1])
-        for k, out in enumerate(outs, start=1)
+        pltpu.make_async_copy(a_ref.at[:, pl.ds(d0, out.shape[1]), block_of(owner ^ k)], out, sem.at[k - first])
+        for k, out in enumerate(outs, start=first)
     ]
     for copy in copies:
         copy.start()
@@ -84,11 +83,11 @@
         copy.wait()
 
 
-def slice_chunk(turn, flipped, owners, d0, dn):
+def slice_chunk(turn, flipped, owners, d0, dn, first=1):
     rows = flipped.shape[0]
-    n = owners - 1
-    return pl.pallas_call(
-        lambda _, *refs: slice_kernel(d0, *refs),
+    n = owners - first
+    return pl.pallas_call(
+        functools.partial(slice_kernel, d0, first),
         out_shape=[sds(rows, dn, LANES)] * n,
         in_specs=[pl.BlockSpec(memory_space=pl.ANY)] * 2,
         out_specs=[pl.BlockSpec(memory_space=pltpu.VMEM)] * n,
@@ -99,51 +98,56 @@
     )(turn, flipped)
 
 
-def window_kernel(window, counts, a_ref, out_ref):
-    rows, depth, _ = a_ref.shape
-    flat = a_ref[...].reshape(rows * depth, LANES)
-    pair = lax.broadcasted_iota(jnp.int32, (window, rows * depth), 1) // depth
-    out_ref[...] = jnp.where(pair < counts[lax.axis_index("occ")], flat.T[:window], 0.0)
-
-
-def cycle_window(counts, flipped, window):
+def window_kernel(turn_ref, counts, a_ref, out_ref, tile_ref, sem):
+    parts, rows, depth, _ = tile_ref.shape
+    copies = [
+        pltpu.make_async_copy(a_ref.at[pl.ds(p * rows, rows), :, pl.ds(0, LANES)], tile_ref.at[p], sem.at[p])
+        for p in range(parts)
+    ]
+    for copy in copies:
+        copy.start()
+    live = counts[lax.axis_index("occ")]
+    window = out_ref.shape[1]
+    per_tile = LANES // depth
+    pair = lax.broadcasted_iota(jnp.int32, (window, LANES), 1) // depth
+    for p, copy in enumerate(copies):
+        copy.wait()
+        for t in range(rows // per_tile):
+            flat = tile_ref[p, pl.ds(t * per_tile, per_tile)].reshape(LANES, LANES)
+            tile = p * (rows // per_tile) + t
+            out_ref[tile] = jnp.where(pair + tile * per_tile < live, flat.T[:window], 0.0)
+
+
+def cycle_window(turn, counts, flipped, window):
     rows, depth, _ = flipped.shape
-    return pl.pallas_call(
-        functools.partial(window_kernel, window),
-        out_shape=sds(window, rows * depth),
-        grid_spec=pltpu.PrefetchScalarGridSpec(
-            num_scalar_prefetch=1,
-            grid=(1,),
-            in_specs=[pl.BlockSpec((rows, depth, LANES), lambda i, counts: (0, 0, 0))],
-            out_specs=pl.BlockSpec((window, rows * depth), lambda i, counts: (0, 0)),
-        ),
+    hbm = pl.BlockSpec(memory_space=pl.ANY)
+    return pl.pallas_call(
+        window_kernel,
+        out_shape=sds(rows * depth // LANES, window, LANES),
+        in_specs=[hbm, pl.BlockSpec(memory_space=pltpu.SMEM), hbm],
+        out_specs=pl.BlockSpec(memory_space=pltpu.VMEM),
+        scratch_shapes=[pltpu.VMEM((4, rows // 4, depth, LANES), f32), pltpu.SemaphoreType.DMA((4,))],
         compiler_params=pltpu.CompilerParams(vmem_limit_bytes=VMEM_LIMIT),
         cost_estimate=pl.CostEstimate(flops=0, bytes_accessed=4 * rows * depth * LANES, transcendentals=0),
         name="cycle_window",
-    )(counts, flipped)
-
-
-def ladder_kernel(n, first, last, steps, ids, *refs):
+    )(turn, counts, flipped)
+
+
+def two_steps(refs, d):
+    return jnp.concatenate([jnp.concatenate([r[:, d, :], r[:, d + 1, :]], axis=1) for r in refs], axis=0)
+
+
+def ladder_kernel(n, first, ids, *refs):
     a_refs, w_ref, rest = refs[:n], refs[n], refs[n + 1 :]
     acc_ref = rest[-1]
-    step = pl.program_id(0)
-
-    @pl.when(step == 0)
+
+    @pl.when(pl.program_id(0) == 0)
     def _():
         acc_ref[...] = jnp.zeros_like(acc_ref) if first else rest[0][...]
 
     for d in range(0, D_STEP, 2):
-        a = jnp.concatenate(
-            [jnp.concatenate([r[:, d, :], r[:, d + 1, :]], axis=1) for r in a_refs], axis=0
-        )
         w = jnp.concatenate([w_ref[:, d, :], w_ref[:, d + 1, :]], axis=0)
-        acc_ref[...] += dot_split(a, w)
-
-    if last:
-
-        @pl.when(step == steps - 1)
-        def _():
-            pair_halves(acc_ref, rest[-3], rest[-2])
+        acc_ref[...] += dot_split(two_steps(a_refs, d), *split(w))
 
 
 def pair_halves(src_ref, send_ref, keep_ref):
@@ -154,26 +158,23 @@
         keep_ref[:, cols] = src_ref[:, block_of(2 * z + core)]
 
 
-def ladder_product(ids, flipped, arrived, ladder_ints, acc, d0, last):
+def ladder_product(ids, flipped, arrived, ladder_ints, acc, d0, dn):
     n = len(arrived) + 1
-    rows, dn, _ = arrived[0].shape
+    rows = flipped.shape[0]
     cols = ladder_ints.shape[2]
     first = acc is None
-    steps = dn // D_STEP
     total = pl.BlockSpec((n * rows, cols), lambda i, ids: (0, 0))
-    half = pl.BlockSpec((n * rows, cols // 2), lambda i, ids: (0, 0))
-    return pl.pallas_call(
-        functools.partial(ladder_kernel, n, first, last, steps),
-        out_shape=[sds(n * rows, cols // 2)] * 2 if last else sds(n * rows, cols),
+    return pl.pallas_call(
+        functools.partial(ladder_kernel, n, first),
+        out_shape=sds(n * rows, cols),
         grid_spec=pltpu.PrefetchScalarGridSpec(
             num_scalar_prefetch=1,
-            grid=(steps,),
+            grid=(dn // D_STEP,),
             in_specs=[pl.BlockSpec((rows, D_STEP, LANES), lambda i, ids: (0, d0 // D_STEP + i, ids[0]))]
             + [pl.BlockSpec((rows, D_STEP, LANES), lambda i, ids: (0, i, 0))] * (n - 1)
             + [pl.BlockSpec((LANES, D_STEP, cols), lambda i, ids: (0, d0 // D_STEP + i, 0))]
             + ([] if first else [total]),
-            out_specs=[half] * 2 if last else total,
-            scratch_shapes=[pltpu.VMEM((n * rows, cols), f32)] if last else [],
+            out_specs=total,
         ),
         compiler_params=pltpu.CompilerParams(vmem_limit_bytes=VMEM_LIMIT),
         cost_estimate=pl.CostEstimate(
@@ -185,6 +186,42 @@
     )(ids, flipped, *arrived, ladder_ints, *([] if first else [acc]))
 
 
+def fetch_kernel(d0, turn_ref, w_ref, hi_ref, lo_ref, raw_ref, sem):
+    copies = [
+        pltpu.make_async_copy(w_ref.at[:, d0 + d, :], raw_ref.at[d], sem.at[d]) for d in range(raw_ref.shape[0])
+    ]
+    for copy in copies:
+        copy.start()
+    for d, copy in enumerate(copies):
+        copy.wait()
+        hi_ref[d], lo_ref[d] = split(raw_ref[d])
+
+
+def fetch_integrals(turn, ladder_ints, d0):
+    depth, _, cols = ladder_ints.shape
+    vmem = pl.BlockSpec(memory_space=pltpu.VMEM)
+    return pl.pallas_call(
+        functools.partial(fetch_kernel, d0),
+        out_shape=[jax.ShapeDtypeStruct((D_STEP, depth, cols), bf16)] * 2,
+        in_specs=[pl.BlockSpec(memory_space=pl.ANY)] * 2,
+        out_specs=[vmem] * 2,
+        scratch_shapes=[pltpu.VMEM((D_STEP, depth, cols), f32), pltpu.SemaphoreType.DMA((D_STEP,))],
+        compiler_params=pltpu.CompilerParams(vmem_limit_bytes=SMALL_LIMIT),
+        cost_estimate=pl.CostEstimate(flops=0, bytes_accessed=8 * D_STEP * depth * cols, transcendentals=0),
+        name="fetch_integrals",
+    )(turn, ladder_ints)
+
+
+def closing_kernel(n, *refs):
+    a_refs, (hi_ref, lo_ref, acc_in, send_ref, keep_ref, acc_ref) = refs[:n], refs[n:]
+    acc_ref[...] = acc_in[...]
+    for d in range(0, D_STEP, 2):
+        w_hi = hi_ref[d : d + 2].reshape(2 * LANES, -1)
+        w_lo = lo_ref[d : d + 2].reshape(2 * LANES, -1)
+        acc_ref[...] += dot_split(two_steps(a_refs, d), w_hi, w_lo)
+    pair_halves(acc_ref, send_ref, keep_ref)
+
+
 def cycle_kernel(owners, steps, *refs):
     a_refs, u_ref, (send_ref, keep_ref, acc_ref, flat_ref) = refs[:owners], refs[owners], refs[owners + 1 :]
     step = pl.program_id(0)
@@ -195,8 +232,9 @@
         flat_ref[...] = jnp.zeros_like(flat_ref)
 
     u = u_ref[...]
-    a = jnp.concatenate([r[...] for r in a_refs], axis=0)
-    acc_ref[...] += dot_split(a, u.reshape(u.shape[0] * u.shape[1], u.shape[2]))
+    tiles = a_refs[0].shape[0]
+    a = jnp.concatenate([jnp.concatenate([r[t] for t in range(tiles)], axis=1) for r in a_refs], axis=0)
+    acc_ref[...] += dot_split(a, *split(u.reshape(u.shape[0] * u.shape[1], u.shape[2])))
 
     @pl.when(step == steps - 1)
     def _():
@@ -210,18 +248,19 @@
         pair_halves(flat_ref, send_ref, keep_ref)
 
 
-def cycle_product(windows, cycle_ints):
-    owners = len(windows)
-    window, depth = windows[0].shape
+def cycle_product(own, arrived, cycle_ints):
+    owners = len(arrived) + 1
+    tiles, window, _ = own.shape
     ks, cs, cols = cycle_ints.shape
     kb = 8
     steps = ks // kb
+    per_step = tiles // steps
     half = (owners * CYCLE_PAD, window * LANES // 2)
     return pl.pallas_call(
         functools.partial(cycle_kernel, owners, steps),
         out_shape=[sds(*half)] * 2,
         grid=(steps,),
-        in_specs=[pl.BlockSpec((window, kb * cs), lambda i: (0, i))] * owners
+        in_specs=[pl.BlockSpec((per_step, window, LANES), lambda i: (i, 0, 0))] * owners
         + [pl.BlockSpec((kb, cs, cols), lambda i: (i, 0, 0))],
         out_specs=[pl.BlockSpec(half, lambda i: (0, 0))] * 2,
         scratch_shapes=[
@@ -230,10 +269,10 @@
         ],
         compiler_params=pltpu.CompilerParams(vmem_limit_bytes=VMEM_LIMIT),
         cost_estimate=pl.CostEstimate(
-            flops=6 * owners * window * depth * cols, bytes_accessed=4 * depth * cols, transcendentals=0
+            flops=6 * owners * window * ks * cs * cols, bytes_accessed=4 * ks * cs * cols, transcendentals=0
         ),
         name="cycle_product",
-    )(*windows, cycle_ints)
+    )(own, *arrived, cycle_ints)
 
 
 def add_blocks_kernel(keep_ref, recv_ref, *outs):
@@ -248,20 +287,25 @@
     return small(add_blocks_kernel, [sds(rows // n, cols)] * n, [keep, recv])
 
 
-def line_kernel(owners, owner_cols, *refs):
-    blocks, terms, outs, all_ref = refs[:owners], refs[owners : 2 * owners], refs[2 * owners : -1], refs[-1]
+def place_kernel(owner_cols, *refs):
+    blocks, out_ref = refs[:-1], refs[-1]
     owner = lax.axis_index("occ")
-    total = terms[0][...]
-    for t in terms[1:]:
-        total = total + t[...]
-    all_ref[...] = 0.5 * total
     for k, src in enumerate(blocks):
         offset = (owner ^ k) * owner_cols
         for j in range(owner_cols):
-            all_ref[pl.ds(offset + j, 1), :] += src[j : j + 1, :]
+            out_ref[pl.ds(offset + j, 1), :] = src[j : j + 1, :]
+
+
+def line_kernel(*refs):
+    half = len(refs) // 2 + 1
+    cycle_ref, terms, outs = refs[0], refs[1:half], refs[half:]
     z = lax.axis_index("sec") // 2
     for q, out in enumerate(outs):
-        out[...] = all_ref[:, block_of(z ^ q)]
+        cols = block_of(z ^ q)
+        total = terms[0][:, cols]
+        for t in terms[1:]:
+            total = total + t[:, cols]
+        out[...] = 0.5 * total + cycle_ref[:, cols]
 
 
 def final_kernel(*refs):
@@ -286,46 +330,57 @@
     live_count = lax.dynamic_slice_in_dim(live_pairs, owner_index, 1)[0]
 
     def exchange(values):
-        return [
-            lax.ppermute(value, "occ", [(o, o ^ k) for o in range(owners)])
-            for k, value in enumerate(values, start=1)
-        ]
+        moved = {}
+        for k in reversed(range(1, owners)):
+            moved[k] = lax.ppermute(values[k - 1], "occ", [(o, o ^ k) for o in range(owners)])
+        return [moved[k] for k in range(1, owners)]
 
     def swap_pair(value):
         return lax.ppermute(value, "sec", [(s, s ^ 1) for s in range(sections)])
 
     starts = [d_share * c // CHUNK_UNITS for c in CHUNKS]
-    chunks = list(zip(starts, [*starts[1:], d_share]))
-    window = cycle_window(live_pairs, flipped, A_WINDOW)
-    windows = [window] + exchange([window] * (owners - 1))
+    chunks = [(d0, d1 - d0) for d0, d1 in zip(starts, [*starts[1:], d_share])]
     arrived = []
-    turn = window
-    for d0, d1 in chunks:
-        pieces = slice_chunk(after(ids, turn), flipped, owners, d0, d1 - d0)
+    turn = ids
+    for c, (d0, dn) in enumerate(chunks):
+        if c < len(chunks) - 1:
+            pieces = slice_chunk(after(ids, turn), flipped, owners, d0, dn)
+        else:
+            closing_own, *pieces = slice_chunk(after(ids, turn), flipped, owners, d0, dn, 0)
         arrived.append(exchange(pieces))
         turn = pieces[0]
-
-    send, keep = cycle_product(windows, cycle_ints)
+        if c == 0:
+            window = cycle_window(after(ids, turn), live_pairs, flipped, A_WINDOW)
+            windows = exchange([window] * (owners - 1))
+            turn = window
+
+    send, keep = cycle_product(window, windows, cycle_ints)
     recv = swap_pair(send)
     own, *sends = add_blocks(keep, recv, owners)
     blocks = [own, *exchange(sends)]
+    cycle = small(functools.partial(place_kernel, owner_cols), sds(owner_rows, own.shape[1]), blocks)
 
     acc = None
     turn = own
-    for (d0, d1), values in zip(chunks, arrived):
-        acc = ladder_product(after(ids, turn), flipped, values, ladder_ints, acc, d0, d1 == d_share)
+    for c, ((d0, dn), values) in enumerate(zip(chunks[:-1], arrived)):
+        acc = ladder_product(after(ids, turn), flipped, values, ladder_ints, acc, d0, dn)
         turn = ids
-    send, keep = acc
+        if c == 0:
+            parts = fetch_integrals(after(ids, acc), ladder_ints, chunks[-1][0])
+            turn = parts[0]
+    send, keep = small(
+        functools.partial(closing_kernel, owners),
+        [sds(acc.shape[0], acc.shape[1] // 2)] * 2,
+        [closing_own, *arrived[-1], *parts, acc],
+        [pltpu.VMEM(acc.shape, f32)],
+    )
     own, *sends = add_blocks(keep, swap_pair(send), owners)
-    terms = [*blocks, own, *exchange(sends)]
+    terms = [cycle, own, *exchange(sends)]
     lines = sections // 2
-    pieces = small(
-        functools.partial(line_kernel, owners, owner_cols),
-        [sds(owner_rows, LANES)] * lines,
-        terms,
-        [pltpu.VMEM((owner_rows, lines * LANES), f32)],
-    )
-    recvs = [lax.ppermute(pieces[q], "sec", [(s, s ^ (2 * q)) for s in range(sections)]) for q in range(1, lines)]
+    pieces = small(line_kernel, [sds(owner_rows, LANES)] * lines, terms)
+    recvs = [
+        lax.ppermute(pieces[q], "sec", [(s, s ^ (2 * q)) for s in range(sections)]) for q in reversed(range(1, lines))
+    ]
 
     occ_rows = lax.dynamic_slice_in_dim(occ_energy, owner_index * I_OWNER, I_OWNER)
     pair_energy = (occ_rows[:, None] + occ_energy[None, :]).reshape(owner_rows, 1)
@@ -410,6 +465,8 @@
         and A_WINDOW * B_WINDOW == sections * LANES
         and B_WINDOW == LANES
         and OCCUPIED // owners <= CYCLE_PAD
+        and A_WINDOW == D_STEP
+        and LANES % (VIRTUAL // sections) == 0
         and sections // 2 == owners
         and VIRTUAL // sections % (D_STEP * CHUNK_UNITS) == 0
     )

time: 137 us -> 136 us (level)
  waiting for transfers between devices: 34.9 us -> 43.1 us
  local copies, waits for them, and re-layouts: 11.1 us -> 5.7 us
  Pallas kernels: 52.8 us -> 51.1 us
  starting transfers between devices: 35.5 us -> 34.1 us
    ppermute x21, waiting for transfers between devices: 30.1 us -> 39.8 us  [exchange(): lax.ppermute(values[k - 1], 'occ', [(o, o ^ k) for o in range(owners)])]
    unnamed x48 -> x26, local copies, waits for them, and re-layouts: 9.71 us -> 4.29 us
    pallas_call x9, Pallas kernels: 41.8 us -> 39.1 us  [the longest x3 26.9 us: ladder_product(): pl.pallas_call(functools.partial(ladder_kernel, n, first), out_shape=sds(...]
    ppermute x3, waiting for transfers between devices: 4.83 us -> 3.28 us  [streamed_parts(): lax.ppermute(pieces[q], 'sec', [(s, s ^ 2 * q) for s in range(sections)])]
    ppermute x21, starting transfers between devices: 31 us -> 29.5 us  [exchange(): lax.ppermute(values[k - 1], 'occ', [(o, o ^ k) for o in range(owners)])]
  transfers between devices with their start and end apart: 26 -> 26, of which waited for: 7 -> 9; matrix products, arithmetic and copies ran while one was open for 2% -> 2% of each run, Pallas kernels for 31% -> 31%
where the time goes in v2:
time: 136 us
  Pallas kernels  51.1 us (38%)
  waiting for transfers between devices  43.1 us (32%)
  starting transfers between devices  34.1 us (25%)
  local copies, waits for them, and re-layouts  5.7 us (4%)
  other arithmetic  1.48 us (1%)
    ppermute x21, waiting for transfers between devices, exchange(): lax.ppermute(values[k - 1], 'occ', [(o, o ^ k) for o in range(owners)])  39.8 us
    ppermute x21, starting transfers between devices, exchange(): lax.ppermute(values[k - 1], 'occ', [(o, o ^ k) for o in range(owners)])  29.5 us
    pallas_call x3, Pallas kernels, ladder_product(): pl.pallas_call(functools.partial(ladder_kernel, n, first), out_shape=sds(...  26.9 us
    pallas_call x1, Pallas kernels, cycle_product(): pl.pallas_call(functools.partial(cycle_kernel, owners, steps), out_shape=...  9.47 us
    pallas_call x4, Pallas kernels, slice_chunk(): pl.pallas_call(functools.partial(slice_kernel, d0, first), out_shape=[sds...  7.57 us
    ppermute x3, starting transfers between devices, streamed_parts(): lax.ppermute(pieces[q], 'sec', [(s, s ^ 2 * q) for s in range(sections)])  4.45 us
    unnamed x26, local copies, waits for them, and re-layouts  4.29 us
    ppermute x3, waiting for transfers between devices, streamed_parts(): lax.ppermute(pieces[q], 'sec', [(s, s ^ 2 * q) for s in range(sections)])  3.28 us
  transfers between devices with their start and end apart: 26, of which 9 were waited for; matrix products, arithmetic and copies ran while one was open for 2% of the time, Pallas kernels for 31%

profile of v2, /device:TPU:0, one launch (start us, length us, event | category | flops | bytes accessed | tf_op | source)
XLA Modules:
  0.0 135.8 jit_solution(14357458151039572531)
XLA Ops:
  0.0 1.9 %slices.4 = (f32[48,8,128]{2,1,0:T(8,128)S(1)}, f32[48,8,128]{2,1,0:T(8,128)}, f32[48,8,128]{2,1,0:T(8,128)}) custom-call(s32[1]{0:T(128)} %bitcast.turn_ref.ids, f32[48,64,512]{2,1,0:T(8,128)} %bitcast.6), custom_call_target="tpu_custom_call" | custom-call | bytes 1179648 | tf_op jit(solution)/shard_map/slices/pallas_call | solution.py:89
  1.9 2.1 %cycle_window.1.refs_0_ = f32[24,8,128]{2,1,0:T(8,128)S(1)} custom-call(s32[1]{0:T(128)} %bitcast.turn_ref.ids, s32[4]{0:T(128)S(1)} %copy-done.1, f32[48,64,512]{2,1,0:T(8,128)} %bitcast.7), custom_call_target="tpu_custom_call" | custom-call | bytes 1572864 | tf_op jit(solution)/shard_map/cycle_window/pallas_call | solution.py:124
  4.1 3.1 %slices.5 = (f32[48,32,128]{2,1,0:T(8,128)}, f32[48,32,128]{2,1,0:T(8,128)}, f32[48,32,128]{2,1,0:T(8,128)}) custom-call(s32[1]{0:T(128)} %bitcast.turn_ref.ids, f32[48,64,512]{2,1,0:T(8,128)} %bitcast.8), custom_call_target="tpu_custom_call" | custom-call | bytes 4718592 | tf_op jit(solution)/shard_map/slices/pallas_call | solution.py:89
  7.2 3.0 %collective-permute-start.16 = (f32[48,32,128]{2,1,0:T(8,128)}, f32[48,32,128]{2,1,0:T(8,128)S(1)}, u32[]{:S(2)}, u32[]{:S(2)}) collective-permute-start(f32[48,32,128]{2,1,0:T(8,128)} %get-tuple-element.54), channel_id=1, source_target_pairs={{0,8},{8,0},{16,24},{24,16},{1,9},{9,1},{17,25},{25,17},{2,10},{10... | collective-permute-start | bytes 2359304 | tf_op jit(solution)/shard_map/ppermute | solution.py:335
  10.2 1.5 %collective-permute-start.17 = (f32[48,32,128]{2,1,0:T(8,128)}, f32[48,32,128]{2,1,0:T(8,128)S(1)}, u32[]{:S(2)}, u32[]{:S(2)}) collective-permute-start(f32[48,32,128]{2,1,0:T(8,128)} %get-tuple-element.71), channel_id=1, source_target_pairs={{0,16},{8,24},{16,0},{24,8},{1,17},{9,25},{17,1},{25,9},{2,18},{10... | collective-permute-start | bytes 2359304 | tf_op jit(solution)/shard_map/ppermute | solution.py:335
  11.7 1.9 %collective-permute-start = (f32[24,8,128]{2,1,0:T(8,128)S(1)}, f32[24,8,128]{2,1,0:T(8,128)S(1)}, u32[]{:S(2)}, u32[]{:S(2)}) collective-permute-start(f32[24,8,128]{2,1,0:T(8,128)S(1)} %cycle_window.1.refs_0_), channel_id=1, source_target_pairs={{0,8},{8,0},{16,24},{24,16},{1,9},{9,1},{17,25},{25,17},{2,10},{10... | collective-permute-start | bytes 294920 | tf_op jit(solution)/shard_map/ppermute | solution.py:335
  13.7 1.5 %collective-permute-start.1 = (f32[24,8,128]{2,1,0:T(8,128)S(1)}, f32[24,8,128]{2,1,0:T(8,128)S(1)}, u32[]{:S(2)}, u32[]{:S(2)}) collective-permute-start(f32[24,8,128]{2,1,0:T(8,128)S(1)} %cycle_window.1.refs_0_), channel_id=1, source_target_pairs={{0,16},{8,24},{16,0},{24,8},{1,17},{9,25},{17,1},{25,9},{2,18},{10... | collective-permute-start | bytes 294920 | tf_op jit(solution)/shard_map/ppermute | solution.py:335
  15.2 31.7 %collective-permute-done.refs_1_ = f32[24,8,128]{2,1,0:T(8,128)S(1)} collective-permute-done((f32[24,8,128]{2,1,0:T(8,128)S(1)}, f32[24,8,128]{2,1,0:T(8,128)S(1)}, u32[]{:S(2)}, u32[]{:S(2)}) %collective-permute-start) | collective-permute-done | bytes 98336 | tf_op jit(solution)/shard_map/ppermute | solution.py:335
  47.0 2.7 %collective-permute-start.2 = (f32[24,8,128]{2,1,0:T(8,128)S(1)}, f32[24,8,128]{2,1,0:T(8,128)S(1)}, u32[]{:S(2)}, u32[]{:S(2)}) collective-permute-start(f32[24,8,128]{2,1,0:T(8,128)S(1)} %cycle_window.1.refs_0_), channel_id=1, source_target_pairs={{0,24},{8,16},{16,8},{24,0},{1,25},{9,17},{17,9},{25,1},{2,26},{10... | collective-permute-start | bytes 294920 | tf_op jit(solution)/shard_map/ppermute | solution.py:335
  50.2 3.3 %collective-permute-done.2.refs_3_ = f32[24,8,128]{2,1,0:T(8,128)S(1)} collective-permute-done((f32[24,8,128]{2,1,0:T(8,128)S(1)}, f32[24,8,128]{2,1,0:T(8,128)S(1)}, u32[]{:S(2)}, u32[]{:S(2)}) %collective-permute-start.2) | collective-permute-done | bytes 98336 | tf_op jit(solution)/shard_map/ppermute | solution.py:335
  53.5 9.5 %cycle_product.1 = (f32[64,512]{1,0:T(8,128)S(1)}, f32[64,512]{1,0:T(8,128)S(1)}) custom-call(f32[24,8,128]{2,1,0:T(8,128)S(1)} %cycle_window.1.refs_0_, f32[24,8,128]{2,1,0:T(8,128)S(1)} %collective-permute-done.refs_1_, f32[24,8,128]{2,1,0:T(8,128)S(1)} %collective-permute-done.1.refs_2_, f32[24,8,128]{2,1,0:T(8,128)S(1)} %collective-permute-done.2.refs_3_, ...), custom_call_target="tpu_custom_call" | custom-call | flops 905969664 | bytes 18874368 | tf_op jit(solution)/shard_map/cycle_product/pallas_call | solution.py:259
  63.1 1.8 %collective-permute-start.11 = (f32[48,8,128]{2,1,0:T(8,128)}, f32[48,8,128]{2,1,0:T(8,128)S(1)}, u32[]{:S(2)}, u32[]{:S(2)}) collective-permute-start(f32[48,8,128]{2,1,0:T(8,128)} %get-tuple-element.63), channel_id=1, source_target_pairs={{0,16},{8,24},{16,0},{24,8},{1,17},{9,25},{17,1},{25,9},{2,18},{10... | collective-permute-start | bytes 589832 | tf_op jit(solution)/shard_map/ppermute | solution.py:335
  64.9 2.2 %collective-permute-start.12 = (f32[48,8,128]{2,1,0:T(8,128)}, f32[48,8,128]{2,1,0:T(8,128)S(1)}, u32[]{:S(2)}, u32[]{:S(2)}) collective-permute-start(f32[48,8,128]{2,1,0:T(8,128)} %get-tuple-element.64), channel_id=1, source_target_pairs={{0,24},{8,16},{16,8},{24,0},{1,25},{9,17},{17,9},{25,1},{2,26},{10... | collective-permute-start | bytes 589832 | tf_op jit(solution)/shard_map/ppermute | solution.py:335
  67.1 1.3 slices.6
  70.6 1.3 slices.7
  74.8 1.7 %collective-permute-start.13 = (f32[48,16,128]{2,1,0:T(8,128)}, f32[48,16,128]{2,1,0:T(8,128)S(1)}, u32[]{:S(2)}, u32[]{:S(2)}) collective-permute-start(f32[48,16,128]{2,1,0:T(8,128)} %copy-done.5), channel_id=1, source_target_pairs={{0,8},{8,0},{16,24},{24,16},{1,9},{9,1},{17,25},{25,17},{2,10},{10... | collective-permute-start | bytes 1179656 | tf_op jit(solution)/shard_map/ppermute | solution.py:335
  76.6 1.5 %collective-permute-start.14 = (f32[48,16,128]{2,1,0:T(8,128)}, f32[48,16,128]{2,1,0:T(8,128)S(1)}, u32[]{:S(2)}, u32[]{:S(2)}) collective-permute-start(f32[48,16,128]{2,1,0:T(8,128)} %copy-done.4), channel_id=1, source_target_pairs={{0,16},{8,24},{16,0},{24,8},{1,17},{9,25},{17,1},{25,9},{2,18},{10... | collective-permute-start | bytes 1179656 | tf_op jit(solution)/shard_map/ppermute | solution.py:335
  78.1 5.0 %ladder_product.3.refs_5_ = f32[192,1024]{1,0:T(8,128)S(1)} custom-call(s32[1]{0:T(128)} %bitcast.turn_ref.ids, f32[48,64,512]{2,1,0:T(8,128)} %bitcast.11, f32[48,8,128]{2,1,0:T(8,128)S(1)} %collective-permute-done.10.refs_1_, f32[48,8,128]{2,1,0:T(8,128)S(1)} %collective-permute-done.11.refs_2_, f32[48,8,128]{2,1,0:T(8,128)S(1)} %collective-permute-done.12.refs_3_, ...), custom_call_target="tpu_custom_call" | custom-call | flops 1207959552 | bytes 4194304 | tf_op jit(solution)/shard_map/ladder_product/pallas_call | solution.py:167
  83.2 2.5 %fetch_integrals.1 = (bf16[8,128,1024]{2,1,0:T(8,128)(2,1)S(1)}, bf16[8,128,1024]{2,1,0:T(8,128)(2,1)S(1)}) custom-call(s32[1]{0:T(128)} %bitcast.turn_ref.ids, f32[128,64,1024]{2,1,0:T(8,128)} %refs_4_.8), custom_call_target="tpu_custom_call" | custom-call | bytes 8388608 | tf_op jit(solution)/shard_map/fetch_integrals/pallas_call | solution.py:203
  86.1 1.7 %collective-permute-start.7 = (f32[48,8,128]{2,1,0:T(8,128)S(1)}, f32[48,8,128]{2,1,0:T(8,128)S(1)}, u32[]{:S(2)}, u32[]{:S(2)}) collective-permute-start(f32[48,8,128]{2,1,0:T(8,128)S(1)} %copy-done.11), channel_id=1, source_target_pairs={{0,8},{8,0},{16,24},{24,16},{1,9},{9,1},{17,25},{25,17},{2,10},{10... | collective-permute-start | bytes 589832 | tf_op jit(solution)/shard_map/ppermute | solution.py:335
  87.8 1.6 %collective-permute-start.8 = (f32[48,8,128]{2,1,0:T(8,128)S(1)}, f32[48,8,128]{2,1,0:T(8,128)S(1)}, u32[]{:S(2)}, u32[]{:S(2)}) collective-permute-start(f32[48,8,128]{2,1,0:T(8,128)S(1)} %copy-done.9), channel_id=1, source_target_pairs={{0,16},{8,24},{16,0},{24,8},{1,17},{9,25},{17,1},{25,9},{2,18},{10... | collective-permute-start | bytes 589832 | tf_op jit(solution)/shard_map/ppermute | solution.py:335
  89.4 13.7 %ladder_product.4.refs_5_ = f32[192,1024]{1,0:T(8,128)S(1)} custom-call(s32[1]{0:T(128)} %bitcast.turn_ref.ids, f32[48,64,512]{2,1,0:T(8,128)} %bitcast.12, f32[48,32,128]{2,1,0:T(8,128)S(1)} %collective-permute-done.16.refs_1_, f32[48,32,128]{2,1,0:T(8,128)S(1)} %collective-permute-done.17.refs_2_, f32[48,32,128]{2,1,0:T(8,128)S(1)} %collective-permute-done.18.refs_3_, ...), custom_call_target="tpu_custom_call" | custom-call | flops 4831838208 | bytes 16777216 | tf_op jit(solution)/shard_map/ladder_product/pallas_call | solution.py:167
  103.5 8.1 %ladder_product.5.refs_6_ = f32[192,1024]{1,0:T(8,128)S(1)} custom-call(s32[1]{0:T(128)} %bitcast.turn_ref.ids, f32[48,64,512]{2,1,0:T(8,128)} %bitcast.13, f32[48,16,128]{2,1,0:T(8,128)S(1)} %collective-permute-done.13.refs_1_, f32[48,16,128]{2,1,0:T(8,128)S(1)} %collective-permute-done.14.refs_2_, f32[48,16,128]{2,1,0:T(8,128)S(1)} %collective-permute-done.15.refs_3_, ...), custom_call_target="tpu_custom_call" | custom-call | flops 2415919104 | bytes 8388608 | tf_op jit(solution)/shard_map/ladder_product/pallas_call | solution.py:167
  111.6 1.7 %shard_map.75 = (f32[192,512]{1,0:T(8,128)S(1)}, f32[192,512]{1,0:T(8,128)S(1)}) custom-call(f32[48,8,128]{2,1,0:T(8,128)S(1)} %get-tuple-element.58.refs_0_, f32[48,8,128]{2,1,0:T(8,128)S(1)} %collective-permute-done.7.refs_1_, f32[48,8,128]{2,1,0:T(8,128)S(1)} %collective-permute-done.8.refs_2_, f32[48,8,128]{2,1,0:T(8,128)S(1)} %collective-permute-done.9.refs_3_, ...), custom_call_target="tpu_custom_call" | custom-call | bytes 10747904 | tf_op jit(solution)/shard_map/pallas_call | solution.py:54
  113.5 1.7 %collective-permute-start.4 = (f32[16,512]{1,0:T(8,128)S(1)}, f32[16,512]{1,0:T(8,128)S(1)}, u32[]{:S(2)}, u32[]{:S(2)}) collective-permute-start(f32[16,512]{1,0:T(8,128)S(1)} %get-tuple-element.50), channel_id=1, source_target_pairs={{0,8},{8,0},{16,24},{24,16},{1,9},{9,1},{17,25},{25,17},{2,10},{10... | collective-permute-start | bytes 98312 | tf_op jit(solution)/shard_map/ppermute | solution.py:335
  116.0 1.5 %collective-permute-start.5 = (f32[16,512]{1,0:T(8,128)S(1)}, f32[16,512]{1,0:T(8,128)S(1)}, u32[]{:S(2)}, u32[]{:S(2)}) collective-permute-start(f32[16,512]{1,0:T(8,128)S(1)} %get-tuple-element.51), channel_id=1, source_target_pairs={{0,16},{8,24},{16,0},{24,8},{1,17},{9,25},{17,1},{25,9},{2,18},{10... | collective-permute-start | bytes 98312 | tf_op jit(solution)/shard_map/ppermute | solution.py:335
  117.8 1.8 %collective-permute-start.20 = (f32[48,512]{1,0:T(8,128)S(1)}, f32[48,512]{1,0:T(8,128)S(1)}, u32[]{:S(2)}, u32[]{:S(2)}) collective-permute-start(f32[48,512]{1,0:T(8,128)S(1)} %get-tuple-element.76), channel_id=1, source_target_pairs={{0,8},{8,0},{16,24},{24,16},{1,9},{9,1},{17,25},{25,17},{2,10},{10... | collective-permute-start | bytes 294920 | tf_op jit(solution)/shard_map/ppermute | solution.py:335
  119.6 1.5 %collective-permute-start.21 = (f32[48,512]{1,0:T(8,128)S(1)}, f32[48,512]{1,0:T(8,128)S(1)}, u32[]{:S(2)}, u32[]{:S(2)}) collective-permute-start(f32[48,512]{1,0:T(8,128)S(1)} %get-tuple-element.77), channel_id=1, source_target_pairs={{0,16},{8,24},{16,0},{24,8},{1,17},{9,25},{17,1},{25,9},{2,18},{10... | collective-permute-start | bytes 294920 | tf_op jit(solution)/shard_map/ppermute | solution.py:335
  122.8 2.5 %collective-permute-done.21.refs_3_ = f32[48,512]{1,0:T(8,128)S(1)} collective-permute-done((f32[48,512]{1,0:T(8,128)S(1)}, f32[48,512]{1,0:T(8,128)S(1)}, u32[]{:S(2)}, u32[]{:S(2)}) %collective-permute-start.21) | collective-permute-done | bytes 98336 | tf_op jit(solution)/shard_map/ppermute | solution.py:335
  125.2 1.4 collective-permute-done.22.refs_4_
  126.7 3.7 %collective-permute-start.23 = (f32[48,128]{1,0:T(8,128)S(1)}, f32[48,128]{1,0:T(8,128)S(1)}, u32[]{:S(2)}, u32[]{:S(2)}) collective-permute-start(f32[48,128]{1,0:T(8,128)S(1)} %get-tuple-element.80), channel_id=1, source_target_pairs={{0,6},{1,7},{2,4},{3,5},{4,2},{5,3},{6,0},{7,1},{8,14},{9,15},{10,... | collective-permute-start | bytes 73736 | tf_op jit(solution)/shard_map/ppermute | solution.py:382
  132.3 2.7 %collective-permute-done.24.refs_2_ = f32[48,128]{1,0:T(8,128)S(1)} collective-permute-done((f32[48,128]{1,0:T(8,128)S(1)}, f32[48,128]{1,0:T(8,128)S(1)}, u32[]{:S(2)}, u32[]{:S(2)}) %collective-permute-start.24) | collective-permute-done | bytes 24608 | tf_op jit(solution)/shard_map/ppermute | solution.py:382
  (74 shorter events, 12.2 us)
Async XLA Ops:
  7.2 78.5 %collective-permute-start.16 = (f32[48,32,128]{2,1,0:T(8,128)}, f32[48,32,128]{2,1,0:T(8,128)S(1)}, u32[]{:S(2)}, u32[]{:S(2)}) collective-permute-start(f32[48,32,128]{2,1,0:T(8,128)} %get-tuple-element.54), channel_id=1, source_target_pairs={{0,8},{8,0},{16,24},{24,16},{1,9},{9,1},{17,25},{25,17},{2,10},{10... | collective-permute-start | bytes 2359304 | tf_op jit(solution)/shard_map/ppermute | solution.py:335
  10.2 75.9 %collective-permute-start.17 = (f32[48,32,128]{2,1,0:T(8,128)}, f32[48,32,128]{2,1,0:T(8,128)S(1)}, u32[]{:S(2)}, u32[]{:S(2)}) collective-permute-start(f32[48,32,128]{2,1,0:T(8,128)} %get-tuple-element.71), channel_id=1, source_target_pairs={{0,16},{8,24},{16,0},{24,8},{1,17},{9,25},{17,1},{25,9},{2,18},{10... | collective-permute-start | bytes 2359304 | tf_op jit(solution)/shard_map/ppermute | solution.py:335
  11.7 76.1 %collective-permute-start.18 = (f32[48,32,128]{2,1,0:T(8,128)}, f32[48,32,128]{2,1,0:T(8,128)S(1)}, u32[]{:S(2)}, u32[]{:S(2)}) collective-permute-start(f32[48,32,128]{2,1,0:T(8,128)} %get-tuple-element.72), channel_id=1, source_target_pairs={{0,24},{8,16},{16,8},{24,0},{1,25},{9,17},{17,9},{25,1},{2,26},{10... | collective-permute-start | bytes 2359304 | tf_op jit(solution)/shard_map/ppermute | solution.py:335
  11.7 35.2 %collective-permute-start = (f32[24,8,128]{2,1,0:T(8,128)S(1)}, f32[24,8,128]{2,1,0:T(8,128)S(1)}, u32[]{:S(2)}, u32[]{:S(2)}) collective-permute-start(f32[24,8,128]{2,1,0:T(8,128)S(1)} %cycle_window.1.refs_0_), channel_id=1, source_target_pairs={{0,8},{8,0},{16,24},{24,16},{1,9},{9,1},{17,25},{25,17},{2,10},{10... | collective-permute-start | bytes 294920 | tf_op jit(solution)/shard_map/ppermute | solution.py:335
  13.7 36.0 %collective-permute-start.1 = (f32[24,8,128]{2,1,0:T(8,128)S(1)}, f32[24,8,128]{2,1,0:T(8,128)S(1)}, u32[]{:S(2)}, u32[]{:S(2)}) collective-permute-start(f32[24,8,128]{2,1,0:T(8,128)S(1)} %cycle_window.1.refs_0_), channel_id=1, source_target_pairs={{0,16},{8,24},{16,0},{24,8},{1,17},{9,25},{17,1},{25,9},{2,18},{10... | collective-permute-start | bytes 294920 | tf_op jit(solution)/shard_map/ppermute | solution.py:335
  47.0 6.6 %collective-permute-start.2 = (f32[24,8,128]{2,1,0:T(8,128)S(1)}, f32[24,8,128]{2,1,0:T(8,128)S(1)}, u32[]{:S(2)}, u32[]{:S(2)}) collective-permute-start(f32[24,8,128]{2,1,0:T(8,128)S(1)} %cycle_window.1.refs_0_), channel_id=1, source_target_pairs={{0,24},{8,16},{16,8},{24,0},{1,25},{9,17},{17,9},{25,1},{2,26},{10... | collective-permute-start | bytes 294920 | tf_op jit(solution)/shard_map/ppermute | solution.py:335
  49.7 13.4 %collective-permute-start.10 = (f32[48,8,128]{2,1,0:T(8,128)S(1)}, f32[48,8,128]{2,1,0:T(8,128)S(1)}, u32[]{:S(2)}, u32[]{:S(2)}) collective-permute-start(f32[48,8,128]{2,1,0:T(8,128)S(1)} %get-tuple-element.45), channel_id=1, source_target_pairs={{0,8},{8,0},{16,24},{24,16},{1,9},{9,1},{17,25},{25,17},{2,10},{10... | collective-permute-start | bytes 589832 | tf_op jit(solution)/shard_map/ppermute | solution.py:335
  63.0 1.9 %collective-permute-start.3 = (f32[64,512]{1,0:T(8,128)S(1)}, f32[64,512]{1,0:T(8,128)S(1)}, u32[]{:S(2)}, u32[]{:S(2)}) collective-permute-start(f32[64,512]{1,0:T(8,128)S(1)} %get-tuple-element.48), channel_id=1, source_target_pairs={{0,1},{1,0},{2,3},{3,2},{4,5},{5,4},{6,7},{7,6},{8,9},{9,8},{10,11... | collective-permute-start | bytes 393224 | tf_op jit(solution)/shard_map/ppermute | solution.py:339
  63.1 11.7 %collective-permute-start.11 = (f32[48,8,128]{2,1,0:T(8,128)}, f32[48,8,128]{2,1,0:T(8,128)S(1)}, u32[]{:S(2)}, u32[]{:S(2)}) collective-permute-start(f32[48,8,128]{2,1,0:T(8,128)} %get-tuple-element.63), channel_id=1, source_target_pairs={{0,16},{8,24},{16,0},{24,8},{1,17},{9,25},{17,1},{25,9},{2,18},{10... | collective-permute-start | bytes 589832 | tf_op jit(solution)/shard_map/ppermute | solution.py:335
  64.9 11.6 %collective-permute-start.12 = (f32[48,8,128]{2,1,0:T(8,128)}, f32[48,8,128]{2,1,0:T(8,128)S(1)}, u32[]{:S(2)}, u32[]{:S(2)}) collective-permute-start(f32[48,8,128]{2,1,0:T(8,128)} %get-tuple-element.64), channel_id=1, source_target_pairs={{0,24},{8,16},{16,8},{24,0},{1,25},{9,17},{17,9},{25,1},{2,26},{10... | collective-permute-start | bytes 589832 | tf_op jit(solution)/shard_map/ppermute | solution.py:335
  67.1 6.9 %copy-start.12 = (f32[48]{0:T(128)S(1)}, f32[48]{0:T(128)}, u32[]{:S(2)}) copy-start(f32[48]{0:T(128)} %param.12) | copy-start | bytes 580
  74.8 28.2 %collective-permute-start.13 = (f32[48,16,128]{2,1,0:T(8,128)}, f32[48,16,128]{2,1,0:T(8,128)S(1)}, u32[]{:S(2)}, u32[]{:S(2)}) collective-permute-start(f32[48,16,128]{2,1,0:T(8,128)} %copy-done.5), channel_id=1, source_target_pairs={{0,8},{8,0},{16,24},{24,16},{1,9},{9,1},{17,25},{25,17},{2,10},{10... | collective-permute-start | bytes 1179656 | tf_op jit(solution)/shard_map/ppermute | solution.py:335
  76.6 26.9 %collective-permute-start.14 = (f32[48,16,128]{2,1,0:T(8,128)}, f32[48,16,128]{2,1,0:T(8,128)S(1)}, u32[]{:S(2)}, u32[]{:S(2)}) collective-permute-start(f32[48,16,128]{2,1,0:T(8,128)} %copy-done.4), channel_id=1, source_target_pairs={{0,16},{8,24},{16,0},{24,8},{1,17},{9,25},{17,1},{25,9},{2,18},{10... | collective-permute-start | bytes 1179656 | tf_op jit(solution)/shard_map/ppermute | solution.py:335
  83.2 4.6 %copy-start.9 = (f32[48,8,128]{2,1,0:T(8,128)S(1)}, f32[48,8,128]{2,1,0:T(8,128)}, u32[]{:S(2)}) copy-start(f32[48,8,128]{2,1,0:T(8,128)} %copy-done.8) | copy-start | bytes 589828
  85.7 17.7 %collective-permute-start.15 = (f32[48,16,128]{2,1,0:T(8,128)S(1)}, f32[48,16,128]{2,1,0:T(8,128)S(1)}, u32[]{:S(2)}, u32[]{:S(2)}) collective-permute-start(f32[48,16,128]{2,1,0:T(8,128)S(1)} %copy-done.3), channel_id=1, source_target_pairs={{0,24},{8,16},{16,8},{24,0},{1,25},{9,17},{17,9},{25,1},{2,26},{10... | collective-permute-start | bytes 1179656 | tf_op jit(solution)/shard_map/ppermute | solution.py:335
  86.1 25.5 %collective-permute-start.7 = (f32[48,8,128]{2,1,0:T(8,128)S(1)}, f32[48,8,128]{2,1,0:T(8,128)S(1)}, u32[]{:S(2)}, u32[]{:S(2)}) collective-permute-start(f32[48,8,128]{2,1,0:T(8,128)S(1)} %copy-done.11), channel_id=1, source_target_pairs={{0,8},{8,0},{16,24},{24,16},{1,9},{9,1},{17,25},{25,17},{2,10},{10... | collective-permute-start | bytes 589832 | tf_op jit(solution)/shard_map/ppermute | solution.py:335
  87.8 15.3 %copy-start.7 = (f32[48,8,128]{2,1,0:T(8,128)S(1)}, f32[48,8,128]{2,1,0:T(8,128)}, u32[]{:S(2)}) copy-start(f32[48,8,128]{2,1,0:T(8,128)} %copy-done.6) | copy-start | bytes 589828
  87.8 23.8 %collective-permute-start.8 = (f32[48,8,128]{2,1,0:T(8,128)S(1)}, f32[48,8,128]{2,1,0:T(8,128)S(1)}, u32[]{:S(2)}, u32[]{:S(2)}) collective-permute-start(f32[48,8,128]{2,1,0:T(8,128)S(1)} %copy-done.9), channel_id=1, source_target_pairs={{0,16},{8,24},{16,0},{24,8},{1,17},{9,25},{17,1},{25,9},{2,18},{10... | collective-permute-start | bytes 589832 | tf_op jit(solution)/shard_map/ppermute | solution.py:335
  103.1 10.3 %slice-start = ((f32[512]{0:T(512)}), f32[8]{0:T(128)S(1)}, s32[]{:S(2)}) async-start(f32[512]{0:T(512)} %param.13), calls=%async_computation | async-start | bytes 1024 | tf_op jit(solution)/shard_map/slice | solution.py:387
  103.1 10.3 %slice-start.1 = ((f32[512]{0:T(512)}), f32[128]{0:T(128)S(1)}, s32[]{:S(2)}) async-start(f32[512]{0:T(512)} %param.13), calls=%async_computation.1 | async-start | bytes 1024 | tf_op jit(solution)/shard_map/slice | solution.py:387
  103.1 8.5 %collective-permute-start.9 = (f32[48,8,128]{2,1,0:T(8,128)S(1)}, f32[48,8,128]{2,1,0:T(8,128)S(1)}, u32[]{:S(2)}, u32[]{:S(2)}) collective-permute-start(f32[48,8,128]{2,1,0:T(8,128)S(1)} %copy-done.7), channel_id=1, source_target_pairs={{0,24},{8,16},{16,8},{24,0},{1,25},{9,17},{17,9},{25,1},{2,26},{10... | collective-permute-start | bytes 589832 | tf_op jit(solution)/shard_map/ppermute | solution.py:335
  111.6 23.5 %copy-start = (f32[48,128]{1,0:T(8,128)S(1)}, f32[48,128]{1,0:T(8,128)}, u32[]{:S(2)}) copy-start(f32[48,128]{1,0:T(8,128)} %refs_4_.9) | copy-start | bytes 73732
  113.3 4.5 %collective-permute-start.19 = (f32[192,512]{1,0:T(8,128)S(1)}, f32[192,512]{1,0:T(8,128)S(1)}, u32[]{:S(2)}, u32[]{:S(2)}) collective-permute-start(f32[192,512]{1,0:T(8,128)S(1)} %get-tuple-element.74), channel_id=1, source_target_pairs={{0,1},{1,0},{2,3},{3,2},{4,5},{5,4},{6,7},{7,6},{8,9},{9,8},{10,11... | collective-permute-start | bytes 1179656 | tf_op jit(solution)/shard_map/ppermute | solution.py:339
  113.5 7.6 %collective-permute-start.4 = (f32[16,512]{1,0:T(8,128)S(1)}, f32[16,512]{1,0:T(8,128)S(1)}, u32[]{:S(2)}, u32[]{:S(2)}) collective-permute-start(f32[16,512]{1,0:T(8,128)S(1)} %get-tuple-element.50), channel_id=1, source_target_pairs={{0,8},{8,0},{16,24},{24,16},{1,9},{9,1},{17,25},{25,17},{2,10},{10... | collective-permute-start | bytes 98312 | tf_op jit(solution)/shard_map/ppermute | solution.py:335
  116.0 6.1 %collective-permute-start.5 = (f32[16,512]{1,0:T(8,128)S(1)}, f32[16,512]{1,0:T(8,128)S(1)}, u32[]{:S(2)}, u32[]{:S(2)}) collective-permute-start(f32[16,512]{1,0:T(8,128)S(1)} %get-tuple-element.51), channel_id=1, source_target_pairs={{0,16},{8,24},{16,0},{24,8},{1,17},{9,25},{17,1},{25,9},{2,18},{10... | collective-permute-start | bytes 98312 | tf_op jit(solution)/shard_map/ppermute | solution.py:335
  117.5 5.2 %collective-permute-start.6 = (f32[16,512]{1,0:T(8,128)S(1)}, f32[16,512]{1,0:T(8,128)S(1)}, u32[]{:S(2)}, u32[]{:S(2)}) collective-permute-start(f32[16,512]{1,0:T(8,128)S(1)} %get-tuple-element.52), channel_id=1, source_target_pairs={{0,24},{8,16},{16,8},{24,0},{1,25},{9,17},{17,9},{25,1},{2,26},{10... | collective-permute-start | bytes 98312 | tf_op jit(solution)/shard_map/ppermute | solution.py:335
  117.8 5.0 %collective-permute-start.20 = (f32[48,512]{1,0:T(8,128)S(1)}, f32[48,512]{1,0:T(8,128)S(1)}, u32[]{:S(2)}, u32[]{:S(2)}) collective-permute-start(f32[48,512]{1,0:T(8,128)S(1)} %get-tuple-element.76), channel_id=1, source_target_pairs={{0,8},{8,0},{16,24},{24,16},{1,9},{9,1},{17,25},{25,17},{2,10},{10... | collective-permute-start | bytes 294920 | tf_op jit(solution)/shard_map/ppermute | solution.py:335
  119.6 5.7 %collective-permute-start.21 = (f32[48,512]{1,0:T(8,128)S(1)}, f32[48,512]{1,0:T(8,128)S(1)}, u32[]{:S(2)}, u32[]{:S(2)}) collective-permute-start(f32[48,512]{1,0:T(8,128)S(1)} %get-tuple-element.77), channel_id=1, source_target_pairs={{0,16},{8,24},{16,0},{24,8},{1,17},{9,25},{17,1},{25,9},{2,18},{10... | collective-permute-start | bytes 294920 | tf_op jit(solution)/shard_map/ppermute | solution.py:335
  121.1 5.5 %collective-permute-start.22 = (f32[48,512]{1,0:T(8,128)S(1)}, f32[48,512]{1,0:T(8,128)S(1)}, u32[]{:S(2)}, u32[]{:S(2)}) collective-permute-start(f32[48,512]{1,0:T(8,128)S(1)} %get-tuple-element.78), channel_id=1, source_target_pairs={{0,24},{8,16},{16,8},{24,0},{1,25},{9,17},{17,9},{25,1},{2,26},{10... | collective-permute-start | bytes 294920 | tf_op jit(solution)/shard_map/ppermute | solution.py:335
  126.7 5.7 %collective-permute-start.23 = (f32[48,128]{1,0:T(8,128)S(1)}, f32[48,128]{1,0:T(8,128)S(1)}, u32[]{:S(2)}, u32[]{:S(2)}) collective-permute-start(f32[48,128]{1,0:T(8,128)S(1)} %get-tuple-element.80), channel_id=1, source_target_pairs={{0,6},{1,7},{2,4},{3,5},{4,2},{5,3},{6,0},{7,1},{8,14},{9,15},{10,... | collective-permute-start | bytes 73736 | tf_op jit(solution)/shard_map/ppermute | solution.py:382
  130.3 4.7 %collective-permute-start.24 = (f32[48,128]{1,0:T(8,128)S(1)}, f32[48,128]{1,0:T(8,128)S(1)}, u32[]{:S(2)}, u32[]{:S(2)}) collective-permute-start(f32[48,128]{1,0:T(8,128)S(1)} %get-tuple-element.81), channel_id=1, source_target_pairs={{0,4},{1,5},{2,6},{3,7},{4,0},{5,1},{6,2},{7,3},{8,12},{9,13},{10,... | collective-permute-start | bytes 73736 | tf_op jit(solution)/shard_map/ppermute | solution.py:382
  130.3 4.7 %collective-permute-start.25 = (f32[48,128]{1,0:T(8,128)S(1)}, f32[48,128]{1,0:T(8,128)S(1)}, u32[]{:S(2)}, u32[]{:S(2)}) collective-permute-start(f32[48,128]{1,0:T(8,128)S(1)} %get-tuple-element.82), channel_id=1, source_target_pairs={{0,2},{1,3},{2,0},{3,1},{4,6},{5,7},{6,4},{7,5},{8,10},{9,11},{10,... | collective-permute-start | bytes 73736 | tf_op jit(solution)/shard_map/ppermute | solution.py:382
  (9 other events, 11.7 us)

commit v3 on v2

--- a/solution.py
+++ b/solution.py
@@ -70,12 +70,12 @@
     return pl.ds(pl.multiple_of(index * LANES, LANES), LANES)
 
 
-def slice_kernel(d0, first, turn_ref, a_ref, *refs):
+def slice_kernel(d0, turn_ref, a_ref, *refs):
     outs, sem = refs[:-1], refs[-1]
     owner = lax.axis_index("occ")
     copies = [
-        pltpu.make_async_copy(a_ref.at[:, pl.ds(d0, out.shape[1]), block_of(owner ^ k)], out, sem.at[k - first])
-        for k, out in enumerate(outs, start=first)
+        pltpu.make_async_copy(a_ref.at[:, pl.ds(d0, out.shape[1]), block_of(owner ^ k)], out, sem.at[k - 1])
+        for k, out in enumerate(outs, start=1)
     ]
     for copy in copies:
         copy.start()
@@ -83,11 +83,11 @@
         copy.wait()
 
 
-def slice_chunk(turn, flipped, owners, d0, dn, first=1):
+def slice_chunk(turn, flipped, owners, d0, dn):
     rows = flipped.shape[0]
-    n = owners - first
-    return pl.pallas_call(
-        functools.partial(slice_kernel, d0, first),
+    n = owners - 1
+    return pl.pallas_call(
+        functools.partial(slice_kernel, d0),
         out_shape=[sds(rows, dn, LANES)] * n,
         in_specs=[pl.BlockSpec(memory_space=pl.ANY)] * 2,
         out_specs=[pl.BlockSpec(memory_space=pltpu.VMEM)] * n,
@@ -133,21 +133,64 @@
     )(turn, counts, flipped)
 
 
-def two_steps(refs, d):
-    return jnp.concatenate([jnp.concatenate([r[:, d, :], r[:, d + 1, :]], axis=1) for r in refs], axis=0)
-
-
-def ladder_kernel(n, first, ids, *refs):
-    a_refs, w_ref, rest = refs[:n], refs[n], refs[n + 1 :]
-    acc_ref = rest[-1]
-
-    @pl.when(pl.program_id(0) == 0)
+def side_by_side(refs):
+    return jnp.concatenate([jnp.concatenate([r[:, d, :] for d in range(D_STEP)], axis=1) for r in refs], axis=0)
+
+
+def gather_copies(w_ref, buf_ref, sem, block, slot):
+    return [
+        pltpu.make_async_copy(w_ref.at[:, block * D_STEP + d, :], buf_ref.at[slot, d], sem.at[slot, d])
+        for d in range(D_STEP)
+    ]
+
+
+def ladder_kernel(block0, steps, own, last, n, turn, *refs):
+    own_refs, refs = refs[:own], refs[own:]
+    groups = [refs[g * n : (g + 1) * n] for g in range(len(steps))]
+    w_ref, rest = refs[len(steps) * n], refs[len(steps) * n + 1 :]
+    buf_ref, sem = rest[-2:]
+    acc_in, outs = rest[: 1 if own or last else 0], rest[1 if own or last else 0 : -2]
+    acc_ref = outs[-1]
+    own_rows = own_refs[0].shape[0] if own else 0
+    step, count = pl.program_id(0), pl.num_programs(0)
+    slot = lax.rem(step, 2)
+
+    @pl.when(step == 0)
     def _():
-        acc_ref[...] = jnp.zeros_like(acc_ref) if first else rest[0][...]
-
-    for d in range(0, D_STEP, 2):
-        w = jnp.concatenate([w_ref[:, d, :], w_ref[:, d + 1, :]], axis=0)
-        acc_ref[...] += dot_split(two_steps(a_refs, d), *split(w))
+        for copy in gather_copies(w_ref, buf_ref, sem, block0, 0):
+            copy.start()
+        if last:
+            acc_ref[...] = acc_in[0][...]
+        else:
+            acc_ref[own_rows:] = jnp.zeros((acc_ref.shape[0] - own_rows, acc_ref.shape[1]), f32)
+        if own:
+            acc_ref[:own_rows] = acc_in[0][...]
+
+    @pl.when(step + 1 < count)
+    def _():
+        for copy in gather_copies(w_ref, buf_ref, sem, block0 + step + 1, 1 - slot):
+            copy.start()
+
+    for copy in gather_copies(w_ref, buf_ref, sem, block0 + step, slot):
+        copy.wait()
+
+    a = side_by_side(groups[-1])
+    bound = sum(steps)
+    for g in reversed(range(len(steps) - 1)):
+        bound -= steps[g + 1]
+        a = jnp.where(step < bound, side_by_side(groups[g]), a)
+    if own:
+        a = jnp.concatenate([side_by_side(own_refs), a], axis=0)
+    w = buf_ref[slot].reshape(D_STEP * LANES, -1)
+    acc_ref[...] += dot_split(a, *split(w))
+
+    @pl.when(step == count - 1)
+    def _():
+        if last:
+            pair_halves(acc_ref, outs[0], outs[1])
+        if own:
+            pair_halves(acc_ref.at[pl.ds(0, own_rows)], outs[0], outs[1])
+            outs[2][...] = acc_ref[own_rows:]
 
 
 def pair_halves(src_ref, send_ref, keep_ref):
@@ -158,43 +201,74 @@
         keep_ref[:, cols] = src_ref[:, block_of(2 * z + core)]
 
 
-def ladder_product(ids, flipped, arrived, ladder_ints, acc, d0, dn):
-    n = len(arrived) + 1
-    rows = flipped.shape[0]
-    cols = ladder_ints.shape[2]
-    first = acc is None
-    total = pl.BlockSpec((n * rows, cols), lambda i, ids: (0, 0))
-    return pl.pallas_call(
-        functools.partial(ladder_kernel, n, first),
-        out_shape=sds(n * rows, cols),
+def ladder_product(turn, groups, ladder_ints, d0, own=None, acc=None, lanes=False):
+    n = len(groups[0])
+    rows = groups[0][0].shape[0]
+    depth, _, cols = ladder_ints.shape
+    with_own, last = own is not None, own is None and acc is not None
+    steps = [group[0].shape[1] // D_STEP for group in groups]
+    block0 = d0 // D_STEP
+    if lanes:
+        steps = [steps[0] - block0]
+    count = sum(steps)
+
+    def total(rows, cols):
+        return sds(rows, cols), pl.BlockSpec((rows, cols), lambda i, turn: (0, 0))
+
+    def rows_spec(g):
+        before = sum(steps[:g])
+        return pl.BlockSpec((rows, D_STEP, LANES), lambda i, turn: (0, jnp.clip(i - before, 0, steps[g] - 1), 0))
+
+    own_spec = pl.BlockSpec((rows, D_STEP, LANES), lambda i, turn: (0, block0 + i, turn[0]))
+    if with_own:
+        outs = [total(rows, cols // 2)] * 2 + [total(n * rows, cols)]
+    else:
+        outs = [total(n * rows, cols // 2)] * 2 if last else [total(n * rows, cols)]
+    all_rows = (n + with_own) * rows
+    return pl.pallas_call(
+        functools.partial(ladder_kernel, block0, steps, with_own, last, n),
+        out_shape=[shape for shape, _ in outs],
         grid_spec=pltpu.PrefetchScalarGridSpec(
             num_scalar_prefetch=1,
-            grid=(dn // D_STEP,),
-            in_specs=[pl.BlockSpec((rows, D_STEP, LANES), lambda i, ids: (0, d0 // D_STEP + i, ids[0]))]
-            + [pl.BlockSpec((rows, D_STEP, LANES), lambda i, ids: (0, i, 0))] * (n - 1)
-            + [pl.BlockSpec((LANES, D_STEP, cols), lambda i, ids: (0, d0 // D_STEP + i, 0))]
-            + ([] if first else [total]),
-            out_specs=total,
+            grid=(count,),
+            in_specs=[own_spec] * with_own
+            + [own_spec if lanes else rows_spec(g) for g in range(len(groups)) for _ in range(n)]
+            + [pl.BlockSpec(memory_space=pl.ANY)]
+            + ([] if acc is None else [total(*acc.shape)[1]]),
+            out_specs=[spec for _, spec in outs],
+            scratch_shapes=([pltpu.VMEM((all_rows, cols), f32)] if with_own or last else [])
+            + [pltpu.VMEM((2, D_STEP, depth, cols), f32), pltpu.SemaphoreType.DMA((2, D_STEP))],
         ),
         compiler_params=pltpu.CompilerParams(vmem_limit_bytes=VMEM_LIMIT),
         cost_estimate=pl.CostEstimate(
-            flops=6 * n * rows * dn * LANES * cols,
-            bytes_accessed=4 * dn * LANES * cols,
+            flops=6 * all_rows * count * D_STEP * depth * cols,
+            bytes_accessed=4 * count * D_STEP * depth * cols,
             transcendentals=0,
         ),
         name="ladder_product",
-    )(ids, flipped, *arrived, ladder_ints, *([] if first else [acc]))
-
-
-def fetch_kernel(d0, turn_ref, w_ref, hi_ref, lo_ref, raw_ref, sem):
+    )(
+        turn,
+        *([own] if with_own else []),
+        *[value for group in groups for value in group],
+        ladder_ints,
+        *([] if acc is None else [acc]),
+    )
+
+
+def fetch_kernel(d0, turn_ref, w_ref, *refs):
+    send_refs, keep_refs, (raw_ref, sem) = refs[:2], refs[2:4], refs[4:]
     copies = [
         pltpu.make_async_copy(w_ref.at[:, d0 + d, :], raw_ref.at[d], sem.at[d]) for d in range(raw_ref.shape[0])
     ]
     for copy in copies:
         copy.start()
+    core = lax.rem(lax.axis_index("sec"), 2)
     for d, copy in enumerate(copies):
         copy.wait()
-        hi_ref[d], lo_ref[d] = split(raw_ref[d])
+        for z in range(send_refs[0].shape[2] // LANES):
+            cols = slice(z * LANES, (z + 1) * LANES)
+            send_refs[0][d, :, cols], send_refs[1][d, :, cols] = split(raw_ref[d, :, block_of(2 * z + 1 - core)])
+            keep_refs[0][d, :, cols], keep_refs[1][d, :, cols] = split(raw_ref[d, :, block_of(2 * z + core)])
 
 
 def fetch_integrals(turn, ladder_ints, d0):
@@ -202,9 +276,9 @@
     vmem = pl.BlockSpec(memory_space=pltpu.VMEM)
     return pl.pallas_call(
         functools.partial(fetch_kernel, d0),
-        out_shape=[jax.ShapeDtypeStruct((D_STEP, depth, cols), bf16)] * 2,
+        out_shape=[jax.ShapeDtypeStruct((D_STEP, depth, cols // 2), bf16)] * 4,
         in_specs=[pl.BlockSpec(memory_space=pl.ANY)] * 2,
-        out_specs=[vmem] * 2,
+        out_specs=[vmem] * 4,
         scratch_shapes=[pltpu.VMEM((D_STEP, depth, cols), f32), pltpu.SemaphoreType.DMA((D_STEP,))],
         compiler_params=pltpu.CompilerParams(vmem_limit_bytes=SMALL_LIMIT),
         cost_estimate=pl.CostEstimate(flops=0, bytes_accessed=8 * D_STEP * depth * cols, transcendentals=0),
@@ -212,14 +286,12 @@
     )(turn, ladder_ints)
 
 
-def closing_kernel(n, *refs):
-    a_refs, (hi_ref, lo_ref, acc_in, send_ref, keep_ref, acc_ref) = refs[:n], refs[n:]
-    acc_ref[...] = acc_in[...]
-    for d in range(0, D_STEP, 2):
-        w_hi = hi_ref[d : d + 2].reshape(2 * LANES, -1)
-        w_lo = lo_ref[d : d + 2].reshape(2 * LANES, -1)
-        acc_ref[...] += dot_split(two_steps(a_refs, d), w_hi, w_lo)
-    pair_halves(acc_ref, send_ref, keep_ref)
+def closing_kernel(n, turn_ref, *refs):
+    a_refs, (hi_ref, lo_ref, acc_ref, out_ref) = refs[:n], refs[n:]
+    deep = D_STEP * LANES
+    w_hi = hi_ref[...].reshape(deep, -1)
+    w_lo = lo_ref[...].reshape(deep, -1)
+    out_ref[...] = acc_ref[...] + dot_split(side_by_side(a_refs), w_hi, w_lo)
 
 
 def cycle_kernel(owners, steps, *refs):
@@ -296,9 +368,8 @@
             out_ref[pl.ds(offset + j, 1), :] = src[j : j + 1, :]
 
 
-def line_kernel(*refs):
-    half = len(refs) // 2 + 1
-    cycle_ref, terms, outs = refs[0], refs[1:half], refs[half:]
+def line_kernel(n, *refs):
+    cycle_ref, terms, outs = refs[0], refs[1:n], refs[n:]
     z = lax.axis_index("sec") // 2
     for q, out in enumerate(outs):
         cols = block_of(z ^ q)
@@ -308,6 +379,30 @@
         out[...] = 0.5 * total + cycle_ref[:, cols]
 
 
+def setup_kernel(turn_ref, counts, occ, vir, occ_ref, vir_ref, pair_in, pair_ref, den_ref, live_ref):
+    owner = lax.axis_index("occ")
+    rows, cols = pair_in.shape
+    pair_ref[...] = pair_in[...]
+    column = jnp.broadcast_to(occ_ref[...], (cols, rows)).T
+    vir_pairs = vir[lax.axis_index("sec")] + vir_ref[:, :cols]
+    den_ref[...] = (occ[owner] + column) - vir_pairs
+    row = lax.broadcasted_iota(jnp.int32, (rows, cols), 0)
+    live_ref[...] = (row < counts[owner]).astype(f32)
+
+
+def setup(turn, live_pairs, occ_energy, vir_energy, pair_ints):
+    vmem, smem = pl.BlockSpec(memory_space=pltpu.VMEM), pl.BlockSpec(memory_space=pltpu.SMEM)
+    return pl.pallas_call(
+        setup_kernel,
+        out_shape=[sds(*pair_ints.shape)] * 3,
+        in_specs=[pl.BlockSpec(memory_space=pl.ANY)] + [smem] * 3 + [vmem] * 3,
+        out_specs=[vmem] * 3,
+        compiler_params=pltpu.CompilerParams(vmem_limit_bytes=SMALL_LIMIT),
+        cost_estimate=pl.CostEstimate(flops=0, bytes_accessed=16 * pair_ints.size, transcendentals=0),
+        name="setup",
+    )(turn, live_pairs, occ_energy, vir_energy, occ_energy.reshape(1, -1), vir_energy.reshape(1, -1), pair_ints)
+
+
 def final_kernel(*refs):
     *terms, pair_ref, den_ref, live_ref, out_ref = refs
     total = pair_ref[...]
@@ -320,14 +415,11 @@
     owners = lax.axis_size("occ")
     sections = lax.axis_size("sec")
     owner_index = lax.axis_index("occ")
-    section = lax.axis_index("sec")
     owner_rows = I_OWNER * OCCUPIED
     owner_cols = OCCUPIED // owners
-    col_share = A_WINDOW * B_WINDOW // sections
     d_share = amplitudes.shape[2]
     ids = owner_index.reshape(1).astype(jnp.int32)
     flipped = amplitudes.transpose(0, 2, 1)
-    live_count = lax.dynamic_slice_in_dim(live_pairs, owner_index, 1)[0]
 
     def exchange(values):
         moved = {}
@@ -343,10 +435,7 @@
     arrived = []
     turn = ids
     for c, (d0, dn) in enumerate(chunks):
-        if c < len(chunks) - 1:
-            pieces = slice_chunk(after(ids, turn), flipped, owners, d0, dn)
-        else:
-            closing_own, *pieces = slice_chunk(after(ids, turn), flipped, owners, d0, dn, 0)
+        pieces = slice_chunk(after(ids, turn), flipped, owners, d0, dn)
         arrived.append(exchange(pieces))
         turn = pieces[0]
         if c == 0:
@@ -360,36 +449,31 @@
     blocks = [own, *exchange(sends)]
     cycle = small(functools.partial(place_kernel, owner_cols), sds(owner_rows, own.shape[1]), blocks)
 
-    acc = None
-    turn = own
-    for c, ((d0, dn), values) in enumerate(zip(chunks[:-1], arrived)):
-        acc = ladder_product(after(ids, turn), flipped, values, ladder_ints, acc, d0, dn)
-        turn = ids
-        if c == 0:
-            parts = fetch_integrals(after(ids, acc), ladder_ints, chunks[-1][0])
-            turn = parts[0]
-    send, keep = small(
-        functools.partial(closing_kernel, owners),
-        [sds(acc.shape[0], acc.shape[1] // 2)] * 2,
-        [closing_own, *arrived[-1], *parts, acc],
-        [pltpu.VMEM(acc.shape, f32)],
-    )
-    own, *sends = add_blocks(keep, swap_pair(send), owners)
-    terms = [cycle, own, *exchange(sends)]
+    parts = fetch_integrals(after(ids, own), ladder_ints, chunks[-1][0])
+    pair, denominator, live_out = setup(after(ids, parts[0]), live_pairs, occ_energy, vir_energy, pair_ints)
+    far = chunks[2][0]
+    (acc,) = ladder_product(after(ids, pair), [[flipped]], ladder_ints, far, lanes=True)
+    own_send, own_keep, acc = ladder_product(ids, arrived[:2], ladder_ints, 0, own=flipped, acc=acc)
+    own_recv = swap_pair(own_send)
+    far_send, far_keep = ladder_product(ids, arrived[2:-1], ladder_ints, far, acc=acc)
+
+    def closing(turn, hi, lo, acc):
+        operands = [turn, *arrived[-1], hi, lo, acc]
+        return small(functools.partial(closing_kernel, len(arrived[-1])), sds(*acc.shape), operands)
+
+    far_send = closing(ids, *parts[:2], far_send)
+    far_recv = swap_pair(far_send)
+    far_keep = closing(after(ids, far_send), *parts[2:], far_keep)
+    sends = add_blocks(far_keep, far_recv, owners - 1)
+    terms = [cycle, own_keep, own_recv, *exchange(sends)]
     lines = sections // 2
-    pieces = small(line_kernel, [sds(owner_rows, LANES)] * lines, terms)
+    pieces = small(functools.partial(line_kernel, len(terms)), [sds(owner_rows, LANES)] * lines, terms)
     recvs = [
         lax.ppermute(pieces[q], "sec", [(s, s ^ (2 * q)) for s in range(sections)]) for q in reversed(range(1, lines))
     ]
 
-    occ_rows = lax.dynamic_slice_in_dim(occ_energy, owner_index * I_OWNER, I_OWNER)
-    pair_energy = (occ_rows[:, None] + occ_energy[None, :]).reshape(owner_rows, 1)
-    vir_pairs = (vir_energy[:A_WINDOW, None] + vir_energy[None, :B_WINDOW]).reshape(A_WINDOW * B_WINDOW)
-    vir_cols = lax.dynamic_slice_in_dim(vir_pairs, section * col_share, col_share)
-    denominator = pair_energy - vir_cols[None, :]
-    live_out = (lax.broadcasted_iota(jnp.int32, (owner_rows, col_share), 0) < live_count).astype(f32)
-    operands = [pieces[0], *recvs, pair_ints, denominator, live_out]
-    return small(final_kernel, sds(owner_rows, col_share), operands)
+    operands = [pieces[0], *recvs, pair, denominator, live_out]
+    return small(final_kernel, sds(*pair_ints.shape), operands)
 
 
 def gathered(amplitudes, live_pairs, ladder_ints, cycle_ints, pair_ints, occ_energy, vir_energy):

time: 136 us -> 141 us (1.037)
  waiting for transfers between devices: 43.1 us -> 56 us
  local copies, waits for them, and re-layouts: 5.7 us -> 0.67 us
  other arithmetic: 1.48 us -> 0 us
    ppermute x21, waiting for transfers between devices: 39.8 us -> 50.5 us  [exchange(): lax.ppermute(values[k - 1], 'occ', [(o, o ^ k) for o in range(owners)])]
    unnamed x26 -> x10, local copies, waits for them, and re-layouts: 4.29 us -> 0.67 us
    ppermute x2 -> x3, waiting for transfers between devices: 0.01 us -> 1.58 us  [swap_pair(): return lax.ppermute(value, 'sec', [(s, s ^ 1) for s in range(sections)])]
    pallas_call x7 -> x8, Pallas kernels: 34.4 us -> 33.5 us  [the longest x3 27.5 us: ladder_product(): pl.pallas_call(functools.partial(ladder_kernel, block0, steps, with_own,...]
  transfers between devices with their start and end apart: 26 -> 27, of which waited for: 9 -> 9; matrix products, arithmetic and copies ran while one was open for 2% -> 0% of each run, Pallas kernels for 31% -> 31%
where the time goes in v3:
time: 141 us; the launch traced here: 140 us
  waiting for transfers between devices  56 us (40%)
  Pallas kernels  49.9 us (35%)
  starting transfers between devices  33.4 us (24%)
    ppermute x21, waiting for transfers between devices, exchange(): lax.ppermute(values[k - 1], 'occ', [(o, o ^ k) for o in range(owners)])  50.5 us
    ppermute x21, starting transfers between devices, exchange(): lax.ppermute(values[k - 1], 'occ', [(o, o ^ k) for o in range(owners)])  28.6 us
    pallas_call x3, Pallas kernels, ladder_product(): pl.pallas_call(functools.partial(ladder_kernel, block0, steps, with_own,...  27.5 us
    pallas_call x1, Pallas kernels, cycle_product(): pl.pallas_call(functools.partial(cycle_kernel, owners, steps), out_shape=...  9.47 us
    pallas_call x4, Pallas kernels, slice_chunk(): pl.pallas_call(functools.partial(slice_kernel, d0), out_shape=[sds(rows,...  5.27 us
    ppermute x3, starting transfers between devices, streamed_parts(): lax.ppermute(pieces[q], 'sec', [(s, s ^ 2 * q) for s in range(sections)])  4.45 us
    ppermute x3, waiting for transfers between devices, streamed_parts(): lax.ppermute(pieces[q], 'sec', [(s, s ^ 2 * q) for s in range(sections)])  3.94 us
  transfers between devices with their start and end apart: 27, of which 9 were waited for; matrix products, arithmetic and copies ran while one was open for 0% of the time, Pallas kernels for 31%

profile of v3, /device:TPU:0, one launch (start us, length us, event | category | flops | bytes accessed | tf_op | source)
XLA Modules:
  0.0 140.2 jit_solution(12504679787977768895)
XLA Ops:
  1.8 2.1 %cycle_window.1.refs_0_ = f32[24,8,128]{2,1,0:T(8,128)S(1)} custom-call(s32[1]{0:T(128)} %bitcast.turn_ref.turn, s32[4]{0:T(128)S(1)} %copy-done.3, f32[48,64,512]{2,1,0:T(8,128)} %bitcast.7), custom_call_target="tpu_custom_call" | custom-call | bytes 1572864 | tf_op jit(solution)/shard_map/cycle_window/pallas_call | solution.py:124
  3.9 1.7 %slices.5 = (f32[48,32,128]{2,1,0:T(8,128)S(1)}, f32[48,32,128]{2,1,0:T(8,128)S(1)}, f32[48,32,128]{2,1,0:T(8,128)S(1)}) custom-call(s32[1]{0:T(128)} %bitcast.turn_ref.turn, f32[48,64,512]{2,1,0:T(8,128)} %bitcast.8), custom_call_target="tpu_custom_call" | custom-call | bytes 4718592 | tf_op jit(solution)/shard_map/slices/pallas_call | solution.py:89
  5.6 3.0 %collective-permute-start.10 = (f32[48,32,128]{2,1,0:T(8,128)S(1)}, f32[48,32,128]{2,1,0:T(8,128)S(1)}, u32[]{:S(2)}, u32[]{:S(2)}) collective-permute-start(f32[48,32,128]{2,1,0:T(8,128)S(1)} %get-tuple-element.63), channel_id=1, source_target_pairs={{0,8},{8,0},{16,24},{24,16},{1,9},{9,1},{17,25},{25,17},{2,10},{10... | collective-permute-start | bytes 2359304 | tf_op jit(solution)/shard_map/ppermute | solution.py:427
  8.7 1.5 %collective-permute-start.11 = (f32[48,32,128]{2,1,0:T(8,128)S(1)}, f32[48,32,128]{2,1,0:T(8,128)S(1)}, u32[]{:S(2)}, u32[]{:S(2)}) collective-permute-start(f32[48,32,128]{2,1,0:T(8,128)S(1)} %get-tuple-element.64), channel_id=1, source_target_pairs={{0,16},{8,24},{16,0},{24,8},{1,17},{9,25},{17,1},{25,9},{2,18},{10... | collective-permute-start | bytes 2359304 | tf_op jit(solution)/shard_map/ppermute | solution.py:427
  10.2 1.9 %collective-permute-start = (f32[24,8,128]{2,1,0:T(8,128)S(1)}, f32[24,8,128]{2,1,0:T(8,128)S(1)}, u32[]{:S(2)}, u32[]{:S(2)}) collective-permute-start(f32[24,8,128]{2,1,0:T(8,128)S(1)} %cycle_window.1.refs_0_), channel_id=1, source_target_pairs={{0,8},{8,0},{16,24},{24,16},{1,9},{9,1},{17,25},{25,17},{2,10},{10... | collective-permute-start | bytes 294920 | tf_op jit(solution)/shard_map/ppermute | solution.py:427
  12.2 1.5 %collective-permute-start.1 = (f32[24,8,128]{2,1,0:T(8,128)S(1)}, f32[24,8,128]{2,1,0:T(8,128)S(1)}, u32[]{:S(2)}, u32[]{:S(2)}) collective-permute-start(f32[24,8,128]{2,1,0:T(8,128)S(1)} %cycle_window.1.refs_0_), channel_id=1, source_target_pairs={{0,16},{8,24},{16,0},{24,8},{1,17},{9,25},{17,1},{25,9},{2,18},{10... | collective-permute-start | bytes 294920 | tf_op jit(solution)/shard_map/ppermute | solution.py:427
  13.7 31.5 %collective-permute-done.refs_1_ = f32[24,8,128]{2,1,0:T(8,128)S(1)} collective-permute-done((f32[24,8,128]{2,1,0:T(8,128)S(1)}, f32[24,8,128]{2,1,0:T(8,128)S(1)}, u32[]{:S(2)}, u32[]{:S(2)}) %collective-permute-start) | collective-permute-done | bytes 98336 | tf_op jit(solution)/shard_map/ppermute | solution.py:427
  45.2 2.7 %collective-permute-start.2 = (f32[24,8,128]{2,1,0:T(8,128)S(1)}, f32[24,8,128]{2,1,0:T(8,128)S(1)}, u32[]{:S(2)}, u32[]{:S(2)}) collective-permute-start(f32[24,8,128]{2,1,0:T(8,128)S(1)} %cycle_window.1.refs_0_), channel_id=1, source_target_pairs={{0,24},{8,16},{16,8},{24,0},{1,25},{9,17},{17,9},{25,1},{2,26},{10... | collective-permute-start | bytes 294920 | tf_op jit(solution)/shard_map/ppermute | solution.py:427
  48.5 3.3 %collective-permute-done.2.refs_3_ = f32[24,8,128]{2,1,0:T(8,128)S(1)} collective-permute-done((f32[24,8,128]{2,1,0:T(8,128)S(1)}, f32[24,8,128]{2,1,0:T(8,128)S(1)}, u32[]{:S(2)}, u32[]{:S(2)}) %collective-permute-start.2) | collective-permute-done | bytes 98336 | tf_op jit(solution)/shard_map/ppermute | solution.py:427
  51.8 1.8 %collective-permute-start.8 = (f32[48,8,128]{2,1,0:T(8,128)S(1)}, f32[48,8,128]{2,1,0:T(8,128)S(1)}, u32[]{:S(2)}, u32[]{:S(2)}) collective-permute-start(f32[48,8,128]{2,1,0:T(8,128)S(1)} %get-tuple-element.60), channel_id=1, source_target_pairs={{0,16},{8,24},{16,0},{24,8},{1,17},{9,25},{17,1},{25,9},{2,18},{10... | collective-permute-start | bytes 589832 | tf_op jit(solution)/shard_map/ppermute | solution.py:427
  53.6 1.3 slices.6
  54.9 1.6 %collective-permute-start.17 = (f32[48,16,128]{2,1,0:T(8,128)S(1)}, f32[48,16,128]{2,1,0:T(8,128)S(1)}, u32[]{:S(2)}, u32[]{:S(2)}) collective-permute-start(f32[48,16,128]{2,1,0:T(8,128)S(1)} %get-tuple-element.74), channel_id=1, source_target_pairs={{0,8},{8,0},{16,24},{24,16},{1,9},{9,1},{17,25},{25,17},{2,10},{10... | collective-permute-start | bytes 1179656 | tf_op jit(solution)/shard_map/ppermute | solution.py:427
  56.4 9.5 %cycle_product.1 = (f32[64,512]{1,0:T(8,128)S(1)}, f32[64,512]{1,0:T(8,128)S(1)}) custom-call(f32[24,8,128]{2,1,0:T(8,128)S(1)} %cycle_window.1.refs_0_, f32[24,8,128]{2,1,0:T(8,128)S(1)} %collective-permute-done.refs_1_, f32[24,8,128]{2,1,0:T(8,128)S(1)} %collective-permute-done.1.refs_2_, f32[24,8,128]{2,1,0:T(8,128)S(1)} %collective-permute-done.2.refs_3_, ...), custom_call_target="tpu_custom_call" | custom-call | flops 905969664 | bytes 18874368 | tf_op jit(solution)/shard_map/cycle_product/pallas_call | solution.py:331
  66.0 1.3 collective-permute-done.3.recv_ref
  68.8 2.5 %fetch_integrals.1 = (bf16[8,128,512]{2,1,0:T(8,128)(2,1)S(1)}, bf16[8,128,512]{2,1,0:T(8,128)(2,1)S(1)}, bf16[8,128,512]{2,1,0:T(8,128)(2,1)S(1)}, bf16[8,128,512]{2,1,0:T(8,128)(2,1)S(1)}) custom-call(s32[1]{0:T(128)} %bitcast.turn_ref.turn, f32[128,64,1024]{2,1,0:T(8,128)} %refs_3_.1), custom_call_target="tpu_custom_call" | custom-call | bytes 8388608 | tf_op jit(solution)/shard_map/fetch_integrals/pallas_call | solution.py:277
  72.0 7.9 %ladder_product.3.refs_8_ = f32[48,1024]{1,0:T(8,128)S(1)} custom-call(s32[1]{0:T(128)} %bitcast.turn_ref.turn, f32[48,64,512]{2,1,0:T(8,128)} %bitcast.11, f32[128,64,1024]{2,1,0:T(8,128)} %refs_3_.1), custom_call_target="tpu_custom_call" | custom-call | flops 905969664 | bytes 12582912 | tf_op jit(solution)/shard_map/ladder_product/pallas_call | solution.py:228
  79.9 1.8 %collective-permute-start.14 = (f32[48,8,128]{2,1,0:T(8,128)S(1)}, f32[48,8,128]{2,1,0:T(8,128)S(1)}, u32[]{:S(2)}, u32[]{:S(2)}) collective-permute-start(f32[48,8,128]{2,1,0:T(8,128)S(1)} %get-tuple-element.76), channel_id=1, source_target_pairs={{0,8},{8,0},{16,24},{24,16},{1,9},{9,1},{17,25},{25,17},{2,10},{10... | collective-permute-start | bytes 589832 | tf_op jit(solution)/shard_map/ppermute | solution.py:427
  81.7 1.5 %collective-permute-start.15 = (f32[48,8,128]{2,1,0:T(8,128)S(1)}, f32[48,8,128]{2,1,0:T(8,128)S(1)}, u32[]{:S(2)}, u32[]{:S(2)}) collective-permute-start(f32[48,8,128]{2,1,0:T(8,128)S(1)} %get-tuple-element.77), channel_id=1, source_target_pairs={{0,16},{8,24},{16,0},{24,8},{1,17},{9,25},{17,1},{25,9},{2,18},{10... | collective-permute-start | bytes 589832 | tf_op jit(solution)/shard_map/ppermute | solution.py:427
  83.4 1.8 %collective-permute-start.18 = (f32[48,16,128]{2,1,0:T(8,128)S(1)}, f32[48,16,128]{2,1,0:T(8,128)S(1)}, u32[]{:S(2)}, u32[]{:S(2)}) collective-permute-start(f32[48,16,128]{2,1,0:T(8,128)S(1)} %get-tuple-element.80), channel_id=1, source_target_pairs={{0,16},{8,24},{16,0},{24,8},{1,17},{9,25},{17,1},{25,9},{2,18},{10... | collective-permute-start | bytes 1179656 | tf_op jit(solution)/shard_map/ppermute | solution.py:427
  85.2 1.4 %collective-permute-start.19 = (f32[48,16,128]{2,1,0:T(8,128)S(1)}, f32[48,16,128]{2,1,0:T(8,128)S(1)}, u32[]{:S(2)}, u32[]{:S(2)}) collective-permute-start(f32[48,16,128]{2,1,0:T(8,128)S(1)} %get-tuple-element.81), channel_id=1, source_target_pairs={{0,24},{8,16},{16,8},{24,0},{1,25},{9,17},{17,9},{25,1},{2,26},{10... | collective-permute-start | bytes 1179656 | tf_op jit(solution)/shard_map/ppermute | solution.py:427
  86.6 14.3 %ladder_product.4 = (f32[48,512]{1,0:T(8,128)S(1)}, f32[48,512]{1,0:T(8,128)S(1)}, f32[144,1024]{1,0:T(8,128)S(1)}) custom-call(s32[1]{0:T(128)} %bitcast.turn_ref.turn, f32[48,64,512]{2,1,0:T(8,128)} %bitcast.12, f32[48,8,128]{2,1,0:T(8,128)S(1)} %collective-permute-done.7.refs_1_, f32[48,8,128]{2,1,0:T(8,128)S(1)} %collective-permute-done.8.refs_2_, ...), custom_call_target="tpu_custom_call" | custom-call | flops 6039797760 | bytes 20971520 | tf_op jit(solution)/shard_map/ladder_product/pallas_call | solution.py:228
  100.9 8.2 %collective-permute-done.18.refs_1_ = f32[48,16,128]{2,1,0:T(8,128)S(1)} collective-permute-done((f32[48,16,128]{2,1,0:T(8,128)S(1)}, f32[48,16,128]{2,1,0:T(8,128)S(1)}, u32[]{:S(2)}, u32[]{:S(2)}) %collective-permute-start.18) | collective-permute-done | bytes 393248 | tf_op jit(solution)/shard_map/ppermute | solution.py:427
  109.1 5.4 %ladder_product.5 = (f32[144,512]{1,0:T(8,128)S(1)}, f32[144,512]{1,0:T(8,128)S(1)}) custom-call(s32[1]{0:T(128)} %bitcast.turn_ref.turn, f32[48,16,128]{2,1,0:T(8,128)S(1)} %collective-permute-done.17.refs_0_, f32[48,16,128]{2,1,0:T(8,128)S(1)} %collective-permute-done.18.refs_1_, f32[48,16,128]{2,1,0:T(8,128)S(1)} %collective-permute-done.19.refs_2_, ...), custom_call_target="tpu_custom_call" | custom-call | flops 1811939328 | bytes 8388608 | tf_op jit(solution)/shard_map/ladder_product/pallas_call | solution.py:228
  117.0 1.5 %collective-permute-start.21 = (f32[48,512]{1,0:T(8,128)S(1)}, f32[48,512]{1,0:T(8,128)S(1)}, u32[]{:S(2)}, u32[]{:S(2)}) collective-permute-start(f32[48,512]{1,0:T(8,128)S(1)} %get-tuple-element.88), channel_id=1, source_target_pairs={{0,8},{8,0},{16,24},{24,16},{1,9},{9,1},{17,25},{25,17},{2,10},{10... | collective-permute-start | bytes 294920 | tf_op jit(solution)/shard_map/ppermute | solution.py:427
  118.5 1.5 %collective-permute-start.22 = (f32[48,512]{1,0:T(8,128)S(1)}, f32[48,512]{1,0:T(8,128)S(1)}, u32[]{:S(2)}, u32[]{:S(2)}) collective-permute-start(f32[48,512]{1,0:T(8,128)S(1)} %get-tuple-element.89), channel_id=1, source_target_pairs={{0,16},{8,24},{16,0},{24,8},{1,17},{9,25},{17,1},{25,9},{2,18},{10... | collective-permute-start | bytes 294920 | tf_op jit(solution)/shard_map/ppermute | solution.py:427
  120.6 1.5 %collective-permute-start.5 = (f32[16,512]{1,0:T(8,128)S(1)}, f32[16,512]{1,0:T(8,128)S(1)}, u32[]{:S(2)}, u32[]{:S(2)}) collective-permute-start(f32[16,512]{1,0:T(8,128)S(1)} %get-tuple-element.58), channel_id=1, source_target_pairs={{0,16},{8,24},{16,0},{24,8},{1,17},{9,25},{17,1},{25,9},{2,18},{10... | collective-permute-start | bytes 98312 | tf_op jit(solution)/shard_map/ppermute | solution.py:427
  122.1 4.0 %collective-permute-done.5.refs_2_ = f32[16,512]{1,0:T(8,128)S(1)} collective-permute-done((f32[16,512]{1,0:T(8,128)S(1)}, f32[16,512]{1,0:T(8,128)S(1)}, u32[]{:S(2)}, u32[]{:S(2)}) %collective-permute-start.5) | collective-permute-done | bytes 32800 | tf_op jit(solution)/shard_map/ppermute | solution.py:427
  126.1 1.5 %collective-permute-start.6 = (f32[16,512]{1,0:T(8,128)S(1)}, f32[16,512]{1,0:T(8,128)S(1)}, u32[]{:S(2)}, u32[]{:S(2)}) collective-permute-start(f32[16,512]{1,0:T(8,128)S(1)} %get-tuple-element.59), channel_id=1, source_target_pairs={{0,24},{8,16},{16,8},{24,0},{1,25},{9,17},{17,9},{25,1},{2,26},{10... | collective-permute-start | bytes 98312 | tf_op jit(solution)/shard_map/ppermute | solution.py:427
  127.6 3.3 %collective-permute-done.6.refs_3_ = f32[16,512]{1,0:T(8,128)S(1)} collective-permute-done((f32[16,512]{1,0:T(8,128)S(1)}, f32[16,512]{1,0:T(8,128)S(1)}, u32[]{:S(2)}, u32[]{:S(2)}) %collective-permute-start.6) | collective-permute-done | bytes 32800 | tf_op jit(solution)/shard_map/ppermute | solution.py:427
  131.2 3.7 %collective-permute-start.24 = (f32[48,128]{1,0:T(8,128)S(1)}, f32[48,128]{1,0:T(8,128)S(1)}, u32[]{:S(2)}, u32[]{:S(2)}) collective-permute-start(f32[48,128]{1,0:T(8,128)S(1)} %get-tuple-element.92), channel_id=1, source_target_pairs={{0,6},{1,7},{2,4},{3,5},{4,2},{5,3},{6,0},{7,1},{8,14},{9,15},{10,... | collective-permute-start | bytes 73736 | tf_op jit(solution)/shard_map/ppermute | solution.py:472
  135.6 1.4 collective-permute-done.24.refs_1_
  137.0 2.6 %collective-permute-done.25.refs_2_ = f32[48,128]{1,0:T(8,128)S(1)} collective-permute-done((f32[48,128]{1,0:T(8,128)S(1)}, f32[48,128]{1,0:T(8,128)S(1)}, u32[]{:S(2)}, u32[]{:S(2)}) %collective-permute-start.25) | collective-permute-done | bytes 24608 | tf_op jit(solution)/shard_map/ppermute | solution.py:472
  (50 shorter events, 9.4 us)
Async XLA Ops:
  1.2 0.7 copy-start.3
  5.6 77.6 %collective-permute-start.10 = (f32[48,32,128]{2,1,0:T(8,128)S(1)}, f32[48,32,128]{2,1,0:T(8,128)S(1)}, u32[]{:S(2)}, u32[]{:S(2)}) collective-permute-start(f32[48,32,128]{2,1,0:T(8,128)S(1)} %get-tuple-element.63), channel_id=1, source_target_pairs={{0,8},{8,0},{16,24},{24,16},{1,9},{9,1},{17,25},{25,17},{2,10},{10... | collective-permute-start | bytes 2359304 | tf_op jit(solution)/shard_map/ppermute | solution.py:427
  8.7 74.8 %collective-permute-start.11 = (f32[48,32,128]{2,1,0:T(8,128)S(1)}, f32[48,32,128]{2,1,0:T(8,128)S(1)}, u32[]{:S(2)}, u32[]{:S(2)}) collective-permute-start(f32[48,32,128]{2,1,0:T(8,128)S(1)} %get-tuple-element.64), channel_id=1, source_target_pairs={{0,16},{8,24},{16,0},{24,8},{1,17},{9,25},{17,1},{25,9},{2,18},{10... | collective-permute-start | bytes 2359304 | tf_op jit(solution)/shard_map/ppermute | solution.py:427
  10.2 75.0 %collective-permute-start.12 = (f32[48,32,128]{2,1,0:T(8,128)S(1)}, f32[48,32,128]{2,1,0:T(8,128)S(1)}, u32[]{:S(2)}, u32[]{:S(2)}) collective-permute-start(f32[48,32,128]{2,1,0:T(8,128)S(1)} %get-tuple-element.65), channel_id=1, source_target_pairs={{0,24},{8,16},{16,8},{24,0},{1,25},{9,17},{17,9},{25,1},{2,26},{10... | collective-permute-start | bytes 2359304 | tf_op jit(solution)/shard_map/ppermute | solution.py:427
  10.2 35.0 %collective-permute-start = (f32[24,8,128]{2,1,0:T(8,128)S(1)}, f32[24,8,128]{2,1,0:T(8,128)S(1)}, u32[]{:S(2)}, u32[]{:S(2)}) collective-permute-start(f32[24,8,128]{2,1,0:T(8,128)S(1)} %cycle_window.1.refs_0_), channel_id=1, source_target_pairs={{0,8},{8,0},{16,24},{24,16},{1,9},{9,1},{17,25},{25,17},{2,10},{10... | collective-permute-start | bytes 294920 | tf_op jit(solution)/shard_map/ppermute | solution.py:427
  12.2 35.8 %collective-permute-start.1 = (f32[24,8,128]{2,1,0:T(8,128)S(1)}, f32[24,8,128]{2,1,0:T(8,128)S(1)}, u32[]{:S(2)}, u32[]{:S(2)}) collective-permute-start(f32[24,8,128]{2,1,0:T(8,128)S(1)} %cycle_window.1.refs_0_), channel_id=1, source_target_pairs={{0,16},{8,24},{16,0},{24,8},{1,17},{9,25},{17,1},{25,9},{2,18},{10... | collective-permute-start | bytes 294920 | tf_op jit(solution)/shard_map/ppermute | solution.py:427
  45.2 6.6 %collective-permute-start.2 = (f32[24,8,128]{2,1,0:T(8,128)S(1)}, f32[24,8,128]{2,1,0:T(8,128)S(1)}, u32[]{:S(2)}, u32[]{:S(2)}) collective-permute-start(f32[24,8,128]{2,1,0:T(8,128)S(1)} %cycle_window.1.refs_0_), channel_id=1, source_target_pairs={{0,24},{8,16},{16,8},{24,0},{1,25},{9,17},{17,9},{25,1},{2,26},{10... | collective-permute-start | bytes 294920 | tf_op jit(solution)/shard_map/ppermute | solution.py:427
  47.9 6.9 %collective-permute-start.7 = (f32[48,8,128]{2,1,0:T(8,128)S(1)}, f32[48,8,128]{2,1,0:T(8,128)S(1)}, u32[]{:S(2)}, u32[]{:S(2)}) collective-permute-start(f32[48,8,128]{2,1,0:T(8,128)S(1)} %get-tuple-element.52), channel_id=1, source_target_pairs={{0,8},{8,0},{16,24},{24,16},{1,9},{9,1},{17,25},{25,17},{2,10},{10... | collective-permute-start | bytes 589832 | tf_op jit(solution)/shard_map/ppermute | solution.py:427
  51.8 14.1 %collective-permute-start.8 = (f32[48,8,128]{2,1,0:T(8,128)S(1)}, f32[48,8,128]{2,1,0:T(8,128)S(1)}, u32[]{:S(2)}, u32[]{:S(2)}) collective-permute-start(f32[48,8,128]{2,1,0:T(8,128)S(1)} %get-tuple-element.60), channel_id=1, source_target_pairs={{0,16},{8,24},{16,0},{24,8},{1,17},{9,25},{17,1},{25,9},{2,18},{10... | collective-permute-start | bytes 589832 | tf_op jit(solution)/shard_map/ppermute | solution.py:427
  54.9 26.8 %collective-permute-start.17 = (f32[48,16,128]{2,1,0:T(8,128)S(1)}, f32[48,16,128]{2,1,0:T(8,128)S(1)}, u32[]{:S(2)}, u32[]{:S(2)}) collective-permute-start(f32[48,16,128]{2,1,0:T(8,128)S(1)} %get-tuple-element.74), channel_id=1, source_target_pairs={{0,8},{8,0},{16,24},{24,16},{1,9},{9,1},{17,25},{25,17},{2,10},{10... | collective-permute-start | bytes 1179656 | tf_op jit(solution)/shard_map/ppermute | solution.py:427
  65.9 1.4 %collective-permute-start.3 = (f32[64,512]{1,0:T(8,128)S(1)}, f32[64,512]{1,0:T(8,128)S(1)}, u32[]{:S(2)}, u32[]{:S(2)}) collective-permute-start(f32[64,512]{1,0:T(8,128)S(1)} %get-tuple-element.55), channel_id=1, source_target_pairs={{0,1},{1,0},{2,3},{3,2},{4,5},{5,4},{6,7},{7,6},{8,9},{9,8},{10,11... | collective-permute-start | bytes 393224 | tf_op jit(solution)/shard_map/ppermute | solution.py:431
  67.3 4.0 %copy-start = (f32[48,128]{1,0:T(8,128)S(1)}, f32[48,128]{1,0:T(8,128)}, u32[]{:S(2)}) copy-start(f32[48,128]{1,0:T(8,128)} %pair_in.1) | copy-start | bytes 73732
  67.3 4.0 %copy-start.1 = (f32[512]{0:T(512)S(1)}, f32[512]{0:T(512)}, u32[]{:S(2)}) copy-start(f32[512]{0:T(512)} %vir.1) | copy-start | bytes 6148
  67.3 4.0 %copy-start.2 = (f32[48]{0:T(128)S(1)}, f32[48]{0:T(128)}, u32[]{:S(2)}) copy-start(f32[48]{0:T(128)} %occ.1) | copy-start | bytes 580
  67.3 4.0 %copy-start.4 = (s32[4]{0:T(128)S(1)}, s32[4]{0:T(128)}, u32[]{:S(2)}) copy-start(s32[4]{0:T(128)} %counts.3) | copy-start | bytes 52
  67.3 12.5 %collective-permute-start.9 = (f32[48,8,128]{2,1,0:T(8,128)S(1)}, f32[48,8,128]{2,1,0:T(8,128)S(1)}, u32[]{:S(2)}, u32[]{:S(2)}) collective-permute-start(f32[48,8,128]{2,1,0:T(8,128)S(1)} %get-tuple-element.61), channel_id=1, source_target_pairs={{0,24},{8,16},{16,8},{24,0},{1,25},{9,17},{17,9},{25,1},{2,26},{10... | collective-permute-start | bytes 589832 | tf_op jit(solution)/shard_map/ppermute | solution.py:427
  79.9 34.7 %collective-permute-start.14 = (f32[48,8,128]{2,1,0:T(8,128)S(1)}, f32[48,8,128]{2,1,0:T(8,128)S(1)}, u32[]{:S(2)}, u32[]{:S(2)}) collective-permute-start(f32[48,8,128]{2,1,0:T(8,128)S(1)} %get-tuple-element.76), channel_id=1, source_target_pairs={{0,8},{8,0},{16,24},{24,16},{1,9},{9,1},{17,25},{25,17},{2,10},{10... | collective-permute-start | bytes 589832 | tf_op jit(solution)/shard_map/ppermute | solution.py:427
  81.7 32.9 %collective-permute-start.15 = (f32[48,8,128]{2,1,0:T(8,128)S(1)}, f32[48,8,128]{2,1,0:T(8,128)S(1)}, u32[]{:S(2)}, u32[]{:S(2)}) collective-permute-start(f32[48,8,128]{2,1,0:T(8,128)S(1)} %get-tuple-element.77), channel_id=1, source_target_pairs={{0,16},{8,24},{16,0},{24,8},{1,17},{9,25},{17,1},{25,9},{2,18},{10... | collective-permute-start | bytes 589832 | tf_op jit(solution)/shard_map/ppermute | solution.py:427
  83.2 31.4 %collective-permute-start.16 = (f32[48,8,128]{2,1,0:T(8,128)S(1)}, f32[48,8,128]{2,1,0:T(8,128)S(1)}, u32[]{:S(2)}, u32[]{:S(2)}) collective-permute-start(f32[48,8,128]{2,1,0:T(8,128)S(1)} %get-tuple-element.78), channel_id=1, source_target_pairs={{0,24},{8,16},{16,8},{24,0},{1,25},{9,17},{17,9},{25,1},{2,26},{10... | collective-permute-start | bytes 589832 | tf_op jit(solution)/shard_map/ppermute | solution.py:427
  83.4 25.7 %collective-permute-start.18 = (f32[48,16,128]{2,1,0:T(8,128)S(1)}, f32[48,16,128]{2,1,0:T(8,128)S(1)}, u32[]{:S(2)}, u32[]{:S(2)}) collective-permute-start(f32[48,16,128]{2,1,0:T(8,128)S(1)} %get-tuple-element.80), channel_id=1, source_target_pairs={{0,16},{8,24},{16,0},{24,8},{1,17},{9,25},{17,1},{25,9},{2,18},{10... | collective-permute-start | bytes 1179656 | tf_op jit(solution)/shard_map/ppermute | solution.py:427
  85.2 23.9 %collective-permute-start.19 = (f32[48,16,128]{2,1,0:T(8,128)S(1)}, f32[48,16,128]{2,1,0:T(8,128)S(1)}, u32[]{:S(2)}, u32[]{:S(2)}) collective-permute-start(f32[48,16,128]{2,1,0:T(8,128)S(1)} %get-tuple-element.81), channel_id=1, source_target_pairs={{0,24},{8,16},{16,8},{24,0},{1,25},{9,17},{17,9},{25,1},{2,26},{10... | collective-permute-start | bytes 1179656 | tf_op jit(solution)/shard_map/ppermute | solution.py:427
  115.3 1.6 %collective-permute-start.20 = (f32[144,512]{1,0:T(8,128)S(1)}, f32[144,512]{1,0:T(8,128)S(1)}, u32[]{:S(2)}, u32[]{:S(2)}) collective-permute-start(f32[144,512]{1,0:T(8,128)S(1)} %shard_map.75), channel_id=1, source_target_pairs={{0,1},{1,0},{2,3},{3,2},{4,5},{5,4},{6,7},{7,6},{8,9},{9,8},{10,11... | collective-permute-start | bytes 884744 | tf_op jit(solution)/shard_map/ppermute | solution.py:431
  115.4 5.2 %collective-permute-start.4 = (f32[16,512]{1,0:T(8,128)S(1)}, f32[16,512]{1,0:T(8,128)S(1)}, u32[]{:S(2)}, u32[]{:S(2)}) collective-permute-start(f32[16,512]{1,0:T(8,128)S(1)} %get-tuple-element.57), channel_id=1, source_target_pairs={{0,8},{8,0},{16,24},{24,16},{1,9},{9,1},{17,25},{25,17},{2,10},{10... | collective-permute-start | bytes 98312 | tf_op jit(solution)/shard_map/ppermute | solution.py:427
  115.8 15.2 %collective-permute-start.13 = (f32[48,512]{1,0:T(8,128)S(1)}, f32[48,512]{1,0:T(8,128)S(1)}, u32[]{:S(2)}, u32[]{:S(2)}) collective-permute-start(f32[48,512]{1,0:T(8,128)S(1)} %get-tuple-element.72), channel_id=1, source_target_pairs={{0,1},{1,0},{2,3},{3,2},{4,5},{5,4},{6,7},{7,6},{8,9},{9,8},{10,11... | collective-permute-start | bytes 294920 | tf_op jit(solution)/shard_map/ppermute | solution.py:431
  117.0 14.0 %collective-permute-start.21 = (f32[48,512]{1,0:T(8,128)S(1)}, f32[48,512]{1,0:T(8,128)S(1)}, u32[]{:S(2)}, u32[]{:S(2)}) collective-permute-start(f32[48,512]{1,0:T(8,128)S(1)} %get-tuple-element.88), channel_id=1, source_target_pairs={{0,8},{8,0},{16,24},{24,16},{1,9},{9,1},{17,25},{25,17},{2,10},{10... | collective-permute-start | bytes 294920 | tf_op jit(solution)/shard_map/ppermute | solution.py:427
  118.5 12.5 %collective-permute-start.22 = (f32[48,512]{1,0:T(8,128)S(1)}, f32[48,512]{1,0:T(8,128)S(1)}, u32[]{:S(2)}, u32[]{:S(2)}) collective-permute-start(f32[48,512]{1,0:T(8,128)S(1)} %get-tuple-element.89), channel_id=1, source_target_pairs={{0,16},{8,24},{16,0},{24,8},{1,17},{9,25},{17,1},{25,9},{2,18},{10... | collective-permute-start | bytes 294920 | tf_op jit(solution)/shard_map/ppermute | solution.py:427
  120.0 11.0 %collective-permute-start.23 = (f32[48,512]{1,0:T(8,128)S(1)}, f32[48,512]{1,0:T(8,128)S(1)}, u32[]{:S(2)}, u32[]{:S(2)}) collective-permute-start(f32[48,512]{1,0:T(8,128)S(1)} %get-tuple-element.90), channel_id=1, source_target_pairs={{0,24},{8,16},{16,8},{24,0},{1,25},{9,17},{17,9},{25,1},{2,26},{10... | collective-permute-start | bytes 294920 | tf_op jit(solution)/shard_map/ppermute | solution.py:427
  120.6 5.5 %collective-permute-start.5 = (f32[16,512]{1,0:T(8,128)S(1)}, f32[16,512]{1,0:T(8,128)S(1)}, u32[]{:S(2)}, u32[]{:S(2)}) collective-permute-start(f32[16,512]{1,0:T(8,128)S(1)} %get-tuple-element.58), channel_id=1, source_target_pairs={{0,16},{8,24},{16,0},{24,8},{1,17},{9,25},{17,1},{25,9},{2,18},{10... | collective-permute-start | bytes 98312 | tf_op jit(solution)/shard_map/ppermute | solution.py:427
  126.1 4.8 %collective-permute-start.6 = (f32[16,512]{1,0:T(8,128)S(1)}, f32[16,512]{1,0:T(8,128)S(1)}, u32[]{:S(2)}, u32[]{:S(2)}) collective-permute-start(f32[16,512]{1,0:T(8,128)S(1)} %get-tuple-element.59), channel_id=1, source_target_pairs={{0,24},{8,16},{16,8},{24,0},{1,25},{9,17},{17,9},{25,1},{2,26},{10... | collective-permute-start | bytes 98312 | tf_op jit(solution)/shard_map/ppermute | solution.py:427
  131.2 5.8 %collective-permute-start.24 = (f32[48,128]{1,0:T(8,128)S(1)}, f32[48,128]{1,0:T(8,128)S(1)}, u32[]{:S(2)}, u32[]{:S(2)}) collective-permute-start(f32[48,128]{1,0:T(8,128)S(1)} %get-tuple-element.92), channel_id=1, source_target_pairs={{0,6},{1,7},{2,4},{3,5},{4,2},{5,3},{6,0},{7,1},{8,14},{9,15},{10,... | collective-permute-start | bytes 73736 | tf_op jit(solution)/shard_map/ppermute | solution.py:472
  134.8 4.7 %collective-permute-start.25 = (f32[48,128]{1,0:T(8,128)S(1)}, f32[48,128]{1,0:T(8,128)S(1)}, u32[]{:S(2)}, u32[]{:S(2)}) collective-permute-start(f32[48,128]{1,0:T(8,128)S(1)} %get-tuple-element.93), channel_id=1, source_target_pairs={{0,4},{1,5},{2,6},{3,7},{4,0},{5,1},{6,2},{7,3},{8,12},{9,13},{10,... | collective-permute-start | bytes 73736 | tf_op jit(solution)/shard_map/ppermute | solution.py:472
  134.8 4.7 %collective-permute-start.26 = (f32[48,128]{1,0:T(8,128)S(1)}, f32[48,128]{1,0:T(8,128)S(1)}, u32[]{:S(2)}, u32[]{:S(2)}) collective-permute-start(f32[48,128]{1,0:T(8,128)S(1)} %get-tuple-element.94), channel_id=1, source_target_pairs={{0,2},{1,3},{2,0},{3,1},{4,6},{5,7},{6,4},{7,5},{8,10},{9,11},{10,... | collective-permute-start | bytes 73736 | tf_op jit(solution)/shard_map/ppermute | solution.py:472

commit v4 on v3

--- a/solution.py
+++ b/solution.py
@@ -368,15 +368,35 @@
             out_ref[pl.ds(offset + j, 1), :] = src[j : j + 1, :]
 
 
-def line_kernel(n, *refs):
-    cycle_ref, terms, outs = refs[0], refs[1:n], refs[n:]
+def pair_pieces_kernel(n, keep_ref, recv_ref, *outs):
     z = lax.axis_index("sec") // 2
-    for q, out in enumerate(outs):
+    rows = outs[0].shape[0]
+    per_half = outs[0].shape[1] // LANES
+    for h in range(2):
+        for k in range(n):
+            part = slice(k * rows, (k + 1) * rows)
+            for t in range(per_half):
+                cols = block_of(z ^ (2 * per_half - 1 - h * per_half - t))
+                outs[h * n + k][:, t * LANES : (t + 1) * LANES] = keep_ref[part, cols] + recv_ref[part, cols]
+
+
+def line_kernel(n, lines, cycle_ref, keep_ref, recv_ref, *refs):
+    terms, outs = refs[:n], refs[n:]
+    z = lax.axis_index("sec") // 2
+    for t, (q, out) in enumerate(zip(lines, outs)):
         cols = block_of(z ^ q)
-        total = terms[0][:, cols]
-        for t in terms[1:]:
-            total = total + t[:, cols]
+        total = keep_ref[:, cols] + recv_ref[:, cols]
+        for term in terms:
+            total = total + term[:, t * LANES : (t + 1) * LANES]
         out[...] = 0.5 * total + cycle_ref[:, cols]
+
+
+def final_kernel(*refs):
+    *terms, pair_ref, den_ref, live_ref, out_ref = refs
+    total = pair_ref[...]
+    for t in terms:
+        total = total + t[...]
+    out_ref[...] = total / den_ref[...] * live_ref[...]
 
 
 def setup_kernel(turn_ref, counts, occ, vir, occ_ref, vir_ref, pair_in, pair_ref, den_ref, live_ref):
@@ -464,15 +484,34 @@
     far_send = closing(ids, *parts[:2], far_send)
     far_recv = swap_pair(far_send)
     far_keep = closing(after(ids, far_send), *parts[2:], far_keep)
-    sends = add_blocks(far_keep, far_recv, owners - 1)
-    terms = [cycle, own_keep, own_recv, *exchange(sends)]
     lines = sections // 2
-    pieces = small(functools.partial(line_kernel, len(terms)), [sds(owner_rows, LANES)] * lines, terms)
-    recvs = [
-        lax.ppermute(pieces[q], "sec", [(s, s ^ (2 * q)) for s in range(sections)]) for q in reversed(range(1, lines))
-    ]
-
-    operands = [pieces[0], *recvs, pair, denominator, live_out]
+    n = owners - 1
+    sends = small(
+        functools.partial(pair_pieces_kernel, n), [sds(owner_rows, lines // 2 * LANES)] * (2 * n), [far_keep, far_recv]
+    )
+    far_terms = exchange(sends[:n])
+    near_terms = exchange(sends[n:])
+    order = list(reversed(range(lines)))
+
+    def line(distances, terms):
+        return small(
+            functools.partial(line_kernel, n, distances),
+            [sds(owner_rows, LANES)] * len(distances),
+            [cycle, own_keep, own_recv, *terms],
+        )
+
+    def along(distances, pieces):
+        return [
+            lax.ppermute(piece, "sec", [(s, s ^ (2 * q)) for s in range(sections)])
+            for q, piece in zip(distances, pieces)
+        ]
+
+    pieces = line(order[: lines // 2], far_terms)
+    recvs = along(order, pieces)
+    *pieces, own_piece = line(order[lines // 2 :], near_terms)
+    recvs += along(order[lines // 2 :], pieces)
+
+    operands = [own_piece, *recvs, pair, denominator, live_out]
     return small(final_kernel, sds(*pair_ints.shape), operands)
 
 

time: 141 us -> 139 us (0.986)
  waiting for transfers between devices: 56 us -> 50 us
  starting transfers between devices: 33.4 us -> 37.3 us
    ppermute x21 -> x24, waiting for transfers between devices: 50.5 us -> 44.5 us  [exchange(): lax.ppermute(values[k - 1], 'occ', [(o, o ^ k) for o in range(owners)])]
    ppermute x21 -> x24, starting transfers between devices: 28.6 us -> 32.2 us  [exchange(): lax.ppermute(values[k - 1], 'occ', [(o, o ^ k) for o in range(owners)])]
  transfers between devices with their start and end apart: 27 -> 30, of which waited for: 9 -> 9; matrix products, arithmetic and copies ran while one was open for 0% -> 0% of each run, Pallas kernels for 31% -> 32%
where the time goes in v4:
time: 139 us; the launch traced here: 138 us
  waiting for transfers between devices  50 us (36%)
  Pallas kernels  49.9 us (36%)
  starting transfers between devices  37.3 us (27%)
    ppermute x24, waiting for transfers between devices, exchange(): lax.ppermute(values[k - 1], 'occ', [(o, o ^ k) for o in range(owners)])  44.5 us
    ppermute x24, starting transfers between devices, exchange(): lax.ppermute(values[k - 1], 'occ', [(o, o ^ k) for o in range(owners)])  32.2 us
    pallas_call x3, Pallas kernels, ladder_product(): pl.pallas_call(functools.partial(ladder_kernel, block0, steps, with_own,...  27.5 us
    pallas_call x1, Pallas kernels, cycle_product(): pl.pallas_call(functools.partial(cycle_kernel, owners, steps), out_shape=...  9.47 us
    pallas_call x4, Pallas kernels, slice_chunk(): pl.pallas_call(functools.partial(slice_kernel, d0), out_shape=[sds(rows,...  5.27 us
    ppermute x3, starting transfers between devices, along(): lax.ppermute(piece, 'sec', [(s, s ^ 2 * q) for s in range(sections)])  4.51 us
    ppermute x3, waiting for transfers between devices, along(): lax.ppermute(piece, 'sec', [(s, s ^ 2 * q) for s in range(sections)])  3.83 us
  transfers between devices with their start and end apart: 30, of which 9 were waited for; matrix products, arithmetic and copies ran while one was open for 0% of the time, Pallas kernels for 32%

profile of v4, /device:TPU:0, one launch (start us, length us, event | category | flops | bytes accessed | tf_op | source)
XLA Modules:
  0.0 138.2 jit_solution(3296082349237196947)
XLA Ops:
  0.0 1.1 slices.4
  1.8 2.1 %cycle_window.1.refs_0_ = f32[24,8,128]{2,1,0:T(8,128)S(1)} custom-call(s32[1]{0:T(128)} %bitcast.turn_ref.turn, s32[4]{0:T(128)S(1)} %copy-done.3, f32[48,64,512]{2,1,0:T(8,128)} %bitcast.7), custom_call_target="tpu_custom_call" | custom-call | bytes 1572864 | tf_op jit(solution)/shard_map/cycle_window/pallas_call | solution.py:124
  3.9 1.7 %slices.5 = (f32[48,32,128]{2,1,0:T(8,128)S(1)}, f32[48,32,128]{2,1,0:T(8,128)S(1)}, f32[48,32,128]{2,1,0:T(8,128)S(1)}) custom-call(s32[1]{0:T(128)} %bitcast.turn_ref.turn, f32[48,64,512]{2,1,0:T(8,128)} %bitcast.8), custom_call_target="tpu_custom_call" | custom-call | bytes 4718592 | tf_op jit(solution)/shard_map/slices/pallas_call | solution.py:89
  5.6 3.0 %collective-permute-start.10 = (f32[48,32,128]{2,1,0:T(8,128)S(1)}, f32[48,32,128]{2,1,0:T(8,128)S(1)}, u32[]{:S(2)}, u32[]{:S(2)}) collective-permute-start(f32[48,32,128]{2,1,0:T(8,128)S(1)} %get-tuple-element.66), channel_id=1, source_target_pairs={{0,8},{8,0},{16,24},{24,16},{1,9},{9,1},{17,25},{25,17},{2,10},{10... | collective-permute-start | bytes 2359304 | tf_op jit(solution)/shard_map/ppermute | solution.py:447
  8.7 1.5 %collective-permute-start.11 = (f32[48,32,128]{2,1,0:T(8,128)S(1)}, f32[48,32,128]{2,1,0:T(8,128)S(1)}, u32[]{:S(2)}, u32[]{:S(2)}) collective-permute-start(f32[48,32,128]{2,1,0:T(8,128)S(1)} %get-tuple-element.67), channel_id=1, source_target_pairs={{0,16},{8,24},{16,0},{24,8},{1,17},{9,25},{17,1},{25,9},{2,18},{10... | collective-permute-start | bytes 2359304 | tf_op jit(solution)/shard_map/ppermute | solution.py:447
  10.2 1.9 %collective-permute-start = (f32[24,8,128]{2,1,0:T(8,128)S(1)}, f32[24,8,128]{2,1,0:T(8,128)S(1)}, u32[]{:S(2)}, u32[]{:S(2)}) collective-permute-start(f32[24,8,128]{2,1,0:T(8,128)S(1)} %cycle_window.1.refs_0_), channel_id=1, source_target_pairs={{0,8},{8,0},{16,24},{24,16},{1,9},{9,1},{17,25},{25,17},{2,10},{10... | collective-permute-start | bytes 294920 | tf_op jit(solution)/shard_map/ppermute | solution.py:447
  12.2 1.5 %collective-permute-start.1 = (f32[24,8,128]{2,1,0:T(8,128)S(1)}, f32[24,8,128]{2,1,0:T(8,128)S(1)}, u32[]{:S(2)}, u32[]{:S(2)}) collective-permute-start(f32[24,8,128]{2,1,0:T(8,128)S(1)} %cycle_window.1.refs_0_), channel_id=1, source_target_pairs={{0,16},{8,24},{16,0},{24,8},{1,17},{9,25},{17,1},{25,9},{2,18},{10... | collective-permute-start | bytes 294920 | tf_op jit(solution)/shard_map/ppermute | solution.py:447
  13.7 31.5 %collective-permute-done.refs_1_ = f32[24,8,128]{2,1,0:T(8,128)S(1)} collective-permute-done((f32[24,8,128]{2,1,0:T(8,128)S(1)}, f32[24,8,128]{2,1,0:T(8,128)S(1)}, u32[]{:S(2)}, u32[]{:S(2)}) %collective-permute-start) | collective-permute-done | bytes 98336 | tf_op jit(solution)/shard_map/ppermute | solution.py:447
  45.2 2.7 %collective-permute-start.2 = (f32[24,8,128]{2,1,0:T(8,128)S(1)}, f32[24,8,128]{2,1,0:T(8,128)S(1)}, u32[]{:S(2)}, u32[]{:S(2)}) collective-permute-start(f32[24,8,128]{2,1,0:T(8,128)S(1)} %cycle_window.1.refs_0_), channel_id=1, source_target_pairs={{0,24},{8,16},{16,8},{24,0},{1,25},{9,17},{17,9},{25,1},{2,26},{10... | collective-permute-start | bytes 294920 | tf_op jit(solution)/shard_map/ppermute | solution.py:447
  48.5 3.3 %collective-permute-done.2.refs_3_ = f32[24,8,128]{2,1,0:T(8,128)S(1)} collective-permute-done((f32[24,8,128]{2,1,0:T(8,128)S(1)}, f32[24,8,128]{2,1,0:T(8,128)S(1)}, u32[]{:S(2)}, u32[]{:S(2)}) %collective-permute-start.2) | collective-permute-done | bytes 98336 | tf_op jit(solution)/shard_map/ppermute | solution.py:447
  51.8 1.8 %collective-permute-start.8 = (f32[48,8,128]{2,1,0:T(8,128)S(1)}, f32[48,8,128]{2,1,0:T(8,128)S(1)}, u32[]{:S(2)}, u32[]{:S(2)}) collective-permute-start(f32[48,8,128]{2,1,0:T(8,128)S(1)} %get-tuple-element.63), channel_id=1, source_target_pairs={{0,16},{8,24},{16,0},{24,8},{1,17},{9,25},{17,1},{25,9},{2,18},{10... | collective-permute-start | bytes 589832 | tf_op jit(solution)/shard_map/ppermute | solution.py:447
  53.6 1.3 slices.6
  54.9 1.6 %collective-permute-start.17 = (f32[48,16,128]{2,1,0:T(8,128)S(1)}, f32[48,16,128]{2,1,0:T(8,128)S(1)}, u32[]{:S(2)}, u32[]{:S(2)}) collective-permute-start(f32[48,16,128]{2,1,0:T(8,128)S(1)} %get-tuple-element.77), channel_id=1, source_target_pairs={{0,8},{8,0},{16,24},{24,16},{1,9},{9,1},{17,25},{25,17},{2,10},{10... | collective-permute-start | bytes 1179656 | tf_op jit(solution)/shard_map/ppermute | solution.py:447
  56.4 9.5 %cycle_product.1 = (f32[64,512]{1,0:T(8,128)S(1)}, f32[64,512]{1,0:T(8,128)S(1)}) custom-call(f32[24,8,128]{2,1,0:T(8,128)S(1)} %cycle_window.1.refs_0_, f32[24,8,128]{2,1,0:T(8,128)S(1)} %collective-permute-done.refs_1_, f32[24,8,128]{2,1,0:T(8,128)S(1)} %collective-permute-done.1.refs_2_, f32[24,8,128]{2,1,0:T(8,128)S(1)} %collective-permute-done.2.refs_3_, ...), custom_call_target="tpu_custom_call" | custom-call | flops 905969664 | bytes 18874368 | tf_op jit(solution)/shard_map/cycle_product/pallas_call | solution.py:331
  66.0 1.3 collective-permute-done.3.recv_ref
  68.8 2.5 %fetch_integrals.1 = (bf16[8,128,512]{2,1,0:T(8,128)(2,1)S(1)}, bf16[8,128,512]{2,1,0:T(8,128)(2,1)S(1)}, bf16[8,128,512]{2,1,0:T(8,128)(2,1)S(1)}, bf16[8,128,512]{2,1,0:T(8,128)(2,1)S(1)}) custom-call(s32[1]{0:T(128)} %bitcast.turn_ref.turn, f32[128,64,1024]{2,1,0:T(8,128)} %refs_3_.1), custom_call_target="tpu_custom_call" | custom-call | bytes 8388608 | tf_op jit(solution)/shard_map/fetch_integrals/pallas_call | solution.py:277
  72.0 7.9 %ladder_product.3.refs_8_ = f32[48,1024]{1,0:T(8,128)S(1)} custom-call(s32[1]{0:T(128)} %bitcast.turn_ref.turn, f32[48,64,512]{2,1,0:T(8,128)} %bitcast.11, f32[128,64,1024]{2,1,0:T(8,128)} %refs_3_.1), custom_call_target="tpu_custom_call" | custom-call | flops 905969664 | bytes 12582912 | tf_op jit(solution)/shard_map/ladder_product/pallas_call | solution.py:228
  79.9 1.8 %collective-permute-start.14 = (f32[48,8,128]{2,1,0:T(8,128)S(1)}, f32[48,8,128]{2,1,0:T(8,128)S(1)}, u32[]{:S(2)}, u32[]{:S(2)}) collective-permute-start(f32[48,8,128]{2,1,0:T(8,128)S(1)} %get-tuple-element.79), channel_id=1, source_target_pairs={{0,8},{8,0},{16,24},{24,16},{1,9},{9,1},{17,25},{25,17},{2,10},{10... | collective-permute-start | bytes 589832 | tf_op jit(solution)/shard_map/ppermute | solution.py:447
  81.7 1.5 %collective-permute-start.15 = (f32[48,8,128]{2,1,0:T(8,128)S(1)}, f32[48,8,128]{2,1,0:T(8,128)S(1)}, u32[]{:S(2)}, u32[]{:S(2)}) collective-permute-start(f32[48,8,128]{2,1,0:T(8,128)S(1)} %get-tuple-element.80), channel_id=1, source_target_pairs={{0,16},{8,24},{16,0},{24,8},{1,17},{9,25},{17,1},{25,9},{2,18},{10... | collective-permute-start | bytes 589832 | tf_op jit(solution)/shard_map/ppermute | solution.py:447
  83.4 1.8 %collective-permute-start.18 = (f32[48,16,128]{2,1,0:T(8,128)S(1)}, f32[48,16,128]{2,1,0:T(8,128)S(1)}, u32[]{:S(2)}, u32[]{:S(2)}) collective-permute-start(f32[48,16,128]{2,1,0:T(8,128)S(1)} %get-tuple-element.83), channel_id=1, source_target_pairs={{0,16},{8,24},{16,0},{24,8},{1,17},{9,25},{17,1},{25,9},{2,18},{10... | collective-permute-start | bytes 1179656 | tf_op jit(solution)/shard_map/ppermute | solution.py:447
  85.2 1.4 %collective-permute-start.19 = (f32[48,16,128]{2,1,0:T(8,128)S(1)}, f32[48,16,128]{2,1,0:T(8,128)S(1)}, u32[]{:S(2)}, u32[]{:S(2)}) collective-permute-start(f32[48,16,128]{2,1,0:T(8,128)S(1)} %get-tuple-element.84), channel_id=1, source_target_pairs={{0,24},{8,16},{16,8},{24,0},{1,25},{9,17},{17,9},{25,1},{2,26},{10... | collective-permute-start | bytes 1179656 | tf_op jit(solution)/shard_map/ppermute | solution.py:447
  86.6 14.3 %ladder_product.4 = (f32[48,512]{1,0:T(8,128)S(1)}, f32[48,512]{1,0:T(8,128)S(1)}, f32[144,1024]{1,0:T(8,128)S(1)}) custom-call(s32[1]{0:T(128)} %bitcast.turn_ref.turn, f32[48,64,512]{2,1,0:T(8,128)} %bitcast.12, f32[48,8,128]{2,1,0:T(8,128)S(1)} %collective-permute-done.7.refs_1_, f32[48,8,128]{2,1,0:T(8,128)S(1)} %collective-permute-done.8.refs_2_, ...), custom_call_target="tpu_custom_call" | custom-call | flops 6039797760 | bytes 20971520 | tf_op jit(solution)/shard_map/ladder_product/pallas_call | solution.py:228
  100.9 8.2 %collective-permute-done.18.refs_1_ = f32[48,16,128]{2,1,0:T(8,128)S(1)} collective-permute-done((f32[48,16,128]{2,1,0:T(8,128)S(1)}, f32[48,16,128]{2,1,0:T(8,128)S(1)}, u32[]{:S(2)}, u32[]{:S(2)}) %collective-permute-start.18) | collective-permute-done | bytes 393248 | tf_op jit(solution)/shard_map/ppermute | solution.py:447
  109.1 5.4 %ladder_product.5 = (f32[144,512]{1,0:T(8,128)S(1)}, f32[144,512]{1,0:T(8,128)S(1)}) custom-call(s32[1]{0:T(128)} %bitcast.turn_ref.turn, f32[48,16,128]{2,1,0:T(8,128)S(1)} %collective-permute-done.17.refs_0_, f32[48,16,128]{2,1,0:T(8,128)S(1)} %collective-permute-done.18.refs_1_, f32[48,16,128]{2,1,0:T(8,128)S(1)} %collective-permute-done.19.refs_2_, ...), custom_call_target="tpu_custom_call" | custom-call | flops 1811939328 | bytes 8388608 | tf_op jit(solution)/shard_map/ladder_product/pallas_call | solution.py:228
  117.5 1.7 %collective-permute-start.4 = (f32[16,512]{1,0:T(8,128)S(1)}, f32[16,512]{1,0:T(8,128)S(1)}, u32[]{:S(2)}, u32[]{:S(2)}) collective-permute-start(f32[16,512]{1,0:T(8,128)S(1)} %get-tuple-element.60), channel_id=1, source_target_pairs={{0,8},{8,0},{16,24},{24,16},{1,9},{9,1},{17,25},{25,17},{2,10},{10... | collective-permute-start | bytes 98312 | tf_op jit(solution)/shard_map/ppermute | solution.py:447
  119.1 1.5 %collective-permute-start.5 = (f32[16,512]{1,0:T(8,128)S(1)}, f32[16,512]{1,0:T(8,128)S(1)}, u32[]{:S(2)}, u32[]{:S(2)}) collective-permute-start(f32[16,512]{1,0:T(8,128)S(1)} %get-tuple-element.61), channel_id=1, source_target_pairs={{0,16},{8,24},{16,0},{24,8},{1,17},{9,25},{17,1},{25,9},{2,18},{10... | collective-permute-start | bytes 98312 | tf_op jit(solution)/shard_map/ppermute | solution.py:447
  121.6 1.5 %collective-permute-start.25 = (f32[48,256]{1,0:T(8,128)S(1)}, f32[48,256]{1,0:T(8,128)S(1)}, u32[]{:S(2)}, u32[]{:S(2)}) collective-permute-start(f32[48,256]{1,0:T(8,128)S(1)} %get-tuple-element.96), channel_id=1, source_target_pairs={{0,16},{8,24},{16,0},{24,8},{1,17},{9,25},{17,1},{25,9},{2,18},{10... | collective-permute-start | bytes 147464 | tf_op jit(solution)/shard_map/ppermute | solution.py:447
  123.1 1.6 %collective-permute-start.26 = (f32[48,256]{1,0:T(8,128)S(1)}, f32[48,256]{1,0:T(8,128)S(1)}, u32[]{:S(2)}, u32[]{:S(2)}) collective-permute-start(f32[48,256]{1,0:T(8,128)S(1)} %get-tuple-element.97), channel_id=1, source_target_pairs={{0,24},{8,16},{16,8},{24,0},{1,25},{9,17},{17,9},{25,1},{2,26},{10... | collective-permute-start | bytes 147464 | tf_op jit(solution)/shard_map/ppermute | solution.py:447
  126.6 2.4 %collective-permute-start.23 = (f32[48,256]{1,0:T(8,128)S(1)}, f32[48,256]{1,0:T(8,128)S(1)}, u32[]{:S(2)}, u32[]{:S(2)}) collective-permute-start(f32[48,256]{1,0:T(8,128)S(1)} %get-tuple-element.93), channel_id=1, source_target_pairs={{0,24},{8,16},{16,8},{24,0},{1,25},{9,17},{17,9},{25,1},{2,26},{10... | collective-permute-start | bytes 147464 | tf_op jit(solution)/shard_map/ppermute | solution.py:447
  129.2 3.7 %collective-permute-start.27 = (f32[48,128]{1,0:T(8,128)S(1)}, f32[48,128]{1,0:T(8,128)S(1)}, u32[]{:S(2)}, u32[]{:S(2)}) collective-permute-start(f32[48,128]{1,0:T(8,128)S(1)} %get-tuple-element.98), channel_id=1, source_target_pairs={{0,6},{1,7},{2,4},{3,5},{4,2},{5,3},{6,0},{7,1},{8,14},{9,15},{10,... | collective-permute-start | bytes 73736 | tf_op jit(solution)/shard_map/ppermute | solution.py:505
  133.7 1.3 collective-permute-done.27.refs_1_
  135.0 2.5 %collective-permute-done.28.refs_2_ = f32[48,128]{1,0:T(8,128)S(1)} collective-permute-done((f32[48,128]{1,0:T(8,128)S(1)}, f32[48,128]{1,0:T(8,128)S(1)}, u32[]{:S(2)}, u32[]{:S(2)}) %collective-permute-start.28) | collective-permute-done | bytes 24608 | tf_op jit(solution)/shard_map/ppermute | solution.py:505
  (57 shorter events, 11.0 us)
Async XLA Ops:
  5.6 77.6 %collective-permute-start.10 = (f32[48,32,128]{2,1,0:T(8,128)S(1)}, f32[48,32,128]{2,1,0:T(8,128)S(1)}, u32[]{:S(2)}, u32[]{:S(2)}) collective-permute-start(f32[48,32,128]{2,1,0:T(8,128)S(1)} %get-tuple-element.66), channel_id=1, source_target_pairs={{0,8},{8,0},{16,24},{24,16},{1,9},{9,1},{17,25},{25,17},{2,10},{10... | collective-permute-start | bytes 2359304 | tf_op jit(solution)/shard_map/ppermute | solution.py:447
  8.7 74.8 %collective-permute-start.11 = (f32[48,32,128]{2,1,0:T(8,128)S(1)}, f32[48,32,128]{2,1,0:T(8,128)S(1)}, u32[]{:S(2)}, u32[]{:S(2)}) collective-permute-start(f32[48,32,128]{2,1,0:T(8,128)S(1)} %get-tuple-element.67), channel_id=1, source_target_pairs={{0,16},{8,24},{16,0},{24,8},{1,17},{9,25},{17,1},{25,9},{2,18},{10... | collective-permute-start | bytes 2359304 | tf_op jit(solution)/shard_map/ppermute | solution.py:447
  10.2 75.0 %collective-permute-start.12 = (f32[48,32,128]{2,1,0:T(8,128)S(1)}, f32[48,32,128]{2,1,0:T(8,128)S(1)}, u32[]{:S(2)}, u32[]{:S(2)}) collective-permute-start(f32[48,32,128]{2,1,0:T(8,128)S(1)} %get-tuple-element.68), channel_id=1, source_target_pairs={{0,24},{8,16},{16,8},{24,0},{1,25},{9,17},{17,9},{25,1},{2,26},{10... | collective-permute-start | bytes 2359304 | tf_op jit(solution)/shard_map/ppermute | solution.py:447
  10.2 35.0 %collective-permute-start = (f32[24,8,128]{2,1,0:T(8,128)S(1)}, f32[24,8,128]{2,1,0:T(8,128)S(1)}, u32[]{:S(2)}, u32[]{:S(2)}) collective-permute-start(f32[24,8,128]{2,1,0:T(8,128)S(1)} %cycle_window.1.refs_0_), channel_id=1, source_target_pairs={{0,8},{8,0},{16,24},{24,16},{1,9},{9,1},{17,25},{25,17},{2,10},{10... | collective-permute-start | bytes 294920 | tf_op jit(solution)/shard_map/ppermute | solution.py:447
  12.2 35.8 %collective-permute-start.1 = (f32[24,8,128]{2,1,0:T(8,128)S(1)}, f32[24,8,128]{2,1,0:T(8,128)S(1)}, u32[]{:S(2)}, u32[]{:S(2)}) collective-permute-start(f32[24,8,128]{2,1,0:T(8,128)S(1)} %cycle_window.1.refs_0_), channel_id=1, source_target_pairs={{0,16},{8,24},{16,0},{24,8},{1,17},{9,25},{17,1},{25,9},{2,18},{10... | collective-permute-start | bytes 294920 | tf_op jit(solution)/shard_map/ppermute | solution.py:447
  45.2 6.6 %collective-permute-start.2 = (f32[24,8,128]{2,1,0:T(8,128)S(1)}, f32[24,8,128]{2,1,0:T(8,128)S(1)}, u32[]{:S(2)}, u32[]{:S(2)}) collective-permute-start(f32[24,8,128]{2,1,0:T(8,128)S(1)} %cycle_window.1.refs_0_), channel_id=1, source_target_pairs={{0,24},{8,16},{16,8},{24,0},{1,25},{9,17},{17,9},{25,1},{2,26},{10... | collective-permute-start | bytes 294920 | tf_op jit(solution)/shard_map/ppermute | solution.py:447
  47.9 6.9 %collective-permute-start.7 = (f32[48,8,128]{2,1,0:T(8,128)S(1)}, f32[48,8,128]{2,1,0:T(8,128)S(1)}, u32[]{:S(2)}, u32[]{:S(2)}) collective-permute-start(f32[48,8,128]{2,1,0:T(8,128)S(1)} %get-tuple-element.55), channel_id=1, source_target_pairs={{0,8},{8,0},{16,24},{24,16},{1,9},{9,1},{17,25},{25,17},{2,10},{10... | collective-permute-start | bytes 589832 | tf_op jit(solution)/shard_map/ppermute | solution.py:447
  51.8 14.1 %collective-permute-start.8 = (f32[48,8,128]{2,1,0:T(8,128)S(1)}, f32[48,8,128]{2,1,0:T(8,128)S(1)}, u32[]{:S(2)}, u32[]{:S(2)}) collective-permute-start(f32[48,8,128]{2,1,0:T(8,128)S(1)} %get-tuple-element.63), channel_id=1, source_target_pairs={{0,16},{8,24},{16,0},{24,8},{1,17},{9,25},{17,1},{25,9},{2,18},{10... | collective-permute-start | bytes 589832 | tf_op jit(solution)/shard_map/ppermute | solution.py:447
  54.9 26.8 %collective-permute-start.17 = (f32[48,16,128]{2,1,0:T(8,128)S(1)}, f32[48,16,128]{2,1,0:T(8,128)S(1)}, u32[]{:S(2)}, u32[]{:S(2)}) collective-permute-start(f32[48,16,128]{2,1,0:T(8,128)S(1)} %get-tuple-element.77), channel_id=1, source_target_pairs={{0,8},{8,0},{16,24},{24,16},{1,9},{9,1},{17,25},{25,17},{2,10},{10... | collective-permute-start | bytes 1179656 | tf_op jit(solution)/shard_map/ppermute | solution.py:447
  65.9 1.4 %collective-permute-start.3 = (f32[64,512]{1,0:T(8,128)S(1)}, f32[64,512]{1,0:T(8,128)S(1)}, u32[]{:S(2)}, u32[]{:S(2)}) collective-permute-start(f32[64,512]{1,0:T(8,128)S(1)} %get-tuple-element.58), channel_id=1, source_target_pairs={{0,1},{1,0},{2,3},{3,2},{4,5},{5,4},{6,7},{7,6},{8,9},{9,8},{10,11... | collective-permute-start | bytes 393224 | tf_op jit(solution)/shard_map/ppermute | solution.py:451
  67.3 4.0 %copy-start.2 = (f32[48]{0:T(128)S(1)}, f32[48]{0:T(128)}, u32[]{:S(2)}) copy-start(f32[48]{0:T(128)} %occ.1) | copy-start | bytes 580
  67.3 4.0 %copy-start.4 = (s32[4]{0:T(128)S(1)}, s32[4]{0:T(128)}, u32[]{:S(2)}) copy-start(s32[4]{0:T(128)} %counts.3) | copy-start | bytes 52
  67.3 12.5 %collective-permute-start.9 = (f32[48,8,128]{2,1,0:T(8,128)S(1)}, f32[48,8,128]{2,1,0:T(8,128)S(1)}, u32[]{:S(2)}, u32[]{:S(2)}) collective-permute-start(f32[48,8,128]{2,1,0:T(8,128)S(1)} %get-tuple-element.64), channel_id=1, source_target_pairs={{0,24},{8,16},{16,8},{24,0},{1,25},{9,17},{17,9},{25,1},{2,26},{10... | collective-permute-start | bytes 589832 | tf_op jit(solution)/shard_map/ppermute | solution.py:447
  79.9 34.7 %collective-permute-start.14 = (f32[48,8,128]{2,1,0:T(8,128)S(1)}, f32[48,8,128]{2,1,0:T(8,128)S(1)}, u32[]{:S(2)}, u32[]{:S(2)}) collective-permute-start(f32[48,8,128]{2,1,0:T(8,128)S(1)} %get-tuple-element.79), channel_id=1, source_target_pairs={{0,8},{8,0},{16,24},{24,16},{1,9},{9,1},{17,25},{25,17},{2,10},{10... | collective-permute-start | bytes 589832 | tf_op jit(solution)/shard_map/ppermute | solution.py:447
  81.7 32.9 %collective-permute-start.15 = (f32[48,8,128]{2,1,0:T(8,128)S(1)}, f32[48,8,128]{2,1,0:T(8,128)S(1)}, u32[]{:S(2)}, u32[]{:S(2)}) collective-permute-start(f32[48,8,128]{2,1,0:T(8,128)S(1)} %get-tuple-element.80), channel_id=1, source_target_pairs={{0,16},{8,24},{16,0},{24,8},{1,17},{9,25},{17,1},{25,9},{2,18},{10... | collective-permute-start | bytes 589832 | tf_op jit(solution)/shard_map/ppermute | solution.py:447
  83.2 31.4 %collective-permute-start.16 = (f32[48,8,128]{2,1,0:T(8,128)S(1)}, f32[48,8,128]{2,1,0:T(8,128)S(1)}, u32[]{:S(2)}, u32[]{:S(2)}) collective-permute-start(f32[48,8,128]{2,1,0:T(8,128)S(1)} %get-tuple-element.81), channel_id=1, source_target_pairs={{0,24},{8,16},{16,8},{24,0},{1,25},{9,17},{17,9},{25,1},{2,26},{10... | collective-permute-start | bytes 589832 | tf_op jit(solution)/shard_map/ppermute | solution.py:447
  83.4 25.7 %collective-permute-start.18 = (f32[48,16,128]{2,1,0:T(8,128)S(1)}, f32[48,16,128]{2,1,0:T(8,128)S(1)}, u32[]{:S(2)}, u32[]{:S(2)}) collective-permute-start(f32[48,16,128]{2,1,0:T(8,128)S(1)} %get-tuple-element.83), channel_id=1, source_target_pairs={{0,16},{8,24},{16,0},{24,8},{1,17},{9,25},{17,1},{25,9},{2,18},{10... | collective-permute-start | bytes 1179656 | tf_op jit(solution)/shard_map/ppermute | solution.py:447
  85.2 23.9 %collective-permute-start.19 = (f32[48,16,128]{2,1,0:T(8,128)S(1)}, f32[48,16,128]{2,1,0:T(8,128)S(1)}, u32[]{:S(2)}, u32[]{:S(2)}) collective-permute-start(f32[48,16,128]{2,1,0:T(8,128)S(1)} %get-tuple-element.84), channel_id=1, source_target_pairs={{0,24},{8,16},{16,8},{24,0},{1,25},{9,17},{17,9},{25,1},{2,26},{10... | collective-permute-start | bytes 1179656 | tf_op jit(solution)/shard_map/ppermute | solution.py:447
  115.3 1.6 %collective-permute-start.20 = (f32[144,512]{1,0:T(8,128)S(1)}, f32[144,512]{1,0:T(8,128)S(1)}, u32[]{:S(2)}, u32[]{:S(2)}) collective-permute-start(f32[144,512]{1,0:T(8,128)S(1)} %shard_map.75), channel_id=1, source_target_pairs={{0,1},{1,0},{2,3},{3,2},{4,5},{5,4},{6,7},{7,6},{8,9},{9,8},{10,11... | collective-permute-start | bytes 884744 | tf_op jit(solution)/shard_map/ppermute | solution.py:451
  115.4 10.7 %collective-permute-start.13 = (f32[48,512]{1,0:T(8,128)S(1)}, f32[48,512]{1,0:T(8,128)S(1)}, u32[]{:S(2)}, u32[]{:S(2)}) collective-permute-start(f32[48,512]{1,0:T(8,128)S(1)} %get-tuple-element.75), channel_id=1, source_target_pairs={{0,1},{1,0},{2,3},{3,2},{4,5},{5,4},{6,7},{7,6},{8,9},{9,8},{10,11... | collective-permute-start | bytes 294920 | tf_op jit(solution)/shard_map/ppermute | solution.py:451
  117.1 9.6 %collective-permute-start.24 = (f32[48,256]{1,0:T(8,128)S(1)}, f32[48,256]{1,0:T(8,128)S(1)}, u32[]{:S(2)}, u32[]{:S(2)}) collective-permute-start(f32[48,256]{1,0:T(8,128)S(1)} %get-tuple-element.95), channel_id=1, source_target_pairs={{0,8},{8,0},{16,24},{24,16},{1,9},{9,1},{17,25},{25,17},{2,10},{10... | collective-permute-start | bytes 147464 | tf_op jit(solution)/shard_map/ppermute | solution.py:447
  117.5 4.1 %collective-permute-start.4 = (f32[16,512]{1,0:T(8,128)S(1)}, f32[16,512]{1,0:T(8,128)S(1)}, u32[]{:S(2)}, u32[]{:S(2)}) collective-permute-start(f32[16,512]{1,0:T(8,128)S(1)} %get-tuple-element.60), channel_id=1, source_target_pairs={{0,8},{8,0},{16,24},{24,16},{1,9},{9,1},{17,25},{25,17},{2,10},{10... | collective-permute-start | bytes 98312 | tf_op jit(solution)/shard_map/ppermute | solution.py:447
  119.1 4.0 %collective-permute-start.5 = (f32[16,512]{1,0:T(8,128)S(1)}, f32[16,512]{1,0:T(8,128)S(1)}, u32[]{:S(2)}, u32[]{:S(2)}) collective-permute-start(f32[16,512]{1,0:T(8,128)S(1)} %get-tuple-element.61), channel_id=1, source_target_pairs={{0,16},{8,24},{16,0},{24,8},{1,17},{9,25},{17,1},{25,9},{2,18},{10... | collective-permute-start | bytes 98312 | tf_op jit(solution)/shard_map/ppermute | solution.py:447
  120.7 4.8 %collective-permute-start.6 = (f32[16,512]{1,0:T(8,128)S(1)}, f32[16,512]{1,0:T(8,128)S(1)}, u32[]{:S(2)}, u32[]{:S(2)}) collective-permute-start(f32[16,512]{1,0:T(8,128)S(1)} %get-tuple-element.62), channel_id=1, source_target_pairs={{0,24},{8,16},{16,8},{24,0},{1,25},{9,17},{17,9},{25,1},{2,26},{10... | collective-permute-start | bytes 98312 | tf_op jit(solution)/shard_map/ppermute | solution.py:447
  121.6 7.5 %collective-permute-start.25 = (f32[48,256]{1,0:T(8,128)S(1)}, f32[48,256]{1,0:T(8,128)S(1)}, u32[]{:S(2)}, u32[]{:S(2)}) collective-permute-start(f32[48,256]{1,0:T(8,128)S(1)} %get-tuple-element.96), channel_id=1, source_target_pairs={{0,16},{8,24},{16,0},{24,8},{1,17},{9,25},{17,1},{25,9},{2,18},{10... | collective-permute-start | bytes 147464 | tf_op jit(solution)/shard_map/ppermute | solution.py:447
  123.1 6.0 %collective-permute-start.26 = (f32[48,256]{1,0:T(8,128)S(1)}, f32[48,256]{1,0:T(8,128)S(1)}, u32[]{:S(2)}, u32[]{:S(2)}) collective-permute-start(f32[48,256]{1,0:T(8,128)S(1)} %get-tuple-element.97), channel_id=1, source_target_pairs={{0,24},{8,16},{16,8},{24,0},{1,25},{9,17},{17,9},{25,1},{2,26},{10... | collective-permute-start | bytes 147464 | tf_op jit(solution)/shard_map/ppermute | solution.py:447
  125.5 7.3 %collective-permute-start.21 = (f32[48,256]{1,0:T(8,128)S(1)}, f32[48,256]{1,0:T(8,128)S(1)}, u32[]{:S(2)}, u32[]{:S(2)}) collective-permute-start(f32[48,256]{1,0:T(8,128)S(1)} %get-tuple-element.91), channel_id=1, source_target_pairs={{0,8},{8,0},{16,24},{24,16},{1,9},{9,1},{17,25},{25,17},{2,10},{10... | collective-permute-start | bytes 147464 | tf_op jit(solution)/shard_map/ppermute | solution.py:447
  126.1 6.7 %collective-permute-start.22 = (f32[48,256]{1,0:T(8,128)S(1)}, f32[48,256]{1,0:T(8,128)S(1)}, u32[]{:S(2)}, u32[]{:S(2)}) collective-permute-start(f32[48,256]{1,0:T(8,128)S(1)} %get-tuple-element.92), channel_id=1, source_target_pairs={{0,16},{8,24},{16,0},{24,8},{1,17},{9,25},{17,1},{25,9},{2,18},{10... | collective-permute-start | bytes 147464 | tf_op jit(solution)/shard_map/ppermute | solution.py:447
  126.6 6.2 %collective-permute-start.23 = (f32[48,256]{1,0:T(8,128)S(1)}, f32[48,256]{1,0:T(8,128)S(1)}, u32[]{:S(2)}, u32[]{:S(2)}) collective-permute-start(f32[48,256]{1,0:T(8,128)S(1)} %get-tuple-element.93), channel_id=1, source_target_pairs={{0,24},{8,16},{16,8},{24,0},{1,25},{9,17},{17,9},{25,1},{2,26},{10... | collective-permute-start | bytes 147464 | tf_op jit(solution)/shard_map/ppermute | solution.py:447
  129.2 5.9 %collective-permute-start.27 = (f32[48,128]{1,0:T(8,128)S(1)}, f32[48,128]{1,0:T(8,128)S(1)}, u32[]{:S(2)}, u32[]{:S(2)}) collective-permute-start(f32[48,128]{1,0:T(8,128)S(1)} %get-tuple-element.98), channel_id=1, source_target_pairs={{0,6},{1,7},{2,4},{3,5},{4,2},{5,3},{6,0},{7,1},{8,14},{9,15},{10,... | collective-permute-start | bytes 73736 | tf_op jit(solution)/shard_map/ppermute | solution.py:505
  132.8 4.7 %collective-permute-start.28 = (f32[48,128]{1,0:T(8,128)S(1)}, f32[48,128]{1,0:T(8,128)S(1)}, u32[]{:S(2)}, u32[]{:S(2)}) collective-permute-start(f32[48,128]{1,0:T(8,128)S(1)} %get-tuple-element.99), channel_id=1, source_target_pairs={{0,4},{1,5},{2,6},{3,7},{4,0},{5,1},{6,2},{7,3},{8,12},{9,13},{10,... | collective-permute-start | bytes 73736 | tf_op jit(solution)/shard_map/ppermute | solution.py:505
  132.9 4.7 %collective-permute-start.29 = (f32[48,128]{1,0:T(8,128)S(1)}, f32[48,128]{1,0:T(8,128)S(1)}, u32[]{:S(2)}, u32[]{:S(2)}) collective-permute-start(f32[48,128]{1,0:T(8,128)S(1)} %get-tuple-element.100), channel_id=1, source_target_pairs={{0,2},{1,3},{2,0},{3,1},{4,6},{5,7},{6,4},{7,5},{8,10},{9,11},{10,... | collective-permute-start | bytes 73736 | tf_op jit(solution)/shard_map/ppermute | solution.py:505
  (3 other events, 8.6 us)

commit v5 on v4

--- a/solution.py
+++ b/solution.py
@@ -371,13 +371,13 @@
 def pair_pieces_kernel(n, keep_ref, recv_ref, *outs):
     z = lax.axis_index("sec") // 2
     rows = outs[0].shape[0]
-    per_half = outs[0].shape[1] // LANES
-    for h in range(2):
-        for k in range(n):
-            part = slice(k * rows, (k + 1) * rows)
-            for t in range(per_half):
-                cols = block_of(z ^ (2 * per_half - 1 - h * per_half - t))
-                outs[h * n + k][:, t * LANES : (t + 1) * LANES] = keep_ref[part, cols] + recv_ref[part, cols]
+    others = outs[0].shape[1] // LANES
+    for k in range(n):
+        part = slice(k * rows, (k + 1) * rows)
+        for t in range(others + 1):
+            cols = block_of(z ^ (others - t))
+            out, tile = (outs[k], t) if t < others else (outs[n + k], 0)
+            out[:, tile * LANES : (tile + 1) * LANES] = keep_ref[part, cols] + recv_ref[part, cols]
 
 
 def line_kernel(n, lines, cycle_ref, keep_ref, recv_ref, *refs):
@@ -487,7 +487,9 @@
     lines = sections // 2
     n = owners - 1
     sends = small(
-        functools.partial(pair_pieces_kernel, n), [sds(owner_rows, lines // 2 * LANES)] * (2 * n), [far_keep, far_recv]
+        functools.partial(pair_pieces_kernel, n),
+        [sds(owner_rows, (lines - 1) * LANES)] * n + [sds(owner_rows, LANES)] * n,
+        [far_keep, far_recv],
     )
     far_terms = exchange(sends[:n])
     near_terms = exchange(sends[n:])
@@ -506,10 +508,9 @@
             for q, piece in zip(distances, pieces)
         ]
 
-    pieces = line(order[: lines // 2], far_terms)
-    recvs = along(order, pieces)
-    *pieces, own_piece = line(order[lines // 2 :], near_terms)
-    recvs += along(order[lines // 2 :], pieces)
+    pieces = line(order[:-1], far_terms)
+    recvs = along(order[:-1], pieces)
+    (own_piece,) = line(order[-1:], near_terms)
 
     operands = [own_piece, *recvs, pair, denominator, live_out]
     return small(final_kernel, sds(*pair_ints.shape), operands)

time: 139 us -> 140 us (level)
  waiting for transfers between devices: 50 us -> 51.7 us
    ppermute x24, waiting for transfers between devices: 44.5 us -> 46.5 us  [exchange(): lax.ppermute(values[k - 1], 'occ', [(o, o ^ k) for o in range(owners)])]
  transfers between devices with their start and end apart: 30 -> 30, of which waited for: 9 -> 7; matrix products, arithmetic and copies ran while one was open for 0% -> 0% of each run, Pallas kernels for 32% -> 31%
where the time goes in v5:
time: 140 us
  waiting for transfers between devices  51.7 us (37%)
  Pallas kernels  49.9 us (36%)
  starting transfers between devices  37.1 us (26%)
    ppermute x24, waiting for transfers between devices, exchange(): lax.ppermute(values[k - 1], 'occ', [(o, o ^ k) for o in range(owners)])  46.5 us
    ppermute x24, starting transfers between devices, exchange(): lax.ppermute(values[k - 1], 'occ', [(o, o ^ k) for o in range(owners)])  32.3 us
    pallas_call x3, Pallas kernels, ladder_product(): pl.pallas_call(functools.partial(ladder_kernel, block0, steps, with_own,...  27.5 us
    pallas_call x1, Pallas kernels, cycle_product(): pl.pallas_call(functools.partial(cycle_kernel, owners, steps), out_shape=...  9.47 us
    pallas_call x4, Pallas kernels, slice_chunk(): pl.pallas_call(functools.partial(slice_kernel, d0), out_shape=[sds(rows,...  5.27 us
    ppermute x3, starting transfers between devices, along(): lax.ppermute(piece, 'sec', [(s, s ^ 2 * q) for s in range(sections)])  4.45 us
    ppermute x3, waiting for transfers between devices, along(): lax.ppermute(piece, 'sec', [(s, s ^ 2 * q) for s in range(sections)])  3.9 us
  transfers between devices with their start and end apart: 30, of which 7 were waited for; matrix products, arithmetic and copies ran while one was open for 0% of the time, Pallas kernels for 31%

profile of v5, /device:TPU:0, one launch (start us, length us, event | category | flops | bytes accessed | tf_op | source)
XLA Modules:
  0.0 139.7 jit_solution(1662575370035809899)
XLA Ops:
  1.8 2.1 %cycle_window.1.refs_0_ = f32[24,8,128]{2,1,0:T(8,128)S(1)} custom-call(s32[1]{0:T(128)} %bitcast.turn_ref.turn, s32[4]{0:T(128)S(1)} %copy-done.3, f32[48,64,512]{2,1,0:T(8,128)} %bitcast.7), custom_call_target="tpu_custom_call" | custom-call | bytes 1572864 | tf_op jit(solution)/shard_map/cycle_window/pallas_call | solution.py:124
  3.9 1.7 %slices.5 = (f32[48,32,128]{2,1,0:T(8,128)S(1)}, f32[48,32,128]{2,1,0:T(8,128)S(1)}, f32[48,32,128]{2,1,0:T(8,128)S(1)}) custom-call(s32[1]{0:T(128)} %bitcast.turn_ref.turn, f32[48,64,512]{2,1,0:T(8,128)} %bitcast.8), custom_call_target="tpu_custom_call" | custom-call | bytes 4718592 | tf_op jit(solution)/shard_map/slices/pallas_call | solution.py:89
  5.6 3.0 %collective-permute-start.10 = (f32[48,32,128]{2,1,0:T(8,128)S(1)}, f32[48,32,128]{2,1,0:T(8,128)S(1)}, u32[]{:S(2)}, u32[]{:S(2)}) collective-permute-start(f32[48,32,128]{2,1,0:T(8,128)S(1)} %get-tuple-element.65), channel_id=1, source_target_pairs={{0,8},{8,0},{16,24},{24,16},{1,9},{9,1},{17,25},{25,17},{2,10},{10... | collective-permute-start | bytes 2359304 | tf_op jit(solution)/shard_map/ppermute | solution.py:447
  8.7 1.5 %collective-permute-start.11 = (f32[48,32,128]{2,1,0:T(8,128)S(1)}, f32[48,32,128]{2,1,0:T(8,128)S(1)}, u32[]{:S(2)}, u32[]{:S(2)}) collective-permute-start(f32[48,32,128]{2,1,0:T(8,128)S(1)} %get-tuple-element.66), channel_id=1, source_target_pairs={{0,16},{8,24},{16,0},{24,8},{1,17},{9,25},{17,1},{25,9},{2,18},{10... | collective-permute-start | bytes 2359304 | tf_op jit(solution)/shard_map/ppermute | solution.py:447
  10.2 1.9 %collective-permute-start = (f32[24,8,128]{2,1,0:T(8,128)S(1)}, f32[24,8,128]{2,1,0:T(8,128)S(1)}, u32[]{:S(2)}, u32[]{:S(2)}) collective-permute-start(f32[24,8,128]{2,1,0:T(8,128)S(1)} %cycle_window.1.refs_0_), channel_id=1, source_target_pairs={{0,8},{8,0},{16,24},{24,16},{1,9},{9,1},{17,25},{25,17},{2,10},{10... | collective-permute-start | bytes 294920 | tf_op jit(solution)/shard_map/ppermute | solution.py:447
  12.2 1.5 %collective-permute-start.1 = (f32[24,8,128]{2,1,0:T(8,128)S(1)}, f32[24,8,128]{2,1,0:T(8,128)S(1)}, u32[]{:S(2)}, u32[]{:S(2)}) collective-permute-start(f32[24,8,128]{2,1,0:T(8,128)S(1)} %cycle_window.1.refs_0_), channel_id=1, source_target_pairs={{0,16},{8,24},{16,0},{24,8},{1,17},{9,25},{17,1},{25,9},{2,18},{10... | collective-permute-start | bytes 294920 | tf_op jit(solution)/shard_map/ppermute | solution.py:447
  13.7 31.5 %collective-permute-done.refs_1_ = f32[24,8,128]{2,1,0:T(8,128)S(1)} collective-permute-done((f32[24,8,128]{2,1,0:T(8,128)S(1)}, f32[24,8,128]{2,1,0:T(8,128)S(1)}, u32[]{:S(2)}, u32[]{:S(2)}) %collective-permute-start) | collective-permute-done | bytes 98336 | tf_op jit(solution)/shard_map/ppermute | solution.py:447
  45.2 2.7 %collective-permute-start.2 = (f32[24,8,128]{2,1,0:T(8,128)S(1)}, f32[24,8,128]{2,1,0:T(8,128)S(1)}, u32[]{:S(2)}, u32[]{:S(2)}) collective-permute-start(f32[24,8,128]{2,1,0:T(8,128)S(1)} %cycle_window.1.refs_0_), channel_id=1, source_target_pairs={{0,24},{8,16},{16,8},{24,0},{1,25},{9,17},{17,9},{25,1},{2,26},{10... | collective-permute-start | bytes 294920 | tf_op jit(solution)/shard_map/ppermute | solution.py:447
  48.5 3.3 %collective-permute-done.2.refs_3_ = f32[24,8,128]{2,1,0:T(8,128)S(1)} collective-permute-done((f32[24,8,128]{2,1,0:T(8,128)S(1)}, f32[24,8,128]{2,1,0:T(8,128)S(1)}, u32[]{:S(2)}, u32[]{:S(2)}) %collective-permute-start.2) | collective-permute-done | bytes 98336 | tf_op jit(solution)/shard_map/ppermute | solution.py:447
  51.8 1.8 %collective-permute-start.8 = (f32[48,8,128]{2,1,0:T(8,128)S(1)}, f32[48,8,128]{2,1,0:T(8,128)S(1)}, u32[]{:S(2)}, u32[]{:S(2)}) collective-permute-start(f32[48,8,128]{2,1,0:T(8,128)S(1)} %get-tuple-element.62), channel_id=1, source_target_pairs={{0,16},{8,24},{16,0},{24,8},{1,17},{9,25},{17,1},{25,9},{2,18},{10... | collective-permute-start | bytes 589832 | tf_op jit(solution)/shard_map/ppermute | solution.py:447
  53.6 1.3 slices.6
  54.9 1.6 %collective-permute-start.17 = (f32[48,16,128]{2,1,0:T(8,128)S(1)}, f32[48,16,128]{2,1,0:T(8,128)S(1)}, u32[]{:S(2)}, u32[]{:S(2)}) collective-permute-start(f32[48,16,128]{2,1,0:T(8,128)S(1)} %get-tuple-element.76), channel_id=1, source_target_pairs={{0,8},{8,0},{16,24},{24,16},{1,9},{9,1},{17,25},{25,17},{2,10},{10... | collective-permute-start | bytes 1179656 | tf_op jit(solution)/shard_map/ppermute | solution.py:447
  56.4 9.5 %cycle_product.1 = (f32[64,512]{1,0:T(8,128)S(1)}, f32[64,512]{1,0:T(8,128)S(1)}) custom-call(f32[24,8,128]{2,1,0:T(8,128)S(1)} %cycle_window.1.refs_0_, f32[24,8,128]{2,1,0:T(8,128)S(1)} %collective-permute-done.refs_1_, f32[24,8,128]{2,1,0:T(8,128)S(1)} %collective-permute-done.1.refs_2_, f32[24,8,128]{2,1,0:T(8,128)S(1)} %collective-permute-done.2.refs_3_, ...), custom_call_target="tpu_custom_call" | custom-call | flops 905969664 | bytes 18874368 | tf_op jit(solution)/shard_map/cycle_product/pallas_call | solution.py:331
  66.0 1.3 collective-permute-done.3.recv_ref
  68.8 2.5 %fetch_integrals.1 = (bf16[8,128,512]{2,1,0:T(8,128)(2,1)S(1)}, bf16[8,128,512]{2,1,0:T(8,128)(2,1)S(1)}, bf16[8,128,512]{2,1,0:T(8,128)(2,1)S(1)}, bf16[8,128,512]{2,1,0:T(8,128)(2,1)S(1)}) custom-call(s32[1]{0:T(128)} %bitcast.turn_ref.turn, f32[128,64,1024]{2,1,0:T(8,128)} %refs_3_.1), custom_call_target="tpu_custom_call" | custom-call | bytes 8388608 | tf_op jit(solution)/shard_map/fetch_integrals/pallas_call | solution.py:277
  72.0 7.9 %ladder_product.3.refs_8_ = f32[48,1024]{1,0:T(8,128)S(1)} custom-call(s32[1]{0:T(128)} %bitcast.turn_ref.turn, f32[48,64,512]{2,1,0:T(8,128)} %bitcast.11, f32[128,64,1024]{2,1,0:T(8,128)} %refs_3_.1), custom_call_target="tpu_custom_call" | custom-call | flops 905969664 | bytes 12582912 | tf_op jit(solution)/shard_map/ladder_product/pallas_call | solution.py:228
  79.9 1.8 %collective-permute-start.14 = (f32[48,8,128]{2,1,0:T(8,128)S(1)}, f32[48,8,128]{2,1,0:T(8,128)S(1)}, u32[]{:S(2)}, u32[]{:S(2)}) collective-permute-start(f32[48,8,128]{2,1,0:T(8,128)S(1)} %get-tuple-element.78), channel_id=1, source_target_pairs={{0,8},{8,0},{16,24},{24,16},{1,9},{9,1},{17,25},{25,17},{2,10},{10... | collective-permute-start | bytes 589832 | tf_op jit(solution)/shard_map/ppermute | solution.py:447
  81.7 1.5 %collective-permute-start.15 = (f32[48,8,128]{2,1,0:T(8,128)S(1)}, f32[48,8,128]{2,1,0:T(8,128)S(1)}, u32[]{:S(2)}, u32[]{:S(2)}) collective-permute-start(f32[48,8,128]{2,1,0:T(8,128)S(1)} %get-tuple-element.79), channel_id=1, source_target_pairs={{0,16},{8,24},{16,0},{24,8},{1,17},{9,25},{17,1},{25,9},{2,18},{10... | collective-permute-start | bytes 589832 | tf_op jit(solution)/shard_map/ppermute | solution.py:447
  83.4 1.8 %collective-permute-start.18 = (f32[48,16,128]{2,1,0:T(8,128)S(1)}, f32[48,16,128]{2,1,0:T(8,128)S(1)}, u32[]{:S(2)}, u32[]{:S(2)}) collective-permute-start(f32[48,16,128]{2,1,0:T(8,128)S(1)} %get-tuple-element.82), channel_id=1, source_target_pairs={{0,16},{8,24},{16,0},{24,8},{1,17},{9,25},{17,1},{25,9},{2,18},{10... | collective-permute-start | bytes 1179656 | tf_op jit(solution)/shard_map/ppermute | solution.py:447
  85.2 1.4 %collective-permute-start.19 = (f32[48,16,128]{2,1,0:T(8,128)S(1)}, f32[48,16,128]{2,1,0:T(8,128)S(1)}, u32[]{:S(2)}, u32[]{:S(2)}) collective-permute-start(f32[48,16,128]{2,1,0:T(8,128)S(1)} %get-tuple-element.83), channel_id=1, source_target_pairs={{0,24},{8,16},{16,8},{24,0},{1,25},{9,17},{17,9},{25,1},{2,26},{10... | collective-permute-start | bytes 1179656 | tf_op jit(solution)/shard_map/ppermute | solution.py:447
  86.6 14.3 %ladder_product.4 = (f32[48,512]{1,0:T(8,128)S(1)}, f32[48,512]{1,0:T(8,128)S(1)}, f32[144,1024]{1,0:T(8,128)S(1)}) custom-call(s32[1]{0:T(128)} %bitcast.turn_ref.turn, f32[48,64,512]{2,1,0:T(8,128)} %bitcast.12, f32[48,8,128]{2,1,0:T(8,128)S(1)} %collective-permute-done.7.refs_1_, f32[48,8,128]{2,1,0:T(8,128)S(1)} %collective-permute-done.8.refs_2_, ...), custom_call_target="tpu_custom_call" | custom-call | flops 6039797760 | bytes 20971520 | tf_op jit(solution)/shard_map/ladder_product/pallas_call | solution.py:228
  100.9 8.2 %collective-permute-done.18.refs_1_ = f32[48,16,128]{2,1,0:T(8,128)S(1)} collective-permute-done((f32[48,16,128]{2,1,0:T(8,128)S(1)}, f32[48,16,128]{2,1,0:T(8,128)S(1)}, u32[]{:S(2)}, u32[]{:S(2)}) %collective-permute-start.18) | collective-permute-done | bytes 393248 | tf_op jit(solution)/shard_map/ppermute | solution.py:447
  109.1 5.4 %ladder_product.5 = (f32[144,512]{1,0:T(8,128)S(1)}, f32[144,512]{1,0:T(8,128)S(1)}) custom-call(s32[1]{0:T(128)} %bitcast.turn_ref.turn, f32[48,16,128]{2,1,0:T(8,128)S(1)} %collective-permute-done.17.refs_0_, f32[48,16,128]{2,1,0:T(8,128)S(1)} %collective-permute-done.18.refs_1_, f32[48,16,128]{2,1,0:T(8,128)S(1)} %collective-permute-done.19.refs_2_, ...), custom_call_target="tpu_custom_call" | custom-call | flops 1811939328 | bytes 8388608 | tf_op jit(solution)/shard_map/ladder_product/pallas_call | solution.py:228
  116.0 1.7 %collective-permute-start.5 = (f32[16,512]{1,0:T(8,128)S(1)}, f32[16,512]{1,0:T(8,128)S(1)}, u32[]{:S(2)}, u32[]{:S(2)}) collective-permute-start(f32[16,512]{1,0:T(8,128)S(1)} %get-tuple-element.60), channel_id=1, source_target_pairs={{0,16},{8,24},{16,0},{24,8},{1,17},{9,25},{17,1},{25,9},{2,18},{10... | collective-permute-start | bytes 98312 | tf_op jit(solution)/shard_map/ppermute | solution.py:447
  118.5 1.6 %collective-permute-start.24 = (f32[48,384]{1,0:T(8,128)S(1)}, f32[48,384]{1,0:T(8,128)S(1)}, u32[]{:S(2)}, u32[]{:S(2)}) collective-permute-start(f32[48,384]{1,0:T(8,128)S(1)} %get-tuple-element.93), channel_id=1, source_target_pairs={{0,8},{8,0},{16,24},{24,16},{1,9},{9,1},{17,25},{25,17},{2,10},{10... | collective-permute-start | bytes 221192 | tf_op jit(solution)/shard_map/ppermute | solution.py:447
  120.6 1.5 %collective-permute-start.26 = (f32[48,384]{1,0:T(8,128)S(1)}, f32[48,384]{1,0:T(8,128)S(1)}, u32[]{:S(2)}, u32[]{:S(2)}) collective-permute-start(f32[48,384]{1,0:T(8,128)S(1)} %get-tuple-element.95), channel_id=1, source_target_pairs={{0,24},{8,16},{16,8},{24,0},{1,25},{9,17},{17,9},{25,1},{2,26},{10... | collective-permute-start | bytes 221192 | tf_op jit(solution)/shard_map/ppermute | solution.py:447
  122.1 1.4 %collective-permute-start.6 = (f32[16,512]{1,0:T(8,128)S(1)}, f32[16,512]{1,0:T(8,128)S(1)}, u32[]{:S(2)}, u32[]{:S(2)}) collective-permute-start(f32[16,512]{1,0:T(8,128)S(1)} %get-tuple-element.61), channel_id=1, source_target_pairs={{0,24},{8,16},{16,8},{24,0},{1,25},{9,17},{17,9},{25,1},{2,26},{10... | collective-permute-start | bytes 98312 | tf_op jit(solution)/shard_map/ppermute | solution.py:447
  123.5 3.4 %collective-permute-done.6.refs_3_ = f32[16,512]{1,0:T(8,128)S(1)} collective-permute-done((f32[16,512]{1,0:T(8,128)S(1)}, f32[16,512]{1,0:T(8,128)S(1)}, u32[]{:S(2)}, u32[]{:S(2)}) %collective-permute-start.6) | collective-permute-done | bytes 32800 | tf_op jit(solution)/shard_map/ppermute | solution.py:447
  126.9 1.5 %collective-permute-start.21 = (f32[48,128]{1,0:T(8,128)S(1)}, f32[48,128]{1,0:T(8,128)S(1)}, u32[]{:S(2)}, u32[]{:S(2)}) collective-permute-start(f32[48,128]{1,0:T(8,128)S(1)} %get-tuple-element.90), channel_id=1, source_target_pairs={{0,8},{8,0},{16,24},{24,16},{1,9},{9,1},{17,25},{25,17},{2,10},{10... | collective-permute-start | bytes 73736 | tf_op jit(solution)/shard_map/ppermute | solution.py:447
  129.1 1.5 %collective-permute-start.23 = (f32[48,128]{1,0:T(8,128)S(1)}, f32[48,128]{1,0:T(8,128)S(1)}, u32[]{:S(2)}, u32[]{:S(2)}) collective-permute-start(f32[48,128]{1,0:T(8,128)S(1)} %get-tuple-element.92), channel_id=1, source_target_pairs={{0,24},{8,16},{16,8},{24,0},{1,25},{9,17},{17,9},{25,1},{2,26},{10... | collective-permute-start | bytes 73736 | tf_op jit(solution)/shard_map/ppermute | solution.py:447
  130.6 3.7 %collective-permute-start.27 = (f32[48,128]{1,0:T(8,128)S(1)}, f32[48,128]{1,0:T(8,128)S(1)}, u32[]{:S(2)}, u32[]{:S(2)}) collective-permute-start(f32[48,128]{1,0:T(8,128)S(1)} %get-tuple-element.96), channel_id=1, source_target_pairs={{0,6},{1,7},{2,4},{3,5},{4,2},{5,3},{6,0},{7,1},{8,14},{9,15},{10,... | collective-permute-start | bytes 73736 | tf_op jit(solution)/shard_map/ppermute | solution.py:507
  136.3 2.7 %collective-permute-done.28.refs_2_ = f32[48,128]{1,0:T(8,128)S(1)} collective-permute-done((f32[48,128]{1,0:T(8,128)S(1)}, f32[48,128]{1,0:T(8,128)S(1)}, u32[]{:S(2)}, u32[]{:S(2)}) %collective-permute-start.28) | collective-permute-done | bytes 24608 | tf_op jit(solution)/shard_map/ppermute | solution.py:507
  (57 shorter events, 10.9 us)
Async XLA Ops:
  5.6 77.6 %collective-permute-start.10 = (f32[48,32,128]{2,1,0:T(8,128)S(1)}, f32[48,32,128]{2,1,0:T(8,128)S(1)}, u32[]{:S(2)}, u32[]{:S(2)}) collective-permute-start(f32[48,32,128]{2,1,0:T(8,128)S(1)} %get-tuple-element.65), channel_id=1, source_target_pairs={{0,8},{8,0},{16,24},{24,16},{1,9},{9,1},{17,25},{25,17},{2,10},{10... | collective-permute-start | bytes 2359304 | tf_op jit(solution)/shard_map/ppermute | solution.py:447
  8.7 74.8 %collective-permute-start.11 = (f32[48,32,128]{2,1,0:T(8,128)S(1)}, f32[48,32,128]{2,1,0:T(8,128)S(1)}, u32[]{:S(2)}, u32[]{:S(2)}) collective-permute-start(f32[48,32,128]{2,1,0:T(8,128)S(1)} %get-tuple-element.66), channel_id=1, source_target_pairs={{0,16},{8,24},{16,0},{24,8},{1,17},{9,25},{17,1},{25,9},{2,18},{10... | collective-permute-start | bytes 2359304 | tf_op jit(solution)/shard_map/ppermute | solution.py:447
  10.2 75.0 %collective-permute-start.12 = (f32[48,32,128]{2,1,0:T(8,128)S(1)}, f32[48,32,128]{2,1,0:T(8,128)S(1)}, u32[]{:S(2)}, u32[]{:S(2)}) collective-permute-start(f32[48,32,128]{2,1,0:T(8,128)S(1)} %get-tuple-element.67), channel_id=1, source_target_pairs={{0,24},{8,16},{16,8},{24,0},{1,25},{9,17},{17,9},{25,1},{2,26},{10... | collective-permute-start | bytes 2359304 | tf_op jit(solution)/shard_map/ppermute | solution.py:447
  10.2 35.0 %collective-permute-start = (f32[24,8,128]{2,1,0:T(8,128)S(1)}, f32[24,8,128]{2,1,0:T(8,128)S(1)}, u32[]{:S(2)}, u32[]{:S(2)}) collective-permute-start(f32[24,8,128]{2,1,0:T(8,128)S(1)} %cycle_window.1.refs_0_), channel_id=1, source_target_pairs={{0,8},{8,0},{16,24},{24,16},{1,9},{9,1},{17,25},{25,17},{2,10},{10... | collective-permute-start | bytes 294920 | tf_op jit(solution)/shard_map/ppermute | solution.py:447
  12.2 35.8 %collective-permute-start.1 = (f32[24,8,128]{2,1,0:T(8,128)S(1)}, f32[24,8,128]{2,1,0:T(8,128)S(1)}, u32[]{:S(2)}, u32[]{:S(2)}) collective-permute-start(f32[24,8,128]{2,1,0:T(8,128)S(1)} %cycle_window.1.refs_0_), channel_id=1, source_target_pairs={{0,16},{8,24},{16,0},{24,8},{1,17},{9,25},{17,1},{25,9},{2,18},{10... | collective-permute-start | bytes 294920 | tf_op jit(solution)/shard_map/ppermute | solution.py:447
  45.2 6.6 %collective-permute-start.2 = (f32[24,8,128]{2,1,0:T(8,128)S(1)}, f32[24,8,128]{2,1,0:T(8,128)S(1)}, u32[]{:S(2)}, u32[]{:S(2)}) collective-permute-start(f32[24,8,128]{2,1,0:T(8,128)S(1)} %cycle_window.1.refs_0_), channel_id=1, source_target_pairs={{0,24},{8,16},{16,8},{24,0},{1,25},{9,17},{17,9},{25,1},{2,26},{10... | collective-permute-start | bytes 294920 | tf_op jit(solution)/shard_map/ppermute | solution.py:447
  47.9 6.9 %collective-permute-start.7 = (f32[48,8,128]{2,1,0:T(8,128)S(1)}, f32[48,8,128]{2,1,0:T(8,128)S(1)}, u32[]{:S(2)}, u32[]{:S(2)}) collective-permute-start(f32[48,8,128]{2,1,0:T(8,128)S(1)} %get-tuple-element.54), channel_id=1, source_target_pairs={{0,8},{8,0},{16,24},{24,16},{1,9},{9,1},{17,25},{25,17},{2,10},{10... | collective-permute-start | bytes 589832 | tf_op jit(solution)/shard_map/ppermute | solution.py:447
  51.8 14.1 %collective-permute-start.8 = (f32[48,8,128]{2,1,0:T(8,128)S(1)}, f32[48,8,128]{2,1,0:T(8,128)S(1)}, u32[]{:S(2)}, u32[]{:S(2)}) collective-permute-start(f32[48,8,128]{2,1,0:T(8,128)S(1)} %get-tuple-element.62), channel_id=1, source_target_pairs={{0,16},{8,24},{16,0},{24,8},{1,17},{9,25},{17,1},{25,9},{2,18},{10... | collective-permute-start | bytes 589832 | tf_op jit(solution)/shard_map/ppermute | solution.py:447
  54.9 26.8 %collective-permute-start.17 = (f32[48,16,128]{2,1,0:T(8,128)S(1)}, f32[48,16,128]{2,1,0:T(8,128)S(1)}, u32[]{:S(2)}, u32[]{:S(2)}) collective-permute-start(f32[48,16,128]{2,1,0:T(8,128)S(1)} %get-tuple-element.76), channel_id=1, source_target_pairs={{0,8},{8,0},{16,24},{24,16},{1,9},{9,1},{17,25},{25,17},{2,10},{10... | collective-permute-start | bytes 1179656 | tf_op jit(solution)/shard_map/ppermute | solution.py:447
  65.9 1.4 %collective-permute-start.3 = (f32[64,512]{1,0:T(8,128)S(1)}, f32[64,512]{1,0:T(8,128)S(1)}, u32[]{:S(2)}, u32[]{:S(2)}) collective-permute-start(f32[64,512]{1,0:T(8,128)S(1)} %get-tuple-element.57), channel_id=1, source_target_pairs={{0,1},{1,0},{2,3},{3,2},{4,5},{5,4},{6,7},{7,6},{8,9},{9,8},{10,11... | collective-permute-start | bytes 393224 | tf_op jit(solution)/shard_map/ppermute | solution.py:451
  67.3 4.0 %copy-start.2 = (f32[48]{0:T(128)S(1)}, f32[48]{0:T(128)}, u32[]{:S(2)}) copy-start(f32[48]{0:T(128)} %occ.1) | copy-start | bytes 580
  67.3 4.0 %copy-start.4 = (s32[4]{0:T(128)S(1)}, s32[4]{0:T(128)}, u32[]{:S(2)}) copy-start(s32[4]{0:T(128)} %counts.3) | copy-start | bytes 52
  67.3 12.5 %collective-permute-start.9 = (f32[48,8,128]{2,1,0:T(8,128)S(1)}, f32[48,8,128]{2,1,0:T(8,128)S(1)}, u32[]{:S(2)}, u32[]{:S(2)}) collective-permute-start(f32[48,8,128]{2,1,0:T(8,128)S(1)} %get-tuple-element.63), channel_id=1, source_target_pairs={{0,24},{8,16},{16,8},{24,0},{1,25},{9,17},{17,9},{25,1},{2,26},{10... | collective-permute-start | bytes 589832 | tf_op jit(solution)/shard_map/ppermute | solution.py:447
  79.9 34.7 %collective-permute-start.14 = (f32[48,8,128]{2,1,0:T(8,128)S(1)}, f32[48,8,128]{2,1,0:T(8,128)S(1)}, u32[]{:S(2)}, u32[]{:S(2)}) collective-permute-start(f32[48,8,128]{2,1,0:T(8,128)S(1)} %get-tuple-element.78), channel_id=1, source_target_pairs={{0,8},{8,0},{16,24},{24,16},{1,9},{9,1},{17,25},{25,17},{2,10},{10... | collective-permute-start | bytes 589832 | tf_op jit(solution)/shard_map/ppermute | solution.py:447
  81.7 32.9 %collective-permute-start.15 = (f32[48,8,128]{2,1,0:T(8,128)S(1)}, f32[48,8,128]{2,1,0:T(8,128)S(1)}, u32[]{:S(2)}, u32[]{:S(2)}) collective-permute-start(f32[48,8,128]{2,1,0:T(8,128)S(1)} %get-tuple-element.79), channel_id=1, source_target_pairs={{0,16},{8,24},{16,0},{24,8},{1,17},{9,25},{17,1},{25,9},{2,18},{10... | collective-permute-start | bytes 589832 | tf_op jit(solution)/shard_map/ppermute | solution.py:447
  83.2 31.4 %collective-permute-start.16 = (f32[48,8,128]{2,1,0:T(8,128)S(1)}, f32[48,8,128]{2,1,0:T(8,128)S(1)}, u32[]{:S(2)}, u32[]{:S(2)}) collective-permute-start(f32[48,8,128]{2,1,0:T(8,128)S(1)} %get-tuple-element.80), channel_id=1, source_target_pairs={{0,24},{8,16},{16,8},{24,0},{1,25},{9,17},{17,9},{25,1},{2,26},{10... | collective-permute-start | bytes 589832 | tf_op jit(solution)/shard_map/ppermute | solution.py:447
  83.4 25.7 %collective-permute-start.18 = (f32[48,16,128]{2,1,0:T(8,128)S(1)}, f32[48,16,128]{2,1,0:T(8,128)S(1)}, u32[]{:S(2)}, u32[]{:S(2)}) collective-permute-start(f32[48,16,128]{2,1,0:T(8,128)S(1)} %get-tuple-element.82), channel_id=1, source_target_pairs={{0,16},{8,24},{16,0},{24,8},{1,17},{9,25},{17,1},{25,9},{2,18},{10... | collective-permute-start | bytes 1179656 | tf_op jit(solution)/shard_map/ppermute | solution.py:447
  85.2 23.9 %collective-permute-start.19 = (f32[48,16,128]{2,1,0:T(8,128)S(1)}, f32[48,16,128]{2,1,0:T(8,128)S(1)}, u32[]{:S(2)}, u32[]{:S(2)}) collective-permute-start(f32[48,16,128]{2,1,0:T(8,128)S(1)} %get-tuple-element.83), channel_id=1, source_target_pairs={{0,24},{8,16},{16,8},{24,0},{1,25},{9,17},{17,9},{25,1},{2,26},{10... | collective-permute-start | bytes 1179656 | tf_op jit(solution)/shard_map/ppermute | solution.py:447
  115.3 3.1 %collective-permute-start.20 = (f32[144,512]{1,0:T(8,128)S(1)}, f32[144,512]{1,0:T(8,128)S(1)}, u32[]{:S(2)}, u32[]{:S(2)}) collective-permute-start(f32[144,512]{1,0:T(8,128)S(1)} %shard_map.75), channel_id=1, source_target_pairs={{0,1},{1,0},{2,3},{3,2},{4,5},{5,4},{6,7},{7,6},{8,9},{9,8},{10,11... | collective-permute-start | bytes 884744 | tf_op jit(solution)/shard_map/ppermute | solution.py:451
  115.4 5.2 %collective-permute-start.4 = (f32[16,512]{1,0:T(8,128)S(1)}, f32[16,512]{1,0:T(8,128)S(1)}, u32[]{:S(2)}, u32[]{:S(2)}) collective-permute-start(f32[16,512]{1,0:T(8,128)S(1)} %get-tuple-element.59), channel_id=1, source_target_pairs={{0,8},{8,0},{16,24},{24,16},{1,9},{9,1},{17,25},{25,17},{2,10},{10... | collective-permute-start | bytes 98312 | tf_op jit(solution)/shard_map/ppermute | solution.py:447
  115.8 12.7 %collective-permute-start.13 = (f32[48,512]{1,0:T(8,128)S(1)}, f32[48,512]{1,0:T(8,128)S(1)}, u32[]{:S(2)}, u32[]{:S(2)}) collective-permute-start(f32[48,512]{1,0:T(8,128)S(1)} %get-tuple-element.74), channel_id=1, source_target_pairs={{0,1},{1,0},{2,3},{3,2},{4,5},{5,4},{6,7},{7,6},{8,9},{9,8},{10,11... | collective-permute-start | bytes 294920 | tf_op jit(solution)/shard_map/ppermute | solution.py:451
  116.0 6.1 %collective-permute-start.5 = (f32[16,512]{1,0:T(8,128)S(1)}, f32[16,512]{1,0:T(8,128)S(1)}, u32[]{:S(2)}, u32[]{:S(2)}) collective-permute-start(f32[16,512]{1,0:T(8,128)S(1)} %get-tuple-element.60), channel_id=1, source_target_pairs={{0,16},{8,24},{16,0},{24,8},{1,17},{9,25},{17,1},{25,9},{2,18},{10... | collective-permute-start | bytes 98312 | tf_op jit(solution)/shard_map/ppermute | solution.py:447
  118.5 10.6 %collective-permute-start.24 = (f32[48,384]{1,0:T(8,128)S(1)}, f32[48,384]{1,0:T(8,128)S(1)}, u32[]{:S(2)}, u32[]{:S(2)}) collective-permute-start(f32[48,384]{1,0:T(8,128)S(1)} %get-tuple-element.93), channel_id=1, source_target_pairs={{0,8},{8,0},{16,24},{24,16},{1,9},{9,1},{17,25},{25,17},{2,10},{10... | collective-permute-start | bytes 221192 | tf_op jit(solution)/shard_map/ppermute | solution.py:447
  120.1 10.5 %collective-permute-start.25 = (f32[48,384]{1,0:T(8,128)S(1)}, f32[48,384]{1,0:T(8,128)S(1)}, u32[]{:S(2)}, u32[]{:S(2)}) collective-permute-start(f32[48,384]{1,0:T(8,128)S(1)} %get-tuple-element.94), channel_id=1, source_target_pairs={{0,16},{8,24},{16,0},{24,8},{1,17},{9,25},{17,1},{25,9},{2,18},{10... | collective-permute-start | bytes 221192 | tf_op jit(solution)/shard_map/ppermute | solution.py:447
  120.6 10.0 %collective-permute-start.26 = (f32[48,384]{1,0:T(8,128)S(1)}, f32[48,384]{1,0:T(8,128)S(1)}, u32[]{:S(2)}, u32[]{:S(2)}) collective-permute-start(f32[48,384]{1,0:T(8,128)S(1)} %get-tuple-element.95), channel_id=1, source_target_pairs={{0,24},{8,16},{16,8},{24,0},{1,25},{9,17},{17,9},{25,1},{2,26},{10... | collective-permute-start | bytes 221192 | tf_op jit(solution)/shard_map/ppermute | solution.py:447
  122.1 4.8 %collective-permute-start.6 = (f32[16,512]{1,0:T(8,128)S(1)}, f32[16,512]{1,0:T(8,128)S(1)}, u32[]{:S(2)}, u32[]{:S(2)}) collective-permute-start(f32[16,512]{1,0:T(8,128)S(1)} %get-tuple-element.61), channel_id=1, source_target_pairs={{0,24},{8,16},{16,8},{24,0},{1,25},{9,17},{17,9},{25,1},{2,26},{10... | collective-permute-start | bytes 98312 | tf_op jit(solution)/shard_map/ppermute | solution.py:447
  126.9 7.4 %collective-permute-start.21 = (f32[48,128]{1,0:T(8,128)S(1)}, f32[48,128]{1,0:T(8,128)S(1)}, u32[]{:S(2)}, u32[]{:S(2)}) collective-permute-start(f32[48,128]{1,0:T(8,128)S(1)} %get-tuple-element.90), channel_id=1, source_target_pairs={{0,8},{8,0},{16,24},{24,16},{1,9},{9,1},{17,25},{25,17},{2,10},{10... | collective-permute-start | bytes 73736 | tf_op jit(solution)/shard_map/ppermute | solution.py:447
  128.5 6.6 %collective-permute-start.22 = (f32[48,128]{1,0:T(8,128)S(1)}, f32[48,128]{1,0:T(8,128)S(1)}, u32[]{:S(2)}, u32[]{:S(2)}) collective-permute-start(f32[48,128]{1,0:T(8,128)S(1)} %get-tuple-element.91), channel_id=1, source_target_pairs={{0,16},{8,24},{16,0},{24,8},{1,17},{9,25},{17,1},{25,9},{2,18},{10... | collective-permute-start | bytes 73736 | tf_op jit(solution)/shard_map/ppermute | solution.py:447
  129.1 6.0 %collective-permute-start.23 = (f32[48,128]{1,0:T(8,128)S(1)}, f32[48,128]{1,0:T(8,128)S(1)}, u32[]{:S(2)}, u32[]{:S(2)}) collective-permute-start(f32[48,128]{1,0:T(8,128)S(1)} %get-tuple-element.92), channel_id=1, source_target_pairs={{0,24},{8,16},{16,8},{24,0},{1,25},{9,17},{17,9},{25,1},{2,26},{10... | collective-permute-start | bytes 73736 | tf_op jit(solution)/shard_map/ppermute | solution.py:447
  130.6 5.7 %collective-permute-start.27 = (f32[48,128]{1,0:T(8,128)S(1)}, f32[48,128]{1,0:T(8,128)S(1)}, u32[]{:S(2)}, u32[]{:S(2)}) collective-permute-start(f32[48,128]{1,0:T(8,128)S(1)} %get-tuple-element.96), channel_id=1, source_target_pairs={{0,6},{1,7},{2,4},{3,5},{4,2},{5,3},{6,0},{7,1},{8,14},{9,15},{10,... | collective-permute-start | bytes 73736 | tf_op jit(solution)/shard_map/ppermute | solution.py:507
  134.3 4.7 %collective-permute-start.28 = (f32[48,128]{1,0:T(8,128)S(1)}, f32[48,128]{1,0:T(8,128)S(1)}, u32[]{:S(2)}, u32[]{:S(2)}) collective-permute-start(f32[48,128]{1,0:T(8,128)S(1)} %get-tuple-element.97), channel_id=1, source_target_pairs={{0,4},{1,5},{2,6},{3,7},{4,0},{5,1},{6,2},{7,3},{8,12},{9,13},{10,... | collective-permute-start | bytes 73736 | tf_op jit(solution)/shard_map/ppermute | solution.py:507
  134.3 4.7 %collective-permute-start.29 = (f32[48,128]{1,0:T(8,128)S(1)}, f32[48,128]{1,0:T(8,128)S(1)}, u32[]{:S(2)}, u32[]{:S(2)}) collective-permute-start(f32[48,128]{1,0:T(8,128)S(1)} %get-tuple-element.98), channel_id=1, source_target_pairs={{0,2},{1,3},{2,0},{3,1},{4,6},{5,7},{6,4},{7,5},{8,10},{9,11},{10,... | collective-permute-start | bytes 73736 | tf_op jit(solution)/shard_map/ppermute | solution.py:507
  (3 other events, 8.6 us)
